TPU v7x, 32 devices: a whole 2x2x4 slice. The times are simulated.
32 devices in a mesh: dp: 8 (over y, x, core), mp: 4 (over z).
Axes of the slice: x: 2, y: 2, z: 4, core: 2. Of those that a mesh axis runs over, the one named last changes fastest.
Arguments:
- hidden_in: bfloat16 [6144, 768], P(('dp', 'mp')), may hold values from -6 to 6
- text_lens: int32 [8], P('dp'), may hold values from 1 to 512, as said below
- key_mask: int32 [6144], P('dp'), may hold values 0 or 1
- bucket_x: int32 [8, 768, 768], P('dp'), may hold values from 0 to 63
- bucket_y: int32 [8, 768, 768], P('dp'), may hold values from 0 to 63
- w_qkv: bfloat16 [3, 768, 768], P(None, None, 'mp'), may hold values from -0.21875 to 0.21875
- b_q: bfloat16 [768], P('mp'), may hold values from -1.75 to 1.75
- b_v: bfloat16 [768], P('mp'), may hold values from -1.75 to 1.75
- w_out: bfloat16 [768, 768], P('mp'), may hold values from -0.875 to 0.875
- b_out: bfloat16 [768], replicated, may hold values from -1.75 to 1.75
- g_attn: float32 [768], replicated, may hold values from 0.5 to 1.5
- n_attn: float32 [768], replicated, may hold values from -1.75 to 1.75
- w_up: bfloat16 [768, 3072], P(None, 'mp'), may hold values from -0.21875 to 0.21875
- b_up: bfloat16 [3072], P('mp'), may hold values from -1.75 to 1.75
- w_down: bfloat16 [3072, 768], P('mp'), may hold values from -0.109375 to 0.109375
- b_down: bfloat16 [768], replicated, may hold values from -1.75 to 1.75
- g_ffn: float32 [768], replicated, may hold values from 0.5 to 1.5
- n_ffn: float32 [768], replicated, may hold values from -1.75 to 1.75
- t_pos: bfloat16 [12, 32], P('mp'), may hold values from -48 to 48
- t_x: bfloat16 [12, 64], P('mp'), may hold values from -48 to 48
- t_y: bfloat16 [12, 64], P('mp'), may hold values from -48 to 48
- cotangent: bfloat16 [6144, 768], P(('dp', 'mp')), may hold values from -6 to 6
Outputs:
- layer_out: bfloat16 [6144, 768], P(('dp', 'mp'))
- input_grad: bfloat16 [6144, 768], P(('dp', 'mp'))
- grad_w_qkv: float32 [3, 768, 768], P(None, None, 'mp')
- grad_b_q: float32 [768], P('mp')
- grad_b_v: float32 [768], P('mp')
- grad_w_out: float32 [768, 768], P('mp')
- grad_b_out: float32 [768], replicated
- grad_g_attn: float32 [768], replicated
- grad_n_attn: float32 [768], replicated
- grad_w_up: float32 [768, 3072], P(None, 'mp')
- grad_b_up: float32 [3072], P('mp')
- grad_w_down: float32 [3072, 768], P('mp')
- grad_b_down: float32 [768], replicated
- grad_g_ffn: float32 [768], replicated
- grad_n_ffn: float32 [768], replicated
- grad_t_pos: float32 [12, 32], P('mp')
- grad_t_x: float32 [12, 64], P('mp')
- grad_t_y: float32 [12, 64], P('mp')
Inputs may be any that keep to these rules, and one draw needn't show every extreme that they name: `text_lens`: some document has exactly 512 text tokens.
All inputs are finite; a program needn't handle non-finite values. No bound on the sum of `key_mask` on one device may be relied on, other than what follows from the above.
Results may differ from a plain program's by a relative error of at most 0.015.
Values may be sent and summed in bfloat16 or wider, within the bound.
A program may use at most 128 MiB of HBM per device.

v0:
```python
import jax
import jax.numpy as jnp
from jax import lax
from jax.sharding import PartitionSpec as P

HEAD_DIM = 64
PATCHES = 196


THRESHOLDS = (12, 16, 23, 32, 46, 64, 91)


def relative_bucket(slot_len):
    places = jnp.arange(slot_len, dtype=jnp.int32)
    offset = places[None, :] - places[:, None]
    magnitude = jnp.abs(offset)
    far_part = jnp.full(offset.shape, 8, jnp.int32)
    for border in THRESHOLDS:
        far_part = far_part + (magnitude >= border).astype(jnp.int32)
    near_part = jnp.where(magnitude < 8, magnitude, far_part)
    return jnp.where(offset > 0, 16, 0).astype(jnp.int32) + near_part


def layer_norm(values, norm_gain, norm_shift):
    center = jnp.mean(values, axis=-1, keepdims=True)
    spread = values - center
    varied = jnp.mean(spread * spread, axis=-1, keepdims=True)
    return spread * lax.rsqrt(varied + 1e-05) * norm_gain + norm_shift


def exact_gelu(values):
    return jax.nn.gelu(values, approximate=False)


def plane_onehot(buckets, bin_count):
    bin_ids = jnp.arange(bin_count, dtype=jnp.int32)
    return (buckets[None, :, :] == bin_ids[:, None, None]).astype(jnp.bfloat16)


def on_device(
    hidden_in,
    text_lens,
    key_mask,
    bucket_x,
    bucket_y,
    w_qkv,
    b_q,
    b_v,
    w_out,
    b_out,
    g_attn,
    n_attn,
    w_up,
    b_up,
    w_down,
    b_down,
    g_ffn,
    n_ffn,
    t_pos,
    t_x,
    t_y,
    cotangent,
):
    row_count = hidden_in.shape[0]
    doc_count = bucket_x.shape[0]
    slot_len = bucket_x.shape[1]
    group_rows = doc_count * slot_len
    inner_width = w_qkv.shape[2]
    heads_here = inner_width // HEAD_DIM
    plane_bins = t_x.shape[1]
    score_scale = HEAD_DIM ** (-0.5)
    places = jnp.arange(slot_len, dtype=jnp.int32)
    doc_length = 1 + PATCHES + text_lens
    row_valid = places[None, :] < doc_length[:, None]
    key_valid = row_valid & ((key_mask.reshape(doc_count, slot_len) == 1) | (places[None, :] == 0))
    line_hot = plane_onehot(relative_bucket(slot_len), t_pos.shape[1])
    line_bias = jnp.einsum("hb,bij->hij", t_pos, line_hot, preferred_element_type=jnp.float32)
    full_input = lax.all_gather(hidden_in, "mp", axis=0, tiled=True)
    qkv_raw = jnp.einsum("td,cde->tce", full_input, w_qkv, preferred_element_type=jnp.float32)
    qkv_shift = jnp.stack(
        [b_q.astype(jnp.float32), jnp.zeros((inner_width,), jnp.float32), b_v.astype(jnp.float32)]
    )
    qkv_low = (qkv_raw + qkv_shift[None]).astype(jnp.bfloat16)
    qkv_docs = qkv_low.reshape(doc_count, slot_len, 3, heads_here, HEAD_DIM)

    def doc_scores(doc_qkv, doc_keys, bias):
        scores = (
            jnp.einsum(
                "ihd,jhd->hij", doc_qkv[:, 0], doc_qkv[:, 1], preferred_element_type=jnp.float32
            )
            * score_scale
            + bias
        )
        return jnp.where(doc_keys[None, None, :], scores, -1e30)

    def attend_doc(item):
        doc_qkv, plane_x, plane_y, doc_keys = item
        bias = line_bias + jnp.einsum(
            "hb,bij->hij",
            t_x,
            plane_onehot(plane_x, plane_bins),
            preferred_element_type=jnp.float32,
        )
        bias = bias + jnp.einsum(
            "hb,bij->hij",
            t_y,
            plane_onehot(plane_y, plane_bins),
            preferred_element_type=jnp.float32,
        )
        bias = bias * score_scale
        masked = doc_scores(doc_qkv, doc_keys, bias)
        row_top = jnp.max(masked, axis=-1, keepdims=True)
        log_total = row_top + jnp.log(jnp.sum(jnp.exp(masked - row_top), axis=-1, keepdims=True))
        probs = jnp.exp(masked - log_total).astype(jnp.bfloat16)
        context = jnp.einsum(
            "hij,jhd->ihd", probs, doc_qkv[:, 2], preferred_element_type=jnp.float32
        )
        return (context.astype(jnp.bfloat16).reshape(slot_len, inner_width), log_total, bias)

    ctx_docs, lse_docs, bias_docs = lax.map(attend_doc, (qkv_docs, bucket_x, bucket_y, key_valid))
    ctx_all = ctx_docs.reshape(group_rows, inner_width)
    rows_here = ctx_all
    attn_sum = lax.psum_scatter(
        jnp.dot(rows_here, w_out, preferred_element_type=jnp.float32),
        "mp",
        scatter_dimension=0,
        tiled=True,
    )
    resid_one = hidden_in.astype(jnp.float32) + attn_sum + b_out.astype(jnp.float32)
    normed, norm_back_one = jax.vjp(layer_norm, resid_one, g_attn, n_attn)
    normed_low = normed.astype(jnp.bfloat16)
    normed_full = lax.all_gather(normed_low, "mp", axis=0, tiled=True)
    pre_act = jnp.dot(normed_full, w_up, preferred_element_type=jnp.float32) + b_up.astype(
        jnp.float32
    )
    act_value, gelu_back = jax.vjp(exact_gelu, pre_act)
    act_low = act_value.astype(jnp.bfloat16)
    rows_here = act_low
    branch = lax.psum_scatter(
        jnp.dot(rows_here, w_down, preferred_element_type=jnp.float32),
        "mp",
        scatter_dimension=0,
        tiled=True,
    )
    resid_two = normed + branch + b_down.astype(jnp.float32)
    output_value, norm_back_two = jax.vjp(layer_norm, resid_two, g_ffn, n_ffn)
    layer_out = output_value.astype(jnp.bfloat16)
    first_mine = lax.axis_index("mp") * row_count
    valid_mine = lax.dynamic_slice_in_dim(row_valid.reshape(group_rows), first_mine, row_count, 0)
    grad_y = cotangent.astype(jnp.float32) * valid_mine[:, None].astype(jnp.float32)
    d_resid_two, grad_g_ffn, grad_n_ffn = norm_back_two(grad_y)
    grad_b_down = jnp.sum(d_resid_two, axis=0)
    d_branch = d_resid_two.astype(jnp.bfloat16)
    piece_rows = lax.all_gather(d_branch, "mp", axis=0, tiled=True)
    down_total = jnp.einsum("tf,td->fd", act_low, piece_rows, preferred_element_type=jnp.float32)
    act_part = jnp.einsum("td,fd->tf", piece_rows, w_down, preferred_element_type=jnp.float32)
    act_grad = act_part
    grad_w_down, act_grad = (down_total, act_grad)
    d_pre = gelu_back(act_grad)[0].astype(jnp.bfloat16)
    grad_w_up = jnp.einsum("td,tf->df", normed_full, d_pre, preferred_element_type=jnp.float32)
    grad_b_up = jnp.sum(d_pre.astype(jnp.float32), axis=0)
    rows_here = d_pre
    d_hidden = lax.psum_scatter(
        jnp.einsum("tf,df->td", rows_here, w_up, preferred_element_type=jnp.float32),
        "mp",
        scatter_dimension=0,
        tiled=True,
    )
    d_normed = d_resid_two + d_hidden
    d_resid_one, grad_g_attn, grad_n_attn = norm_back_one(d_normed)
    grad_b_out = jnp.sum(d_resid_one, axis=0)
    d_attn = d_resid_one.astype(jnp.bfloat16)
    piece_rows = lax.all_gather(d_attn, "mp", axis=0, tiled=True)
    out_total = jnp.einsum("te,td->ed", ctx_all, piece_rows, preferred_element_type=jnp.float32)
    ctx_part = jnp.einsum("td,ed->te", piece_rows, w_out, preferred_element_type=jnp.float32)
    ctx_grad = ctx_part
    grad_w_out, ctx_grad = (out_total, ctx_grad)
    ctx_grad_docs = ctx_grad.astype(jnp.bfloat16).reshape(doc_count, slot_len, heads_here, HEAD_DIM)

    def attend_back(carried, item):
        line_total, xplane_total, yplane_total = carried
        doc_qkv, doc_dctx, log_total, bias, plane_x, plane_y, doc_keys = item
        masked = doc_scores(doc_qkv, doc_keys, bias)
        probs_full = jnp.exp(masked - log_total)
        probs = probs_full.astype(jnp.bfloat16)
        d_probs = jnp.einsum(
            "ihd,jhd->hij", doc_dctx, doc_qkv[:, 2], preferred_element_type=jnp.float32
        )
        d_values = jnp.einsum("hij,ihd->jhd", probs, doc_dctx, preferred_element_type=jnp.float32)
        row_dot = jnp.sum(probs_full * d_probs, axis=-1, keepdims=True)
        d_scores = (probs_full * (d_probs - row_dot)).astype(jnp.bfloat16)
        d_query = (
            jnp.einsum("hij,jhd->ihd", d_scores, doc_qkv[:, 1], preferred_element_type=jnp.float32)
            * score_scale
        )
        d_keys = (
            jnp.einsum("hij,ihd->jhd", d_scores, doc_qkv[:, 0], preferred_element_type=jnp.float32)
            * score_scale
        )
        line_total = (
            line_total
            + jnp.einsum("hij,bij->hb", d_scores, line_hot, preferred_element_type=jnp.float32)
            * score_scale
        )
        xplane_total = (
            xplane_total
            + jnp.einsum(
                "hij,bij->hb",
                d_scores,
                plane_onehot(plane_x, plane_bins),
                preferred_element_type=jnp.float32,
            )
            * score_scale
        )
        yplane_total = (
            yplane_total
            + jnp.einsum(
                "hij,bij->hb",
                d_scores,
                plane_onehot(plane_y, plane_bins),
                preferred_element_type=jnp.float32,
            )
            * score_scale
        )
        d_qkv_doc = jnp.stack([d_query, d_keys, d_values], axis=1).astype(jnp.bfloat16)
        return ((line_total, xplane_total, yplane_total), d_qkv_doc)

    table_start = (
        jnp.zeros(t_pos.shape, jnp.float32),
        jnp.zeros(t_x.shape, jnp.float32),
        jnp.zeros(t_y.shape, jnp.float32),
    )
    (grad_t_pos, grad_t_x, grad_t_y), d_qkv_docs = lax.scan(
        attend_back,
        table_start,
        (qkv_docs, ctx_grad_docs, lse_docs, bias_docs, bucket_x, bucket_y, key_valid),
    )
    d_qkv = d_qkv_docs.reshape(group_rows, 3, inner_width)
    grad_w_qkv = jnp.einsum("td,tce->cde", full_input, d_qkv, preferred_element_type=jnp.float32)
    shift_grads = jnp.sum(d_qkv.astype(jnp.float32), axis=0)
    grad_b_q = shift_grads[0]
    grad_b_v = shift_grads[2]
    rows_here = d_qkv
    d_input = lax.psum_scatter(
        jnp.einsum("tce,cde->td", rows_here, w_qkv, preferred_element_type=jnp.float32).astype(
            jnp.bfloat16
        ),
        "mp",
        scatter_dimension=0,
        tiled=True,
    ).astype(jnp.float32)
    input_grad = (d_resid_one + d_input).astype(jnp.bfloat16)
    (
        grad_w_qkv,
        grad_b_q,
        grad_b_v,
        grad_w_out,
        grad_w_up,
        grad_b_up,
        grad_w_down,
        grad_t_pos,
        grad_t_x,
        grad_t_y,
        grad_b_out,
        grad_g_attn,
        grad_n_attn,
        grad_b_down,
        grad_g_ffn,
        grad_n_ffn,
    ) = lax.psum(
        (
            grad_w_qkv,
            grad_b_q,
            grad_b_v,
            grad_w_out,
            grad_w_up,
            grad_b_up,
            grad_w_down,
            grad_t_pos,
            grad_t_x,
            grad_t_y,
            grad_b_out,
            grad_g_attn,
            grad_n_attn,
            grad_b_down,
            grad_g_ffn,
            grad_n_ffn,
        ),
        "dp",
    )
    grad_b_out, grad_g_attn, grad_n_attn, grad_b_down, grad_g_ffn, grad_n_ffn = lax.psum(
        (grad_b_out, grad_g_attn, grad_n_attn, grad_b_down, grad_g_ffn, grad_n_ffn), "mp"
    )
    return (
        layer_out,
        input_grad,
        grad_w_qkv,
        grad_b_q,
        grad_b_v,
        grad_w_out,
        grad_b_out,
        grad_g_attn,
        grad_n_attn,
        grad_w_up,
        grad_b_up,
        grad_w_down,
        grad_b_down,
        grad_g_ffn,
        grad_n_ffn,
        grad_t_pos,
        grad_t_x,
        grad_t_y,
    )


def solution(mesh):
    placed = (
        P(("dp", "mp"), None),
        P("dp"),
        P("dp"),
        P("dp", None, None),
        P("dp", None, None),
        P(None, None, "mp"),
        P("mp"),
        P("mp"),
        P("mp", None),
        P(),
        P(),
        P(),
        P(None, "mp"),
        P("mp"),
        P("mp", None),
        P(),
        P(),
        P(),
        P("mp", None),
        P("mp", None),
        P("mp", None),
        P(("dp", "mp"), None),
    )
    return jax.shard_map(
        on_device,
        mesh=mesh,
        in_specs=placed,
        out_specs=(
            P(("dp", "mp"), None),
            P(("dp", "mp"), None),
            P(None, None, "mp"),
            P("mp"),
            P("mp"),
            P("mp", None),
            P(),
            P(),
            P(),
            P(None, "mp"),
            P("mp"),
            P("mp", None),
            P(),
            P(),
            P(),
            P("mp", None),
            P("mp", None),
            P("mp", None),
        ),
        check_vma=False,
    )
```

profile of v0, /device:TPU:0, one launch (start us, length us, event | category | flops | bytes accessed | tf_op | source)
XLA Modules:
  0.0 576.5 jit_solution(17402110194286184060)
XLA Ops:
  7.3 0.7 all-gather.5.cloned.1.call-update
  8.0 0.7 fusion.16
  8.7 1.0 copy-done.43
  9.7 23.9 %fusion.1 = f32[768,768,3]{1,2,0:T(4,128)} fusion(s32[768,768]{1,0:T(8,128)S(1)} %bitcast.138, bf16[3,64]{1,0:T(4,128)(2,1)S(1)} %copy-done.50), kind=kOutput, calls=%fused_computation.2 | convolution fusion | flops 264241152 | bytes 9437568 | tf_op jit(solution)/shard_map/while/body/eval_jaxpr/hb,bij->hij/dot_general | solution.py:104
  33.6 10.8 %copy.42 = f32[768,768,3]{0,1,2:T(8,128)} copy(f32[768,768,3]{1,2,0:T(4,128)} %fusion.1) | data formatting | bytes 14155776 | tf_op jit(solution)/shard_map/while/body/eval_jaxpr/hb,bij->hij/dot_general | solution.py:104
  44.5 13.2 %fusion.9 = f32[768,768,3]{1,2,0:T(4,128)} fusion(s32[768,768]{1,0:T(8,128)S(1)} %fusion.16, bf16[3,32]{1,0:T(4,128)(2,1)S(1)} %copy-done.51), kind=kOutput, calls=%fused_computation.12 | convolution fusion | flops 132120576 | bytes 9437376 | tf_op jit(solution)/shard_map/hb,bij->hij/dot_general | solution.py:77
  57.6 11.0 %copy.40 = f32[768,768,3]{0,1,2:T(8,128)} copy(f32[768,768,3]{1,2,0:T(4,128)} %fusion.9) | data formatting | bytes 14155776 | tf_op jit(solution)/shard_map/hb,bij->hij/dot_general | solution.py:77
  68.6 24.1 %fusion.3 = f32[768,768,3]{1,2,0:T(4,128)} fusion(s32[768,768]{1,0:T(8,128)S(1)} %bitcast.137, bf16[3,64]{1,0:T(4,128)(2,1)S(1)} %copy-done.52), kind=kOutput, calls=%fused_computation.5 | convolution fusion | flops 264241152 | bytes 9437568 | tf_op jit(solution)/shard_map/while/body/eval_jaxpr/hb,bij->hij/dot_general | solution.py:98
  92.8 10.9 %copy.41 = f32[768,768,3]{0,1,2:T(8,128)} copy(f32[768,768,3]{1,2,0:T(4,128)} %fusion.3) | data formatting | bytes 14155776 | tf_op jit(solution)/shard_map/while/body/eval_jaxpr/hb,bij->hij/dot_general | solution.py:98
  104.6 2.3 fusion.60
  107.0 0.9 copy-done.4
  107.9 6.5 %fusion.59 = (f32[3,768]{1,0:T(4,128)S(1)}, f32[3,768,768]{1,2,0:T(8,128)S(1)}) fusion(f32[768,768,3]{0,1,2:T(8,128)} %copy.42, f32[768,768,3]{0,1,2:T(8,128)S(1)} %copy-done.4, f32[768,768,3]{0,1,2:T(8,128)} %copy.41, bf16[768,3,3,64]{0,3,2,1:T(8,128)(2,1)S(1)} %bitcast.109, pred[768]{0:T(1024)(128)(4,1)S(1)} %fusion.46), kind=kOutput, calls=%fused_computation.123 | convolution fusion | flops 237106944 | bytes 28911616 | tf_op jit(solution)/shard_map/while/body/eval_jaxpr/ihd,jhd->hij/dot_general | solution.py:88
  114.4 0.9 exponential_reduce_fusion
  115.4 1.9 copy-done.2
  117.3 1.2 convolution_convert_fusion.1
  118.5 1.9 fusion.61
  120.5 50.8 %reduce-scatter.5.cloned.1.call-done = f32[192,768]{1,0:T(8,128)} async-done(((f32[768,768]{1,0:T(8,128)}), f32[192,768]{1,0:T(8,128)}) %reduce-scatter.5.cloned.1.call-update) | async-done | bytes 589840 | tf_op jit(solution)/shard_map/reduce_scatter | solution.py:123
  171.3 1.2 fusion.57
  172.9 0.9 fusion.44
  173.9 30.0 %all-gather.7.cloned.1.call-done = bf16[768,768]{1,0:T(8,128)(2,1)} async-done(((bf16[192,768]{1,0:T(8,128)(2,1)}), bf16[768,768]{1,0:T(8,128)(2,1)}) %all-gather.7.cloned.1.call-update) | async-done | bytes 1179664 | tf_op jit(solution)/shard_map/all_gather | solution.py:132
  203.9 8.8 %multiply_convert_fusion.1 = (bf16[768,768]{1,0:T(8,128)(2,1)S(1)}, f32[768,768]{1,0:T(8,128)}, f32[768,768]{1,0:T(8,128)}) fusion(f32[768]{0:T(1024)S(1)} %convert_element_type.173, bf16[768,768]{1,0:T(8,128)(2,1)} %all-gather.7.cloned.1.call-done, bf16[768,768]{1,0:T(8,128)(2,1)S(1)} %copy-done), kind=kOutput, calls=%fused_computation.30 | convolution fusion | flops 944898048 | bytes 8260608 | tf_op jit(solution)/shard_map/dot_general | solution.py:133
  212.6 1.0 copy-done.55
  213.7 2.6 fusion.62
  216.3 0.6 copy-done.41
  216.9 46.7 %reduce-scatter.7.cloned.1.call-done = f32[192,768]{1,0:T(8,128)} async-done(((f32[768,768]{1,0:T(8,128)}), f32[192,768]{1,0:T(8,128)}) %reduce-scatter.7.cloned.1.call-update) | async-done | bytes 589840 | tf_op jit(solution)/shard_map/reduce_scatter | solution.py:139
  263.6 1.4 fusion.55
  265.2 0.9 multiply_reduce_fusion.1
  266.1 2.0 fusion.54
  268.2 0.6 copy-done.32
  268.7 1.4 add_reduce_fusion.1
  270.2 30.0 %all-gather.9.cloned.1.call-done = bf16[768,768]{1,0:T(8,128)(2,1)} async-done(((bf16[192,768]{1,0:T(8,128)(2,1)}), bf16[768,768]{1,0:T(8,128)(2,1)}) %all-gather.9.cloned.1.call-update) | async-done | bytes 1179664 | tf_op jit(solution)/shard_map/all_gather | solution.py:154
  300.3 5.4 convert_reduce_fusion
  305.7 1.0 copy-done.57
  306.7 2.5 fusion.63
  309.3 47.3 %reduce-scatter.9.cloned.1.call-done = f32[192,768]{1,0:T(8,128)} async-done(((f32[768,768]{1,0:T(8,128)}), f32[192,768]{1,0:T(8,128)}) %reduce-scatter.9.cloned.1.call-update) | async-done | bytes 589840 | tf_op jit(solution)/shard_map/reduce_scatter | solution.py:163
  356.6 2.0 multiply_reduce_fusion.2
  358.6 1.0 fusion.53
  359.6 0.8 add_reduce_fusion
  360.7 29.8 %all-gather.11.cloned.1.call-done = bf16[768,768]{1,0:T(8,128)(2,1)} async-done(((bf16[192,768]{1,0:T(8,128)(2,1)}), bf16[768,768]{1,0:T(8,128)(2,1)}) %all-gather.11.cloned.1.call-update) | async-done | bytes 1179664 | tf_op jit(solution)/shard_map/all_gather | solution.py:173
  390.5 1.9 convolution_convert_fusion.2
  392.4 4.4 convolution_convert_fusion
  396.8 7.4 %multiply_reduce_fusion = (f32[3,768]{1,0:T(4,128)S(1)}, f32[3,768,768]{1,2,0:T(8,128)}) fusion(f32[3,768,768]{1,2,0:T(8,128)} %copy-done.2, f32[3,768]{1,0:T(4,128)S(1)} %log_add_fusion, bf16[768,3,64]{0,2,1:T(8,128)(2,1)S(1)} %bitcast.119, bf16[768,3,3,64]{0,3,2,1:T(8,128)(2,1)S(1)} %bitcast.111), kind=kOutput, calls=%fused_computation.19 | convolution fusion | flops 231798528 | bytes 14767104 | tf_op jit(solution)/shard_map/while/body/eval_jaxpr/ihd,jhd->hij/dot_general | solution.py:186
  404.2 4.3 multiply_convert_fusion
  408.5 1.2 fusion.32
  409.8 0.7 fusion.31
  411.0 2.2 bitcast_convert_fusion
  413.3 4.0 fusion.65
  417.3 2.5 fusion.66
  419.8 8.5 %copy.47 = bf16[3,768,768]{2,0,1:T(4,128)(2,1)} copy(bf16[3,768,768]{1,2,0:T(8,128)(2,1)} %copy-done.3) | data formatting | bytes 7077888 | tf_op jit(solution)/shard_map/while/body/eval_jaxpr/convert_element_type | solution.py:191
  428.3 1.2 fusion.64
  429.5 3.6 convolution_bitcast_fusion
  433.1 15.2 %fusion.39 = f32[3,32]{1,0:T(4,128)S(1)} fusion(bf16[3,768,768]{2,0,1:T(4,128)(2,1)} %copy.47, s32[768,768]{1,0:T(8,128)S(1)} %copy-done.7), kind=kOutput, calls=%fused_computation.70 | convolution fusion | flops 132120672 | bytes 5898624 | tf_op jit(solution)/shard_map/while/body/eval_jaxpr/hij,bij->hb/dot_general | solution.py:202
  448.4 0.9 copy-done.12
  449.5 26.4 %fusion.38 = f32[3,64]{1,0:T(4,128)S(1)} fusion(bf16[3,768,768]{2,0,1:T(4,128)(2,1)} %copy.47, s32[768,768]{1,0:T(8,128)} %bitcast.136), kind=kOutput, calls=%fused_computation.69 | convolution fusion | flops 264241344 | bytes 5899008 | tf_op jit(solution)/shard_map/while/body/eval_jaxpr/hij,bij->hb/dot_general | solution.py:207
  476.1 24.9 %fusion.37 = f32[3,64]{1,0:T(4,128)S(1)} fusion(bf16[3,768,768]{2,0,1:T(4,128)(2,1)S(1)} %bitcast.115, s32[768,768]{1,0:T(8,128)S(1)} %bitcast.139), kind=kOutput, calls=%fused_computation.68 | convolution fusion | flops 264241344 | bytes 5899008 | tf_op jit(solution)/shard_map/while/body/eval_jaxpr/hij,bij->hb/dot_general | solution.py:217
  501.0 24.9 %all-reduce = (f32[192]{0:T(256)}, f32[192]{0:T(256)}, f32[768]{0:T(1024)S(1)}, f32[768]{0:T(1024)S(1)}, f32[768]{0:T(1024)S(1)}, /*index=5*/f32[768]{0:T(1024)}...) all-reduce(f32[192]{0:T(256)S(1)} %bitcast.133, ...), channel_id=1, replica_groups=mesh['dp'=8,'mp'=4] {'dp'}, use_global_device_ids=true, to_apply=%region_17.18 | all-reduce | flops 6240 | bytes 49920 | tf_op jit(solution)/shard_map/psum | solution.py:270
  525.9 18.7 %all-reduce.2 = (f32[768]{0:T(1024)}, f32[768]{0:T(1024)}, f32[768]{0:T(1024)}, f32[768]{0:T(1024)}, f32[768]{0:T(1024)}, /*index=5*/f32[768]{0:T(1024)}) all-reduce(f32[768]{0:T(1024)S(1)} %get-tuple-element.98, f32[768]{0:T(1024)S(1)} %get-tuple-element.99, ...), channel_id=1, replica_groups=mesh['dp'=8,'mp'=4] {'mp'}, use_global_device_ids=true, to_apply=%region_22.23 | all-reduce | flops 4608 | bytes 36864 | tf_op jit(solution)/shard_map/psum | solution.py:291
  544.7 1.8 add_convert_fusion.2
  546.5 15.4 %all-reduce.5.cloned.1.call-done = (f32[3,768,192]{1,2,0:T(8,128)}, f32[192,768]{1,0:T(8,128)}, f32[768,768]{1,0:T(8,128)}, f32[768,768]{1,0:T(8,128)}) async-done(((f32[3,768,192]{1,2,0:T(8,128)}, f32[192,768]{1,0:T(8,128)}, f32[768,768]{1,0:T(8,128)}, f32[768,768]{1,0:T(8,128)}), (f32[3,768,192]{1,2,0:T(8,128)}, f32[192,768]{1,0:T(8,128)}, f32[768,768]{1,0:T(8,128)}, ...) | async-done | bytes 7077904 | tf_op jit(solution)/shard_map/psum | solution.py:270
  561.9 2.9 copy.59
  564.8 0.8 copy.60
  565.6 1.4 copy.61
  567.0 1.1 copy-done.8
  568.2 1.4 copy.62
  (159 shorter events, 2.5 us)
Async XLA Ops:
  7.2 196.7 %copy-start = (bf16[768,768]{1,0:T(8,128)(2,1)S(1)}, bf16[768,768]{1,0:T(8,128)(2,1)}, u32[]{:S(2)}) copy-start(bf16[768,768]{1,0:T(8,128)(2,1)} %param.34) | copy-start | bytes 3538948
  7.2 1.5 copy-start.50
  7.2 97.3 %all-gather.5.cloned.1.call-start = ((), (), s32[]{:S(2)}) async-start(), calls=%async_computation.4 | async-start | bytes 1474560 | tf_op jit(solution)/shard_map/all_gather | solution.py:78
  8.0 163.4 %reduce-scatter.5.cloned.1.call-start = ((), (), s32[]{:S(2)}) async-start(), calls=%async_computation.5 | async-start | bytes 2949120 | tf_op jit(solution)/shard_map/reduce_scatter | solution.py:123
  8.0 1.7 copy-start.43
  8.7 35.8 %copy-start.6 = (s32[768,768]{1,0:T(8,128)}, s32[768,768]{1,0:T(8,128)S(1)}, u32[]{:S(2)}) copy-start(s32[768,768]{1,0:T(8,128)S(1)} %fusion.16) | copy-start | bytes 7077892
  33.6 10.8 %copy-start.51 = (bf16[3,32]{1,0:T(4,128)(2,1)S(1)}, bf16[3,32]{1,0:T(4,128)(2,1)}, u32[]{:S(2)}) copy-start(bf16[3,32]{1,0:T(4,128)(2,1)} %param.40) | copy-start | bytes 580
  57.6 11.0 %copy-start.42 = (s32[1,768,768]{2,1,0:T(8,128)S(1)}, s32[1,768,768]{2,1,0:T(8,128)}, u32[]{:S(2)}) copy-start(s32[1,768,768]{2,1,0:T(8,128)} %param.25) | copy-start | bytes 7077892
  57.6 11.0 %copy-start.52 = (bf16[3,64]{1,0:T(4,128)(2,1)S(1)}, bf16[3,64]{1,0:T(4,128)(2,1)}, u32[]{:S(2)}) copy-start(bf16[3,64]{1,0:T(4,128)(2,1)} %param.41) | copy-start | bytes 1156
  92.7 11.0 %copy-start.53 = (bf16[192]{0:T(256)(128)(2,1)S(1)}, bf16[192]{0:T(256)(128)(2,1)}, u32[]{:S(2)}) copy-start(bf16[192]{0:T(256)(128)(2,1)} %param.29) | copy-start | bytes 1156
  92.7 11.0 %copy-start.54 = (bf16[192]{0:T(256)(128)(2,1)S(1)}, bf16[192]{0:T(256)(128)(2,1)}, u32[]{:S(2)}) copy-start(bf16[192]{0:T(256)(128)(2,1)} %param.28) | copy-start | bytes 1156
  92.7 11.8 %copy-start.38 = (s32[768]{0:T(1024)S(1)}, s32[768]{0:T(1024)}, u32[]{:S(2)}) copy-start(s32[768]{0:T(1024)} %param.24) | copy-start | bytes 9220
  92.7 11.8 %copy-start.48 = (bf16[3,768,192]{1,2,0:T(8,128)(2,1)S(1)}, bf16[3,768,192]{1,2,0:T(8,128)(2,1)}, u32[]{:S(2)}) copy-start(bf16[3,768,192]{1,2,0:T(8,128)(2,1)} %param.27) | copy-start | bytes 2654212
  104.6 3.4 copy-start.4
  114.4 2.9 copy-start.2
  117.3 1.2 copy-start.10
  118.5 2.0 copy-start.39
  118.5 52.9 %copy-start.13 = (bf16[192,768]{1,0:T(8,128)(2,1)S(1)}, bf16[192,768]{1,0:T(8,128)(2,1)}, u32[]{:S(2)}) copy-start(bf16[192,768]{1,0:T(8,128)(2,1)} %param.22) | copy-start | bytes 884740
  120.4 52.4 %copy-start.16 = (f32[768]{0:T(1024)S(1)}, f32[768]{0:T(1024)}, u32[]{:S(2)}) copy-start(f32[768]{0:T(1024)} %param.32) | copy-start | bytes 9220
  120.4 52.4 %copy-start.21 = (f32[768]{0:T(1024)S(1)}, f32[768]{0:T(1024)}, u32[]{:S(2)}) copy-start(f32[768]{0:T(1024)} %param.33) | copy-start | bytes 9220
  120.4 53.4 %copy-start.40 = (bf16[768]{0:T(1024)(128)(2,1)S(1)}, bf16[768]{0:T(1024)(128)(2,1)}, u32[]{:S(2)}) copy-start(bf16[768]{0:T(1024)(128)(2,1)} %param.35) | copy-start | bytes 4612
  120.5 83.4 %all-gather.7.cloned.1.call-start = ((), (), s32[]{:S(2)}) async-start(), calls=%async_computation.6 | async-start | bytes 1474560 | tf_op jit(solution)/shard_map/all_gather | solution.py:132
  172.6 91.0 %copy-start.17 = (f32[192]{0:T(256)}, f32[192]{0:T(256)S(1)}, u32[]{:S(2)}) copy-start(f32[192]{0:T(256)S(1)} %broadcast_multiply_fusion.1) | copy-start | bytes 2308
  172.8 39.8 %copy-start.30 = (f32[192]{0:T(256)}, f32[192]{0:T(256)S(1)}, u32[]{:S(2)}) copy-start(f32[192]{0:T(256)S(1)} %multiply_reduce_fusion.6) | copy-start | bytes 2308
  172.8 90.7 %copy-start.19 = (f32[192]{0:T(256)}, f32[192]{0:T(256)S(1)}, u32[]{:S(2)}) copy-start(f32[192]{0:T(256)S(1)} %fusion.51) | copy-start | bytes 2308
  173.8 89.8 %reduce-scatter.7.cloned.1.call-start = ((), (), s32[]{:S(2)}) async-start(), calls=%async_computation.7 | async-start | bytes 2949120 | tf_op jit(solution)/shard_map/reduce_scatter | solution.py:139
  173.8 38.8 %copy-start.37 = (f32[768]{0:T(1024)}, f32[768]{0:T(1024)S(1)}, u32[]{:S(2)}) copy-start(f32[768]{0:T(1024)S(1)} %convert_element_type.173) | copy-start | bytes 9220
  203.9 9.8 %copy-start.45 = (bf16[768,768]{1,0:T(8,128)(2,1)S(1)}, bf16[768,768]{1,0:T(8,128)(2,1)}, u32[]{:S(2)}) copy-start(bf16[768,768]{1,0:T(8,128)(2,1)} %param.36) | copy-start | bytes 3538948
  216.2 47.4 %copy-start.22 = (f32[768]{0:T(1024)S(1)}, f32[768]{0:T(1024)}, u32[]{:S(2)}) copy-start(f32[768]{0:T(1024)} %param.33) | copy-start | bytes 9220
  216.2 49.0 %copy-start.14 = (bf16[192,768]{1,0:T(8,128)(2,1)S(1)}, bf16[192,768]{1,0:T(8,128)(2,1)}, u32[]{:S(2)}) copy-start(bf16[192,768]{1,0:T(8,128)(2,1)} %param.43) | copy-start | bytes 884740
  216.2 49.0 %copy-start.23 = (f32[768]{0:T(1024)S(1)}, f32[768]{0:T(1024)}, u32[]{:S(2)}) copy-start(f32[768]{0:T(1024)} %param.38) | copy-start | bytes 9220
  216.3 84.0 %all-gather.9.cloned.1.call-start = ((), (), s32[]{:S(2)}) async-start(), calls=%async_computation.8 | async-start | bytes 1474560 | tf_op jit(solution)/shard_map/all_gather | solution.py:154
  216.9 49.2 %copy-start.29 = (f32[1,192]{1,0:T(1,128)}, f32[1,192]{1,0:T(1,128)S(1)}, u32[]{:S(2)}) copy-start(f32[1,192]{1,0:T(1,128)S(1)} %compare_convert_fusion) | copy-start | bytes 2308
  270.2 86.4 %reduce-scatter.9.cloned.1.call-start = ((), (), s32[]{:S(2)}) async-start(), calls=%async_computation.9 | async-start | bytes 2949120 | tf_op jit(solution)/shard_map/reduce_scatter | solution.py:163
  309.2 47.4 %copy-start.18 = (f32[192]{0:T(256)S(1)}, f32[192]{0:T(256)}, u32[]{:S(2)}) copy-start(f32[192]{0:T(256)} %copy-done.17) | copy-start | bytes 2308
  309.2 47.4 %copy-start.20 = (f32[192]{0:T(256)S(1)}, f32[192]{0:T(256)}, u32[]{:S(2)}) copy-start(f32[192]{0:T(256)} %copy-done.19) | copy-start | bytes 2308
  309.2 47.4 %copy-start.33 = (f32[192]{0:T(256)S(1)}, f32[192]{0:T(256)}, u32[]{:S(2)}) copy-start(f32[192]{0:T(256)} %copy-done.32) | copy-start | bytes 2308
  309.2 49.4 %copy-start.31 = (f32[192]{0:T(256)S(1)}, f32[192]{0:T(256)}, u32[]{:S(2)}) copy-start(f32[192]{0:T(256)} %copy-done.30) | copy-start | bytes 2308
  309.2 81.3 %all-gather.11.cloned.1.call-start = ((), (), s32[]{:S(2)}) async-start(), calls=%async_computation.10 | async-start | bytes 1474560 | tf_op jit(solution)/shard_map/all_gather | solution.py:173
  360.5 184.2 %reduce-scatter.11.cloned.1.call-start = ((), (), s32[]{:S(2)}) async-start(), calls=%async_computation.11 | async-start | bytes 1474560 | tf_op jit(solution)/shard_map/reduce_scatter | solution.py:244
  392.4 11.8 %slice-start = ((s8[7077888]{0:T(1024)(128)(4,1)}), s8[4194304]{0:T(1024)(128)(4,1)S(1)}, s32[]{:S(2)}) async-start(s8[7077888]{0:T(1024)(128)(4,1)} %bitcast.107), calls=%async_computation.13 | async-start | bytes 8388608
  396.8 7.4 %slice-start.1 = ((s8[7077888]{0:T(1024)(128)(4,1)}), s8[2883584]{0:T(1024)(128)(4,1)S(1)}, s32[]{:S(2)}) async-start(s8[7077888]{0:T(1024)(128)(4,1)} %bitcast.107), calls=%async_computation.14 | async-start | bytes 5767168
  408.5 2.0 copy-start.3
  409.8 1.3 copy-start.49
  411.0 2.3 copy-start.46
  413.2 148.6 %all-reduce.5.cloned.1.call-start = ((), (), s32[]{:S(2)}) async-start(), calls=%async_computation.12 | async-start | bytes 14155776 | tf_op jit(solution)/shard_map/psum | solution.py:270
  413.3 4.0 copy-start.47
  413.3 4.0 copy-start.56
  419.8 8.5 %copy-start.5 = (bf16[768,768]{1,0:T(8,128)(2,1)S(1)}, bf16[768,768]{1,0:T(8,128)(2,1)}, u32[]{:S(2)}) copy-start(bf16[768,768]{1,0:T(8,128)(2,1)} %all-gather.11.cloned.1.call-done) | copy-start | bytes 3538948
  429.5 3.6 copy-start.7
  448.3 27.6 %slice-start.2 = ((s8[4718592]{0:T(1024)(128)(4,1)}), s8[524288]{0:T(1024)(128)(4,1)S(1)}, s32[]{:S(2)}) async-start(s8[4718592]{0:T(1024)(128)(4,1)} %bitcast.114), calls=%async_computation.15 | async-start | bytes 1048576
  449.5 26.5 %slice-start.3 = ((s8[4718592]{0:T(1024)(128)(4,1)}), s8[4194304]{0:T(1024)(128)(4,1)S(1)}, s32[]{:S(2)}) async-start(s8[4718592]{0:T(1024)(128)(4,1)} %bitcast.114), calls=%async_computation.16 | async-start | bytes 8388608
  449.5 26.5 %copy-start.44 = (s32[1,768,768]{2,1,0:T(8,128)S(1)}, s32[1,768,768]{2,1,0:T(8,128)}, u32[]{:S(2)}) copy-start(s32[1,768,768]{2,1,0:T(8,128)} %param.26) | copy-start | bytes 7077892
  476.0 25.0 %copy-start.24 = (f32[768]{0:T(1024)S(1)}, f32[768]{0:T(1024)}, u32[]{:S(2)}) copy-start(f32[768]{0:T(1024)} %get-tuple-element.79) | copy-start | bytes 9220
  476.0 25.0 %copy-start.25 = (f32[768]{0:T(1024)S(1)}, f32[768]{0:T(1024)}, u32[]{:S(2)}) copy-start(f32[768]{0:T(1024)} %get-tuple-element.82) | copy-start | bytes 9220
  476.0 25.0 %copy-start.26 = (f32[768]{0:T(1024)S(1)}, f32[768]{0:T(1024)}, u32[]{:S(2)}) copy-start(f32[768]{0:T(1024)} %get-tuple-element.132) | copy-start | bytes 9220
  476.0 25.0 %copy-start.27 = (f32[768]{0:T(1024)S(1)}, f32[768]{0:T(1024)}, u32[]{:S(2)}) copy-start(f32[768]{0:T(1024)} %get-tuple-element.77) | copy-start | bytes 9220
  476.1 25.0 %copy-start.28 = (f32[768]{0:T(1024)S(1)}, f32[768]{0:T(1024)}, u32[]{:S(2)}) copy-start(f32[768]{0:T(1024)} %get-tuple-element.81) | copy-start | bytes 9220
  476.1 25.0 %copy-start.36 = (f32[768]{0:T(1024)S(1)}, f32[768]{0:T(1024)}, u32[]{:S(2)}) copy-start(f32[768]{0:T(1024)} %get-tuple-element.118) | copy-start | bytes 9220
  476.1 68.6 %copy-start.35 = (f32[192]{0:T(256)S(1)}, f32[192]{0:T(256)}, u32[]{:S(2)}) copy-start(f32[192]{0:T(256)} %copy-done.34) | copy-start | bytes 2308
  561.9 3.0 copy-start.15
  561.9 3.8 copy-start.9
  565.6 2.5 copy-start.8
  565.6 3.9 copy-start.1
  (7 other events, 6.1 us)
Sparse Core Ops, SparseCore 0:
  9.6 32.7 all-gather.4
  120.6 50.7 reduce-scatter.4
  173.9 29.9 all-gather.6
  216.4 47.1 reduce-scatter.6
  270.3 29.9 all-gather.8
  309.4 47.1 reduce-scatter.8
  360.6 29.9 all-gather.10
  413.4 28.2 reduce-scatter.10
  448.5 113.3 all-reduce.4
where the time goes:
time: 585 us; the launch traced here: 577 us
  waiting for transfers between devices  251 us (43%)
  matrix products  188 us (32%)
  local copies, waits for them, and re-layouts  57.7 us (10%)
  blocking collectives  43.6 us (7%)
  other arithmetic  20.3 us (3%)
  between operations  15.5 us (3%)
    reduce_scatter x1, waiting for transfers between devices, on_device(): lax.psum_scatter(jnp.dot(rows_here, w_out, preferred_element_type=jnp.flo...  50.8 us
    reduce_scatter x1, waiting for transfers between devices, on_device(): lax.psum_scatter(jnp.einsum('tf,df->td', rows_here, w_up, preferred_eleme...  47.3 us
    reduce_scatter x1, waiting for transfers between devices, on_device(): lax.psum_scatter(jnp.dot(rows_here, w_down, preferred_element_type=jnp.fl...  46.7 us
    all_gather x1, waiting for transfers between devices, on_device(): piece_rows = lax.all_gather(d_branch, 'mp', axis=0, tiled=True)  30 us
    all_gather x1, waiting for transfers between devices, on_device(): normed_full = lax.all_gather(normed_low, 'mp', axis=0, tiled=True)  30 us
    all_gather x1, waiting for transfers between devices, on_device(): piece_rows = lax.all_gather(d_attn, 'mp', axis=0, tiled=True)  29.8 us
    dot_general x1, matrix products, attend_back(): jnp.einsum('hij,bij->hb', d_scores, plane_onehot(plane_x, plane_bins), pr...  26.4 us
    psum x1, blocking collectives, on_device(): lax.psum((grad_w_qkv, grad_b_q, grad_b_v, grad_w_out, grad_w_up, grad_b_u...  24.9 us
  transfers between devices with their start and end apart: 9, of which 7 were waited for; matrix products, arithmetic and copies ran while one was open for 32% of the time, Pallas kernels for 0%

commit v1 on v0

v1 whole, which is shorter than its diff:
```python
import functools
import jax
import jax.numpy as jnp
from jax import lax
from jax.experimental import pallas as pl
from jax.experimental.pallas import tpu as pltpu
from jax.sharding import PartitionSpec as P

HEAD_DIM = 64
PATCHES = 196
THRESHOLDS = (12, 16, 23, 32, 46, 64, 91)
TILE = 128
F32, BF16 = jnp.float32, jnp.bfloat16
MESH = pl.DeviceIdType.MESH
VMEM = pl.BlockSpec(memory_space=pltpu.VMEM)
ANY = pl.BlockSpec(memory_space=pl.ANY)
BIG = 58 << 20


def line_bucket(off):
    mag = jnp.abs(off)
    far = jnp.full(off.shape, 8, jnp.int32)
    for border in THRESHOLDS:
        far = far + (mag >= border).astype(jnp.int32)
    return jnp.where(off > 0, 16, 0) + jnp.where(mag < 8, mag, far)


def dot(a, b, ca, cb):
    return lax.dot_general(a, b, (((ca,), (cb,)), ((), ())), preferred_element_type=F32)


def flip(index, bit):
    step = 2**bit
    return index + step * (1 - 2 * ((index // step) % 2))


def gather_plan(dp_size, reverse):
    bits = list(range(1, dp_size.bit_length() - 1))
    return (bits[::-1] if reverse else bits) + [0]


def plan_label(index, plan):
    label = 0
    for place, bit in enumerate(plan):
        label = label + ((index // 2**bit) % 2) * 2**place
    return label


def front_kernel(
    n_mp, n_dp, plans,
    x_ref, w_ref, bq_ref, bv_ref, bx_hbm, by_hbm, tx_ref, ty_ref, tp_ref, len_ref, km_ref, wo_src, wu_src, wd_src,
    xf_ref, q_ref, k_ref, v_ref, e_ref, inv_ref, cr_ref, wo_out, wu_out, wd_out,
    bx_ref, by_ref, bias_ref, line_ref, cs_ref,
    b_sem, x_send, x_recv, c_send, c_recv, own_sem, z_send, z_recv, p_send, p_recv,
):
    d = lax.axis_index("dp")
    z = lax.axis_index("mp")
    rows = x_ref.shape[0]
    slot = bx_ref.shape[0]
    width = w_ref.shape[2]
    heads = width // HEAD_DIM
    tiles = slot // TILE
    scale = HEAD_DIM**-0.5
    sources = (wo_src, wu_src, wd_src)
    gathered = (wo_out, wu_out, wd_out)

    loads = []
    for c in range(tiles):
        part = pl.ds(c * TILE, TILE)
        pair = (
            pltpu.make_async_copy(bx_hbm.at[part], bx_ref.at[part], b_sem.at[0, c]),
            pltpu.make_async_copy(by_hbm.at[part], by_ref.at[part], b_sem.at[1, c]),
        )
        for copy in pair:
            copy.start()
        loads.append(pair)

    barrier = pltpu.get_barrier_semaphore()
    peers = [(d, (z + k) % n_mp) for k in range(1, n_mp)] + [(flip(d, bit), z) for bit in plans[0]]
    for peer in peers:
        pl.semaphore_signal(barrier, inc=1, device_id=peer, device_id_type=MESH)
    xf_ref[z] = x_ref[...]
    pl.semaphore_wait(barrier, len(peers))

    def hop(block, to, sem):
        return pltpu.make_async_remote_copy(
            xf_ref.at[block], xf_ref.at[block], x_send.at[sem], x_recv.at[block], device_id=(d, to), device_id_type=MESH
        )

    def x_step(step, act):
        low, high = z - step, z + step
        if step == 0:
            @pl.when(z < n_mp - 1)
            def _():
                act(hop(z, z + 1, z))

            @pl.when(z > 0)
            def _():
                act(hop(z, z - 1, n_mp))

            return

        @pl.when(jnp.logical_and(low >= 0, z < n_mp - 1))
        def _():
            act(hop(low, z + 1, low))

        @pl.when(jnp.logical_and(high < n_mp, z > 0))
        def _():
            act(hop(high, z - 1, high))

    def x_arrived(step):
        low, high = z - step, z + step

        @pl.when(low >= 0)
        def _():
            hop(low, z, low).wait_recv()

        @pl.when(high < n_mp)
        def _():
            hop(high, z, high).wait_recv()

    x_step(0, lambda c: c.start())

    labels = [plan_label(d, plan) for plan in plans]

    def z_copy(w, to, shard):
        label = labels[w]
        return pltpu.make_async_remote_copy(
            sources[w].at[label], gathered[w].at[shard, label], z_send.at[w, to], z_recv.at[w, shard],
            device_id=(d, to), device_id_type=MESH,
        )

    def own_copy(w):
        return pltpu.make_async_copy(sources[w], gathered[w].at[z], own_sem.at[w])

    def plane_copy(w, place, shard, incoming):
        size = 2**place
        base = (labels[w] // size) * size
        if incoming:
            base = flip(base, place)
        part = gathered[w].at[shard, pl.ds(base, size)]
        return pltpu.make_async_remote_copy(
            part, part, p_send.at[w, place, shard], p_recv.at[w, place, shard],
            device_id=(flip(d, plans[w][place]), z), device_id_type=MESH,
        )

    others = [(z + k) % n_mp for k in range(1, n_mp)]
    depth = len(plans[0])
    for w in range(3):
        for to in others:
            z_copy(w, to, z).start()
    for w in range(3):
        own_copy(w).start()

    def plane_start(w, place):
        for shard in others:
            if place == 0:
                z_copy(w, shard, shard).wait_recv()
            else:
                plane_copy(w, place - 1, shard, True).wait_recv()
            plane_copy(w, place, shard, False).start()

    tab = [
        jnp.broadcast_to(
            jnp.concatenate([tx_ref[h : h + 1, :].astype(F32), ty_ref[h : h + 1, :].astype(F32)], axis=1) * scale, (8, TILE)
        )
        for h in range(heads)
    ]
    bins_x = tx_ref.shape[1]
    pad = jnp.zeros((1, TILE - tp_ref.shape[1]), F32)
    ltab = [
        jnp.broadcast_to(jnp.concatenate([tp_ref[h : h + 1, :].astype(F32) * scale, pad], axis=1), (8, TILE))
        for h in range(heads)
    ]
    ci = lax.broadcasted_iota(jnp.int32, (8, TILE), 1)
    ri = lax.broadcasted_iota(jnp.int32, (8, TILE), 0)

    @pl.loop(0, TILE // 8)
    def _(g):
        at = pl.ds(pl.multiple_of(g * 8, 8), 8)
        for off in range(5):
            idx = line_bucket(ci - ri - g * 8 + (off - 2) * TILE)
            for h in range(heads):
                line_ref[h, off, at, :] = jnp.take_along_axis(ltab[h], idx, axis=1)

    place_ids = lax.broadcasted_iota(jnp.int32, (1, slot), 1)
    live = place_ids < 1 + PATCHES + len_ref[0]
    seen = jnp.where(live & ((km_ref[...] == 1) | (place_ids == 0)), 0.0, -1e30)

    def bias_chunk(c):
        for copy in loads[c]:
            copy.wait()

        @pl.loop(0, TILE // 8)
        def _(g):
            at = pl.ds(pl.multiple_of(c * TILE + g * 8, 8), 8)
            near = pl.ds(pl.multiple_of(g * 8, 8), 8)
            for j in range(tiles):
                cols = slice(j * TILE, (j + 1) * TILE)
                ix = bx_ref[at, cols]
                iy = by_ref[at, cols] + bins_x
                hide = seen[:, cols]
                off = min(max(j - c + 2, 0), 4)
                for h in range(heads):
                    b = jnp.take_along_axis(tab[h], ix, axis=1) + jnp.take_along_axis(tab[h], iy, axis=1)
                    bias_ref[h, at, cols] = (b + line_ref[h, off, near, :]) + hide

    for c in range(tiles):
        if c == tiles - 2:
            x_arrived(1)
            x_step(1, lambda copy: copy.start())
        bias_chunk(c)
    x_arrived(2)
    x_step(2, lambda copy: copy.start())
    plane_start(0, 0)
    x_arrived(3)

    lane = lax.broadcasted_iota(jnp.int32, (1, width), 1)
    mine = [(lane >= h * HEAD_DIM) & (lane < (h + 1) * HEAD_DIM) for h in range(heads)]
    for b in range(n_mp):
        at = pl.ds(b * rows, rows)
        xb = xf_ref[b]
        q_ref[at, :] = ((dot(xb, w_ref[0], 1, 0) + bq_ref[...].astype(F32)).astype(BF16).astype(F32) * scale).astype(BF16)
        k_ref[at, :] = dot(xb, w_ref[1], 1, 0).astype(BF16)
        v_ref[at, :] = (dot(xb, w_ref[2], 1, 0) + bv_ref[...].astype(F32)).astype(BF16)

    def c_copy(turn, to, source):
        return pltpu.make_async_remote_copy(
            cs_ref.at[turn], cr_ref.at[source], c_send.at[turn], c_recv.at[source], device_id=(d, to), device_id_type=MESH
        )

    def attend(turn):
        to = (z + 1 + turn) % n_mp
        at = pl.ds(pl.multiple_of(to * rows, rows), rows)
        q = q_ref[at, :]
        out = jnp.zeros((rows, width), F32)
        for h in range(heads):
            s = dot(jnp.where(mine[h], q, jnp.zeros((), BF16)), k_ref[...], 1, 1) + bias_ref[h, at, :]
            top = jnp.max(s, axis=1, keepdims=True)
            e = jnp.exp(s - top).astype(BF16)
            e_ref[h, at, :] = e
            inv = 1.0 / jnp.sum(e.astype(F32), axis=1, keepdims=True)
            inv_ref[at, h : h + 1] = inv
            out = out + jnp.where(mine[h], dot(e, v_ref[...], 1, 0) * inv, 0.0)
        return to, out.astype(BF16)

    @pl.loop(0, n_mp - 1)
    def _(turn):
        to, out = attend(turn)
        cs_ref[turn] = out
        c_copy(turn, to, z).start()

    cr_ref[z] = attend(n_mp - 1)[1]

    plane_start(0, 1)
    for w in (1, 2):
        plane_start(w, 0)
    for place in range(2, depth):
        plane_start(0, place)
    for place in range(1, depth):
        for w in (1, 2):
            plane_start(w, place)
    for shard in others:
        for w in range(3):
            plane_copy(w, depth - 1, shard, True).wait_recv()

    for turn in range(n_mp - 1):
        c_copy(turn, z, others[turn]).wait_recv()
    for turn in range(n_mp - 1):
        c_copy(turn, z, z).wait_send()
    for step in range(n_mp - 1):
        x_step(step, lambda copy: copy.wait_send())
    for w in range(3):
        own_copy(w).wait()
        for to in others:
            z_copy(w, to, z).wait_send()
            for place in range(depth):
                plane_copy(w, place, to, False).wait_send()


def front(n_mp, n_dp, x, w_qkv, b_q, b_v, bx, by, t_x, t_y, t_pos, text_lens, key_mask, w_out, w_up, w_down):
    rows, wide = x.shape
    slot = bx.shape[0]
    width = w_qkv.shape[2]
    heads = width // HEAD_DIM
    plans = [gather_plan(n_dp, False), gather_plan(n_dp, False), gather_plan(n_dp, True)]
    depth = len(plans[0])
    slices = [w.reshape(n_dp, w.shape[0] // n_dp, w.shape[1]) for w in (w_out, w_up, w_down)]
    sds = jax.ShapeDtypeStruct
    dma = pltpu.SemaphoreType.DMA
    return pl.pallas_call(
        functools.partial(front_kernel, n_mp, n_dp, plans),
        out_shape=[
            sds((n_mp, rows, wide), BF16), sds((slot, width), BF16), sds((slot, width), BF16), sds((slot, width), BF16),
            sds((heads, slot, slot), BF16), sds((slot, heads), F32), sds((n_mp, rows, width), BF16),
        ] + [sds((n_mp,) + s.shape, BF16) for s in slices],
        in_specs=[VMEM, VMEM, VMEM, VMEM, ANY, ANY, VMEM, VMEM, VMEM, pl.BlockSpec(memory_space=pltpu.SMEM), VMEM, ANY, ANY, ANY],
        out_specs=[VMEM] * 7 + [ANY] * 3,
        scratch_shapes=[
            pltpu.VMEM((slot, slot), jnp.int32), pltpu.VMEM((slot, slot), jnp.int32), pltpu.VMEM((heads, slot, slot), F32),
            pltpu.VMEM((heads, 5, TILE, TILE), F32), pltpu.VMEM((n_mp - 1, rows, width), BF16),
            dma((2, slot // TILE)), dma((n_mp + 1,)), dma((n_mp,)), dma((n_mp - 1,)), dma((n_mp,)), dma((3,)),
            dma((3, n_mp)), dma((3, n_mp)), dma((3, depth, n_mp)), dma((3, depth, n_mp)),
        ],
        compiler_params=pltpu.CompilerParams(collective_id=0, has_side_effects=True, vmem_limit_bytes=BIG),
        name="front",
    )(x, w_qkv, b_q.reshape(1, -1), b_v.reshape(1, -1), bx, by, t_x, t_y, t_pos, text_lens, key_mask.reshape(1, -1), *slices)

HI, LO, GROUP, STEP = 4, 16, 16, 2


def back_kernel(
    n_mp,
    g_ref, q_ref, k_ref, v_ref, e_ref, inv_ref, w_ref, xf_ref, da_ref, bx_hbm, by_hbm,
    dx_ref, gw_ref, gb_ref, gt_ref, gl_ref,
    dc_ref, ds_ref, dt_ref, dn_ref, acc_ref, near_ref, part_ref, got_ref, bx_ref, by_ref,
    b_sem, d_send, d_recv, r_send, r_recv,
):
    d = lax.axis_index("dp")
    z = lax.axis_index("mp")
    heads, slot, _ = e_ref.shape
    width = k_ref.shape[1]
    rows = da_ref.shape[0]
    tiles = slot // TILE
    scale = HEAD_DIM**-0.5
    others = [(z + k) % n_mp for k in range(1, n_mp)]

    loads = [pltpu.make_async_copy(bx_hbm, bx_ref, b_sem.at[0]), pltpu.make_async_copy(by_hbm, by_ref, b_sem.at[1])]
    for copy in loads:
        copy.start()
    barrier = pltpu.get_barrier_semaphore()
    for to in others:
        pl.semaphore_signal(barrier, inc=1, device_id=(d, to), device_id_type=MESH)
    pl.semaphore_wait(barrier, n_mp - 1)

    def d_copy(to, source):
        return pltpu.make_async_remote_copy(
            g_ref.at[to], dc_ref.at[source], d_send.at[to], d_recv.at[source], device_id=(d, to), device_id_type=MESH
        )

    for to in others:
        d_copy(to, z).start()
    dc_ref[z] = g_ref[z]

    lane = lax.broadcasted_iota(jnp.int32, (1, width), 1)
    mine = [(lane >= h * HEAD_DIM) & (lane < (h + 1) * HEAD_DIM) for h in range(heads)]
    zero = jnp.zeros((), BF16)
    factor = jnp.zeros((slot, width), F32)
    for h in range(heads):
        factor = jnp.where(mine[h], inv_ref[:, h : h + 1], factor)
    qt = q_ref[...].astype(F32).T.astype(BF16)
    for source in others:
        d_copy(source, source).wait_recv()

    dctx = dc_ref[...].reshape(slot, width)
    gt = (dctx.astype(F32) * factor).T.astype(BF16)
    block = 384
    dq = [None] * (slot // block)
    for h in range(heads):
        hs = slice(h * HEAD_DIM, (h + 1) * HEAD_DIM)
        dk = dv = None
        for r in range(slot // block):
            rs = slice(r * block, (r + 1) * block)
            e = e_ref[h, rs, :]
            p = e.astype(F32) * inv_ref[rs, h : h + 1]
            dp = dot(jnp.where(mine[h], dctx[rs, :], zero), v_ref[...], 1, 1)
            ds = (p * (dp - jnp.sum(p * dp, axis=1, keepdims=True))).astype(BF16)
            ds_ref[h, rs, :] = ds
            a = jnp.where(mine[h], dot(ds, k_ref[...], 1, 0), 0.0)
            dq[r] = a if dq[r] is None else dq[r] + a
            b = dot(qt[hs, rs], ds, 1, 0)
            dk = b if dk is None else dk + b
            c = dot(gt[hs, rs], e, 1, 0)
            dv = c if dv is None else dv + c
        dt_ref[1, hs, :] = dk.astype(BF16)
        dt_ref[2, hs, :] = dv.astype(BF16)
    for r in range(slot // block):
        rs = slice(r * block, (r + 1) * block)
        low = (dq[r] * scale).astype(BF16)
        dn_ref[0, rs, :] = low
        dt_ref[0, :, rs] = low.astype(F32).T.astype(BF16)
    for c in (1, 2):
        dn_ref[c] = dt_ref[c].astype(F32).T.astype(BF16)

    def r_copy(turn, to, source):
        return pltpu.make_async_remote_copy(
            part_ref.at[turn], got_ref.at[source], r_send.at[turn], r_recv.at[source], device_id=(d, to), device_id_type=MESH
        )

    def dx_part(to):
        at = pl.ds(pl.multiple_of(to * rows, rows), rows)
        out = dot(dn_ref[0, at, :], w_ref[0], 1, 1)
        for c in (1, 2):
            out = out + dot(dn_ref[c, at, :], w_ref[c], 1, 1)
        return out

    for turn in range(n_mp - 1):
        part_ref[turn] = dx_part(others[turn]).astype(BF16)
        r_copy(turn, others[turn], z).start()
    da_ref_sum = da_ref[...] + dx_part(z)

    ones = jnp.ones((8, slot), BF16)
    xf = xf_ref[...].reshape(slot, xf_ref.shape[2])
    for c in range(3):
        gw_ref[c] = dot(dt_ref[c], xf, 1, 0)
        gb_ref[c] = dot(ones, dn_ref[c], 1, 0)

    for copy in loads:
        copy.wait()
    acc_ref[...] = jnp.zeros_like(acc_ref)
    one = jnp.ones((), BF16)

    @pl.loop(0, slot // (GROUP * STEP))
    def _(i):
        at = [pl.ds(pl.multiple_of(i * GROUP * STEP + g * GROUP, GROUP), GROUP) for g in range(STEP)]
        ds = [[ds_ref[h, at[g], :] for h in range(heads)] for g in range(STEP)]
        for t, b_ref in enumerate((bx_ref, by_ref)):
            tot = None
            for g in range(STEP):
                b = b_ref[at[g], :]
                hi = (b >> 4).astype(F32).astype(BF16)
                lo = (b & 15).astype(F32).astype(BF16)
                left = []
                for a in range(HI):
                    m = hi == jnp.asarray(a, BF16)
                    left += [jnp.where(m, ds[g][h], zero) for h in range(heads)]
                right = [jnp.where(lo == jnp.asarray(c, BF16), one, zero) for c in range(LO)]
                o = dot(jnp.concatenate(left, 0), jnp.concatenate(right, 0), 1, 1)
                tot = o if tot is None else tot + o
            acc_ref[t] += tot

    m, n = HI * heads * GROUP, LO * GROUP
    same = (lax.broadcasted_iota(jnp.int32, (m, n), 0) & (GROUP - 1)) == (lax.broadcasted_iota(jnp.int32, (m, n), 1) & (GROUP - 1))
    pick = (lax.broadcasted_iota(jnp.int32, (n, LO), 0) // GROUP == lax.broadcasted_iota(jnp.int32, (n, LO), 1)).astype(F32)
    for t in range(2):
        kept = jnp.sum(jnp.where(same, acc_ref[t], 0.0).reshape(m // GROUP, GROUP, n), axis=1)
        gt_ref[t] = lax.dot_general(
            kept, pick, (((1,), (0,)), ((), ())), precision=lax.Precision.HIGHEST, preferred_element_type=F32
        ) * scale

    for h in range(heads):
        for off in range(5):
            tot = jnp.zeros((TILE, TILE), F32)
            for i in range(tiles):
                for j in range(tiles):
                    if min(max(j - i, -2), 2) + 2 == off:
                        tot = tot + ds_ref[h, i * TILE : (i + 1) * TILE, j * TILE : (j + 1) * TILE].astype(F32)
            near_ref[h, off] = tot
    ci = lax.broadcasted_iota(jnp.int32, (TILE, TILE), 1)
    ri = lax.broadcasted_iota(jnp.int32, (TILE, TILE), 0)
    bins = gl_ref.shape[1]
    half = bins // 2
    ids = [line_bucket(ci - ri + (off - 2) * TILE) for off in range(5)]
    for h in range(heads):
        found = []
        for b in range(bins):
            tot = None
            for off in range(5):
                if off in (1, 2, 3) and (off == 2 or (b >= half) == (off == 3)):
                    piece = jnp.where(ids[off] == b, near_ref[h, off], 0.0)
                elif off == 0 and b == half - 1 or off == 4 and b == bins - 1:
                    piece = near_ref[h, off]
                else:
                    continue
                tot = piece if tot is None else tot + piece
            found.append(jnp.sum(tot, axis=0, keepdims=True))
        gl_ref[h] = jnp.sum(jnp.concatenate(found, 0), axis=1, keepdims=True) * scale

    for source in others:
        r_copy(0, z, source).wait_recv()
        da_ref_sum = da_ref_sum + got_ref[source].astype(F32)
    dx_ref[...] = da_ref_sum.astype(BF16)
    for turn in range(n_mp - 1):
        r_copy(turn, z, z).wait_send()
    for to in others:
        d_copy(to, z).wait_send()


def back(n_mp, dctx, q, k, v, e, inv, w_qkv, xf, d_a1, bx, by, bins):
    heads, slot, _ = e.shape
    width = k.shape[1]
    rows, wide = d_a1.shape
    sds = jax.ShapeDtypeStruct
    dma = pltpu.SemaphoreType.DMA
    vm = pltpu.VMEM
    return pl.pallas_call(
        functools.partial(back_kernel, n_mp),
        out_shape=[
            sds((rows, wide), BF16), sds((3, width, wide), F32), sds((3, 8, width), F32), sds((2, HI * heads, LO), F32),
            sds((heads, bins, 1), F32),
        ],
        in_specs=[VMEM] * 9 + [ANY] * 2,
        out_specs=[VMEM] * 5,
        scratch_shapes=[
            vm((n_mp, rows, width), BF16), vm((heads, slot, slot), BF16), vm((3, width, slot), BF16), vm((3, slot, width), BF16),
            vm((2, HI * heads * GROUP, LO * GROUP), F32), vm((heads, 5, TILE, TILE), F32), vm((n_mp - 1, rows, wide), BF16),
            vm((n_mp, rows, wide), BF16), vm((slot, slot), jnp.int32), vm((slot, slot), jnp.int32),
            dma((2,)), dma((n_mp,)), dma((n_mp,)), dma((n_mp - 1,)), dma((n_mp,)),
        ],
        compiler_params=pltpu.CompilerParams(collective_id=1, has_side_effects=True, vmem_limit_bytes=BIG),
        name="back",
    )(dctx, q, k, v, e, inv, w_qkv, xf, d_a1, bx, by)


def layer_norm(values, norm_gain, norm_shift):
    center = jnp.mean(values, axis=-1, keepdims=True)
    spread = values - center
    varied = jnp.mean(spread * spread, axis=-1, keepdims=True)
    return spread * lax.rsqrt(varied + 1e-05) * norm_gain + norm_shift


def exact_gelu(values):
    return jax.nn.gelu(values, approximate=False)


def layer(n_mp, n_dp):
    def on_device(
        hidden_in, text_lens, key_mask, bucket_x, bucket_y, w_qkv, b_q, b_v, w_out, b_out, g_attn, n_attn,
        w_up, b_up, w_down, b_down, g_ffn, n_ffn, t_pos, t_x, t_y, cotangent,
    ):
        rows, wide = hidden_in.shape
        slot = bucket_x.shape[1]
        width = w_qkv.shape[2]
        heads = width // HEAD_DIM
        bx, by = bucket_x[0], bucket_y[0]
        xf, q, k, v, e, inv, ctx, wo, wu, wd = front(
            n_mp, n_dp, hidden_in, w_qkv, b_q, b_v, bx, by, t_x, t_y, t_pos, text_lens, key_mask, w_out, w_up, w_down
        )
        wo = wo.reshape(n_mp, width, wide)
        wu = wu.reshape(n_mp, wide, -1)
        wd = wd.reshape(n_mp, -1, wide)
        b_up_all = lax.all_gather(b_up, "mp", axis=0)

        attn = jnp.einsum("sre,sed->rd", ctx, wo, preferred_element_type=F32)
        resid_one = hidden_in.astype(F32) + attn + b_out.astype(F32)
        normed, norm_back_one = jax.vjp(layer_norm, resid_one, g_attn, n_attn)
        normed_low = normed.astype(BF16)
        normed_full = lax.all_gather(normed_low, "mp", axis=0, tiled=True)
        pre = jnp.einsum("rd,sdf->srf", normed_low, wu, preferred_element_type=F32) + b_up_all.astype(F32)[:, None, :]
        act, gelu_back = jax.vjp(exact_gelu, pre)
        branch = jnp.einsum("srf,sfd->rd", act.astype(BF16), wd, preferred_element_type=F32)
        resid_two = normed + branch + b_down.astype(F32)
        out, norm_back_two = jax.vjp(layer_norm, resid_two, g_ffn, n_ffn)
        layer_out = out.astype(BF16)
        first = lax.axis_index("mp") * rows
        places = first + jnp.arange(rows, dtype=jnp.int32)
        live = (places < 1 + PATCHES + text_lens[0]).astype(F32)
        grad_y = cotangent.astype(F32) * live[:, None]
        d_z2, grad_g_ffn, grad_n_ffn = norm_back_two(grad_y)
        grad_b_down = jnp.sum(d_z2, axis=0)
        d_ffn = d_z2.astype(BF16)
        d_ffn_full = lax.all_gather(d_ffn, "mp", axis=0, tiled=True)
        d_act = jnp.einsum("rd,sfd->srf", d_ffn, wd, preferred_element_type=F32)
        d_pre = gelu_back(d_act)[0].astype(BF16)
        d_normed = d_z2 + jnp.einsum("srf,sdf->rd", d_pre, wu, preferred_element_type=F32)
        d_a1, grad_g_attn, grad_n_attn = norm_back_one(d_normed)
        grad_b_out = jnp.sum(d_a1, axis=0)
        d_attn = d_a1.astype(BF16)
        d_ctx = jnp.einsum("rd,sed->sre", d_attn, wo, preferred_element_type=F32).astype(BF16)
        input_grad, gw, gb, gt, gl = back(n_mp, d_ctx, q, k, v, e, inv, w_qkv, xf, d_a1, bx, by, t_pos.shape[1])

        pre_mine = jnp.dot(normed_full, w_up, preferred_element_type=F32) + b_up.astype(F32)
        act_mine, back_mine = jax.vjp(exact_gelu, pre_mine)
        grad_w_down = jnp.einsum("tf,td->fd", act_mine.astype(BF16), d_ffn_full, preferred_element_type=F32)
        d_act_mine = jnp.einsum("td,fd->tf", d_ffn_full, w_down, preferred_element_type=F32)
        d_pre_mine = back_mine(d_act_mine)[0].astype(BF16)
        grad_w_up = jnp.einsum("td,tf->df", normed_full, d_pre_mine, preferred_element_type=F32)
        grad_b_up = jnp.sum(d_pre_mine.astype(F32), axis=0)
        d_wo = jnp.einsum("sre,rd->sed", ctx, d_attn, preferred_element_type=F32).astype(BF16)
        grad_w_out = lax.psum_scatter(d_wo.reshape(-1, wide), "mp", scatter_dimension=0, tiled=True)

        big = lax.psum((gw.astype(BF16), grad_w_out, grad_w_up.astype(BF16), grad_w_down.astype(BF16)), "dp")
        gw, grad_w_out, grad_w_up, grad_w_down = [g.astype(F32) for g in big]
        grad_w_qkv = jnp.transpose(gw, (0, 2, 1))
        grad_t = gt.reshape(2, HI, heads, LO).transpose(0, 2, 1, 3).reshape(2, heads, HI * LO)
        small = lax.psum((gb[0, 0], gb[2, 0], grad_b_up, gl[:, :, 0], grad_t), "dp")
        grad_b_q, grad_b_v, grad_b_up, grad_t_pos, grad_t = small
        over_rows = lax.psum((grad_b_out, grad_g_attn, grad_n_attn, grad_b_down, grad_g_ffn, grad_n_ffn), ("dp", "mp"))
        grad_b_out, grad_g_attn, grad_n_attn, grad_b_down, grad_g_ffn, grad_n_ffn = over_rows
        return (
            layer_out, input_grad, grad_w_qkv, grad_b_q, grad_b_v, grad_w_out, grad_b_out, grad_g_attn, grad_n_attn,
            grad_w_up, grad_b_up, grad_w_down, grad_b_down, grad_g_ffn, grad_n_ffn, grad_t_pos, grad_t[0], grad_t[1],
        )

    return on_device


def solution(mesh):
    both, split = P(("dp", "mp"), None), P("mp")
    rows_mp, cols_mp, qkv = P("mp", None), P(None, "mp"), P(None, None, "mp")
    doc = P("dp", None, None)
    return jax.shard_map(
        layer(mesh.shape["mp"], mesh.shape["dp"]),
        mesh=mesh,
        in_specs=(
            both, P("dp"), P("dp"), doc, doc, qkv, split, split, rows_mp, P(), P(), P(), cols_mp, split, rows_mp, P(), P(), P(),
            rows_mp, rows_mp, rows_mp, both,
        ),
        out_specs=(
            both, both, qkv, split, split, rows_mp, P(), P(), P(), cols_mp, split, rows_mp, P(), P(), P(), rows_mp, rows_mp, rows_mp,
        ),
        check_vma=False,
    )
```

time: 585 us -> 351 us (0.60); the launches traced: 577 us -> 350 us
  waiting for transfers between devices: 251 us -> 23.6 us
  Pallas kernels: 0 us -> 159 us
  matrix products: 188 us -> 43.9 us
  local copies, waits for them, and re-layouts: 57.7 us -> 10 us
  blocking collectives: 43.6 us -> 76.9 us
    pallas_call x0 -> x2, Pallas kernels: none -> 159 us  [the longest x1 105 us: front(): pl.pallas_call(functools.partial(front_kernel, n_mp, n_dp, plans), out_sh...]
    dot_general x23 -> x10, matrix products: 186 us -> 43.9 us  [the longest x1 13.1 us: on_device(): jnp.einsum('srf,sdf->rd', d_pre, wu, preferred_element_type=F32)]
    reduce_scatter x4 -> x1, waiting for transfers between devices: 145 us -> 10.6 us  [on_device(): lax.psum_scatter(d_wo.reshape(-1, wide), 'mp', scatter_dimension=0, tiled...]
    all_gather x3 -> x1, waiting for transfers between devices: 59.9 us -> 0.02 us  [on_device(): d_ffn_full = lax.all_gather(d_ffn, 'mp', axis=0, tiled=True)]
    dot_general x3 -> x0, local copies, waits for them, and re-layouts: 32.8 us -> none  [the longest x1 11 us: on_device(): jnp.einsum('hb,bij->hij', t_pos, line_hot, preferred_element_type=jnp.flo...]
    all_gather x1, waiting for transfers between devices: 30 us -> 0.01 us  [on_device(): normed_full = lax.all_gather(normed_low, 'mp', axis=0, tiled=True)]
    psum x1, blocking collectives: 18.7 us -> 39.9 us  [on_device(): lax.psum((grad_b_out, grad_g_attn, grad_n_attn, grad_b_down, grad_g_ffn,...]
    all_gather x0 -> x1, blocking collectives: none -> 13.4 us  [on_device(): b_up_all = lax.all_gather(b_up, 'mp', axis=0)]
  transfers between devices with their start and end apart: 9 -> 4, of which waited for: 7 -> 2; matrix products, arithmetic and copies ran while one was open for 32% -> 16% of each run, Pallas kernels for 0% -> 15%
where the time goes in v1:
time: 351 us; the launch traced here: 350 us
  Pallas kernels  159 us (45%)
  blocking collectives  76.9 us (22%)
  matrix products  43.9 us (13%)
  waiting for transfers between devices  23.6 us (7%)
  other arithmetic  21.6 us (6%)
  between operations  14.8 us (4%)
  local copies, waits for them, and re-layouts  10 us (3%)
    pallas_call x1, Pallas kernels, front(): pl.pallas_call(functools.partial(front_kernel, n_mp, n_dp, plans), out_sh...  105 us
    pallas_call x1, Pallas kernels, back(): pl.pallas_call(functools.partial(back_kernel, n_mp), out_shape=[sds((rows...  54 us
    psum x1, blocking collectives, on_device(): lax.psum((grad_b_out, grad_g_attn, grad_n_attn, grad_b_down, grad_g_ffn,...  39.9 us
    psum x1, blocking collectives, on_device(): small = lax.psum((gb[0, 0], gb[2, 0], grad_b_up, gl[:, :, 0], grad_t), 'dp')  23.7 us
    all_gather x1, blocking collectives, on_device(): b_up_all = lax.all_gather(b_up, 'mp', axis=0)  13.4 us
    dot_general x1, matrix products, on_device(): jnp.einsum('srf,sdf->rd', d_pre, wu, preferred_element_type=F32)  13.1 us
    psum x1, waiting for transfers between devices, on_device(): lax.psum((gw.astype(BF16), grad_w_out, grad_w_up.astype(BF16), grad_w_dow...  13 us
    reduce_scatter x1, waiting for transfers between devices, on_device(): lax.psum_scatter(d_wo.reshape(-1, wide), 'mp', scatter_dimension=0, tiled...  10.6 us
  transfers between devices with their start and end apart: 4, of which 2 were waited for; matrix products, arithmetic and copies ran while one was open for 16% of the time, Pallas kernels for 15%

profile of v1, /device:TPU:0, one launch (start us, length us, event | category | flops | bytes accessed | tf_op | source)
XLA Modules:
  0.0 350.0 jit_solution(9033652988267015848)
XLA Ops:
  7.2 0.0 all-gather.5.cloned.1.call-start
  7.2 2.3 copy.51.w_ref
  9.6 1.2 reshape.148.bq_ref
  10.8 1.2 reshape.149.bv_ref
  12.7 1.3 reshape.150.km_ref
  13.9 0.7 convert_element_type.80
  14.6 104.7 %front.1 = (bf16[4,192,768]{2,1,0:T(8,128)(2,1)}, bf16[768,192]{1,0:T(8,128)(2,1)}, bf16[768,192]{1,0:T(8,128)(2,1)}, bf16[768,192]{1,0:T(8,128)(2,1)}, bf16[3,7...) custom-call(bf16[192,768]{1,0:T(8,128)(2,1)} %x_ref.1, ...), custom_call_target="tpu_custom_call" | custom-call | tf_op jit(solution)/shard_map/front/pallas_call | solution.py:291
  119.3 0.0 copy-start.13
  119.4 0.0 copy-start.24
  119.4 0.0 copy-start.27
  119.4 1.9 fusion.65
  121.3 0.2 multiply_reduce_fusion.5
  121.6 0.0 copy-start.19
  121.6 0.0 copy-start.17
  121.6 0.9 fusion.41
  122.5 0.0 all-gather.5.cloned.1.call-update
  122.5 0.0 all-gather.7.cloned.1.call-start
  122.6 0.6 convert_element_type.84
  123.2 3.5 %fusion.46 = f32[4,768,192]{1,2,0:T(8,128)S(1)} fusion(bf16[4,768,768]{2,1,0:T(8,128)(2,1)} %bitcast.181, bf16[192,768]{1,0:T(8,128)(2,1)} %fusion.41), kind=kOutput, calls=%fused_computation.86 | convolution fusion | flops 905969664 | bytes 7372800 | tf_op jit(solution)/shard_map/rd,sdf->srf/dot_general | solution.py:539
  126.8 13.4 %all-gather.1 = bf16[4,1,768]{2,1,0:T(2,128)(2,1)S(1)} all-gather(bf16[1,1,768]{2,1,0:T(2,128)(2,1)S(1)} %reshape.162), channel_id=2, replica_groups=mesh['dp'=8,'mp'=4] {'mp'}, dimensions={0}, use_global_device_ids=true | all-gather | bytes 7680 | tf_op jit(solution)/shard_map/all_gather | solution.py:532
  140.1 0.6 copy.65
  140.7 8.1 %fusion.66 = (f32[192]{0:T(256)S(1)}, f32[192,768]{1,0:T(8,128)S(1)}) fusion(f32[768]{0:T(1024)} %convert_element_type.84, bf16[4,768,768]{2,1,0:T(8,128)(2,1)} %bitcast.196, f32[4,768,192]{1,2,0:T(8,128)S(1)} %fusion.46, f32[4,768]{1,0:T(4,128)} %bitcast.190, f32[768]{0:T(1024)} %param.33, f32[768]{0:T(1024)S(1)} %copy-done.13, f32[192]{0:T(256)S(1)} %fusion.50, ...), kind=kOutput, calls=%fused_computation.116 | convolution fusion | flops 945930048 | bytes 8281344 | tf_op jit(solution)/shard_map/srf,sfd->rd/dot_general | solution.py:541
  148.8 0.2 multiply_reduce_fusion.4
  149.0 0.0 copy-start.21
  149.0 0.6 copy-done.21
  149.6 0.6 fusion.51
  150.2 1.9 multiply_reduce_fusion
  152.1 0.7 multiply_multiply_fusion.6
  152.8 2.2 fusion.62
  155.0 0.6 negate_multiply_fusion.3
  155.5 13.1 %multiply_reduce_fusion.1 = (f32[768]{0:T(1024)}, f32[192]{0:T(256)}, f32[768]{0:T(1024)}, f32[192,768]{1,0:T(8,128)}) fusion(f32[192,768]{1,0:T(8,128)S(1)} %get-tuple-element.86, f32[192]{0:T(256)} %copy-done.17, f32[192]{0:T(256)S(1)} %broadcast_multiply_fusion.1, f32[768]{0:T(1024)S(1)} %copy-done.13, bf16[4,768,768]{2,1,0:T(8,128)(2,1)} %bitcast.182, ...), kind=kOutput, calls=%fused_computation.70 | convolution fusion | flops 1856764160 | bytes 13590528 | tf_op jit(solution)/shard_map/srf,sdf->rd/dot_general | solution.py:555
  168.6 0.7 multiply_multiply_fusion.5
  169.4 1.4 fusion.61
  170.8 1.7 add_reduce_fusion
  172.4 0.0 all-gather.7.cloned.1.call-update
  172.4 0.0 reduce-scatter.2.cloned.1.call-start
  172.5 1.5 convolution_convert_fusion.2
  174.1 0.0 reduce-scatter.2.cloned.1.call-update
  174.1 0.3 all-reduce.5.cloned.1.call-start
  174.4 1.2 fusion.33.g_ref
  175.6 54.0 %back.1 = (bf16[192,768]{1,0:T(8,128)(2,1)}, f32[3,192,768]{2,1,0:T(8,128)}, f32[3,8,192]{2,1,0:T(8,128)}, f32[2,12,16]{2,1,0:T(8,128)}, f32[3,32,1]{2,1,0:T(8,128)}) custom-call(bf16[4,192,192]{2,1,0:T(8,128)(2,1)} %fusion.33.g_ref, bf16[768,192]{1,0:T(8,128)(2,1)} %get-tuple-element.37.q_ref, bf16[768,192]{1,0:T(8,128)(2,1)} %get-tuple-element.38.k_ref, ...), custom_call_target="tpu_custom_call" | custom-call | tf_op jit(solution)/shard_map/back/pallas_call | solution.py:486
  229.7 2.6 convert_bitcast_fusion
  232.2 2.4 fusion.69
  234.6 0.0 all-gather.7.cloned.1.call-done
  234.6 7.7 %convert_reduce_fusion = (f32[768]{0:T(1024)S(1)}, bf16[768,768]{1,0:T(8,128)(2,1)S(1)}, f32[768,768]{1,0:T(8,128)S(1)}) fusion(f32[768,768]{1,0:T(8,128)S(1)} %fusion.69, f32[768]{0:T(1024)S(1)} %convert_element_type.96, bf16[768,768]{1,0:T(8,128)(2,1)} %all-gather.7.cloned.1.call-done, bf16[768,768]{1,0:T(8,128)(2,1)} %param.36), kind=kOutput, calls=%fused_computation.21 | convolution fusion | flops 950205696 | bytes 8263680 | tf_op jit(solution)/shard_map/td,fd->tf/dot_general | solution.py:565
  242.4 2.1 convolution_convert_fusion.1
  244.5 2.3 convolution_convert_fusion
  246.8 0.0 copy-start.25
  246.8 0.0 copy-start.26
  246.9 10.6 %reduce-scatter.2.cloned.1.call-done = bf16[192,768]{1,0:T(8,128)(2,1)} async-done(((bf16[768,768]{1,0:T(8,128)(2,1)}), bf16[192,768]{1,0:T(8,128)(2,1)}) %reduce-scatter.2.cloned.1.call-update) | async-done | bytes 294928 | tf_op jit(solution)/shard_map/reduce_scatter | solution.py:570
  257.4 0.0 all-reduce.5.cloned.1.call-update
  257.5 0.1 reshape.159
  257.6 0.1 reduce
  257.7 39.9 %all-reduce = (f32[768]{0:T(1024)}, f32[768]{0:T(1024)}, f32[768]{0:T(1024)}, f32[768]{0:T(1024)}, f32[768]{0:T(1024)}, /*index=5*/f32[768]{0:T(1024)}) all-reduce(f32[768]{0:T(1024)S(1)} %get-tuple-element.90, f32[768]{0:T(1024)S(1)} %copy-done.25, f32[768]{0:T(1024)S(1)} %copy-done.26, ...), channel_id=1, replica_groups=mesh['dp'=8,'mp'=4] {'dp','mp'}, use_global_device_ids=true, to_apply=%region_14.0 | all-reduce | flops 4608 | bytes 36864 | tf_op jit(solution)/shard_map/psum | solution.py:578
  297.6 0.7 fusion.63
  298.3 23.7 %all-reduce.1 = (f32[192]{0:T(256)}, f32[192]{0:T(256)}, f32[768]{0:T(1024)}, f32[3,32]{1,0:T(4,128)}, f32[2,3,64]{2,0,1:T(2,128)S(1)}) all-reduce(f32[192]{0:T(256)S(1)} %bitcast.193, f32[192]{0:T(256)S(1)} %bitcast.192, f32[768]{0:T(1024)S(1)} %get-tuple-element.71, f32[3,32]{1,0:T(4,128)S(1)} %reduce, ...), channel_id=1, replica_groups=mesh['dp'=8,'mp'=4] {'dp'}, use_global_device_ids=true, to_apply=%region_9.0 | all-reduce | flops 1632 | bytes 13056 | tf_op jit(solution)/shard_map/psum | solution.py:576
  322.0 0.6 copy.67
  322.6 0.6 copy.66
  323.2 13.0 %all-reduce.5.cloned.1.call-done = (bf16[3,768,192]{1,2,0:T(8,128)(2,1)}, bf16[192,768]{1,0:T(8,128)(2,1)}, bf16[768,768]{1,0:T(8,128)(2,1)}, bf16[768,768]{1,0:T(8,128)(2,1)}) async-done(((bf16[3,768,192]{1,2,0:T(8,128)(2,1)}, bf16[192,768]{1,0:T(8,128)(2,1)}, bf16[768,768]{1,0:T(8,128)(2,1)}, bf16[768,768]{1,0:T(8,128)(2,1)}), (bf16[3,768,192]{1,2,0:T(8,128)(2,1)}, bf16[192,768]{1,0:T(8,128)(2,1)}, ...) | async-done | bytes 3538960 | tf_op jit(solution)/shard_map/psum | solution.py:572
  336.1 2.6 transpose.47
  338.8 0.9 convert_element_type.95
  339.6 1.6 convert_element_type.99
  341.2 1.6 convert_element_type.103
  342.8 0.7 copy.74
  (60 shorter events, 0.1 us)
Async XLA Ops:
  7.2 225.0 %all-gather.5.cloned.1.call-start = ((), (), s32[]{:S(2)}) async-start(), calls=%async_computation.2 | async-start | bytes 1474560 | tf_op jit(solution)/shard_map/all_gather | solution.py:538
  14.6 104.8 %copy-start.10 = (bf16[192,768]{1,0:T(8,128)(2,1)S(1)}, bf16[192,768]{1,0:T(8,128)(2,1)}, u32[]{:S(2)}) copy-start(bf16[192,768]{1,0:T(8,128)(2,1)} %x_ref.1) | copy-start | bytes 884740
  119.3 2.2 copy-start.13
  119.4 2.2 copy-start.24
  119.4 3.2 copy-start.27
  121.6 1.6 copy-start.19
  121.6 19.1 %copy-start.17 = (f32[192]{0:T(256)}, f32[192]{0:T(256)S(1)}, u32[]{:S(2)}) copy-start(f32[192]{0:T(256)S(1)} %fusion.50) | copy-start | bytes 2308
  122.5 112.1 %all-gather.7.cloned.1.call-start = ((), (), s32[]{:S(2)}) async-start(), calls=%async_computation.3 | async-start | bytes 1474560 | tf_op jit(solution)/shard_map/all_gather | solution.py:552
  123.2 3.5 %copy-start.22 = (bf16[768]{0:T(1024)(128)(2,1)S(1)}, bf16[768]{0:T(1024)(128)(2,1)}, u32[]{:S(2)}) copy-start(bf16[768]{0:T(1024)(128)(2,1)} %param.35) | copy-start | bytes 4612
  140.7 9.4 %copy-start.12 = (f32[768]{0:T(1024)S(1)}, f32[768]{0:T(1024)}, u32[]{:S(2)}) copy-start(f32[768]{0:T(1024)} %param.38) | copy-start | bytes 9220
  149.0 0.6 copy-start.21
  155.5 13.1 %copy-start.20 = (f32[192]{0:T(256)S(1)}, f32[192]{0:T(256)}, u32[]{:S(2)}) copy-start(f32[192]{0:T(256)} %copy-done.19) | copy-start | bytes 2308
  155.5 13.8 %copy-start.18 = (f32[192]{0:T(256)S(1)}, f32[192]{0:T(256)}, u32[]{:S(2)}) copy-start(f32[192]{0:T(256)} %copy-done.17) | copy-start | bytes 2308
  155.5 15.2 %copy-start.1 = (f32[192,768]{1,0:T(8,128)S(1)}, f32[192,768]{1,0:T(8,128)}, u32[]{:S(2)}) copy-start(f32[192,768]{1,0:T(8,128)} %get-tuple-element.77) | copy-start | bytes 1769476
  168.6 3.9 %copy-start.7 = (bf16[4,192,192]{2,1,0:T(8,128)(2,1)S(1)}, bf16[4,192,192]{2,1,0:T(8,128)(2,1)}, u32[]{:S(2)}) copy-start(bf16[4,192,192]{2,1,0:T(8,128)(2,1)} %get-tuple-element.33) | copy-start | bytes 884740
  170.7 3.6 %copy-start.4 = (bf16[4,8,24,768]{3,2,1,0:T(8,128)(2,1)S(1)}, bf16[4,8,24,768]{3,2,1,0:T(8,128)(2,1)}, u32[]{:S(2)}) copy-start(bf16[4,8,24,768]{3,2,1,0:T(8,128)(2,1)} %get-tuple-element.34) | copy-start | bytes 3538948
  172.4 3.2 copy-start
  172.4 85.0 %reduce-scatter.2.cloned.1.call-start = ((), (), s32[]{:S(2)}) async-start(), calls=%async_computation.1 | async-start | bytes 1474560 | tf_op jit(solution)/shard_map/reduce_scatter | solution.py:570
  172.5 3.1 copy-start.23
  174.1 162.0 %all-reduce.5.cloned.1.call-start = ((), (), s32[]{:S(2)}) async-start(), calls=%async_computation.4 | async-start | bytes 7077888 | tf_op jit(solution)/shard_map/psum | solution.py:572
  229.6 2.6 copy-start.5
  234.6 7.7 %copy-start.28 = (bf16[768,768]{1,0:T(8,128)(2,1)S(1)}, bf16[768,768]{1,0:T(8,128)(2,1)}, u32[]{:S(2)}) copy-start(bf16[768,768]{1,0:T(8,128)(2,1)} %all-gather.5.cloned.1.call-done) | copy-start | bytes 3538948
  242.4 2.2 copy-start.6
  246.8 10.6 %copy-start.16 = (f32[2,12,16]{2,1,0:T(8,128)S(1)}, f32[2,12,16]{2,1,0:T(8,128)}, u32[]{:S(2)}) copy-start(f32[2,12,16]{2,1,0:T(8,128)} %get-tuple-element.47) | copy-start | bytes 4612
  246.8 10.7 %copy-start.11 = (f32[3,32,1]{2,1,0:T(8,128)S(1)}, f32[3,32,1]{2,1,0:T(8,128)}, u32[]{:S(2)}) copy-start(f32[3,32,1]{2,1,0:T(8,128)} %get-tuple-element.46) | copy-start | bytes 1156
  246.8 10.8 %copy-start.14 = (f32[768]{0:T(1024)S(1)}, f32[768]{0:T(1024)}, u32[]{:S(2)}) copy-start(f32[768]{0:T(1024)} %get-tuple-element.50) | copy-start | bytes 9220
  246.8 10.8 %copy-start.15 = (f32[768]{0:T(1024)S(1)}, f32[768]{0:T(1024)}, u32[]{:S(2)}) copy-start(f32[768]{0:T(1024)} %get-tuple-element.53) | copy-start | bytes 9220
  246.8 10.8 %copy-start.25 = (f32[768]{0:T(1024)S(1)}, f32[768]{0:T(1024)}, u32[]{:S(2)}) copy-start(f32[768]{0:T(1024)} %get-tuple-element.48) | copy-start | bytes 9220
  246.8 10.8 %copy-start.26 = (f32[768]{0:T(1024)S(1)}, f32[768]{0:T(1024)}, u32[]{:S(2)}) copy-start(f32[768]{0:T(1024)} %get-tuple-element.52) | copy-start | bytes 9220
  336.1 2.6 copy-start.8
  336.1 3.5 copy-start.3
  338.8 2.4 copy-start.2
  341.2 1.6 copy-start.9
Sparse Core Ops, SparseCore 0:
  122.7 30.5 all-gather.4
  172.6 54.7 all-gather.6
  230.2 27.1 reduce-scatter.1
  262.1 73.9 all-reduce.4

commit v2 on v1

v2 whole, which is shorter than its diff:
```python
import functools
import jax
import jax.numpy as jnp
from jax import lax
from jax.experimental import pallas as pl
from jax.experimental.pallas import tpu as pltpu
from jax.sharding import PartitionSpec as P

HEAD_DIM = 64
PATCHES = 196
THRESHOLDS = (12, 16, 23, 32, 46, 64, 91)
TILE = 128
F32, BF16 = jnp.float32, jnp.bfloat16
MESH = pl.DeviceIdType.MESH
VMEM = pl.BlockSpec(memory_space=pltpu.VMEM)
ANY = pl.BlockSpec(memory_space=pl.ANY)
BIG = 58 << 20


def line_bucket(off):
    mag = jnp.abs(off)
    far = jnp.full(off.shape, 8, jnp.int32)
    for border in THRESHOLDS:
        far = far + (mag >= border).astype(jnp.int32)
    return jnp.where(off > 0, 16, 0) + jnp.where(mag < 8, mag, far)


def dot(a, b, ca, cb):
    return lax.dot_general(a, b, (((ca,), (cb,)), ((), ())), preferred_element_type=F32)


def flip(index, bit):
    step = 2**bit
    return index + step * (1 - 2 * ((index // step) % 2))


def gather_plan(dp_size, reverse):
    bits = list(range(1, dp_size.bit_length() - 1))
    return (bits[::-1] if reverse else bits) + [0]


def plan_label(index, plan):
    label = 0
    for place, bit in enumerate(plan):
        label = label + ((index // 2**bit) % 2) * 2**place
    return label


def front_kernel(
    n_mp, n_dp, plans,
    x_ref, w_ref, bq_ref, bv_ref, bx_hbm, by_hbm, tx_ref, ty_ref, tp_ref, len_ref, km_ref, bu_ref, wo_src, wu_src, wd_src,
    xf_ref, q_ref, k_ref, v_ref, e_ref, inv_ref, cr_ref, bf_ref, wo_out, wu_out, wd_out,
    bx_ref, by_ref, bias_ref, line_ref, cs_ref,
    b_sem, x_send, x_recv, c_send, c_recv, u_send, u_recv, z_send, z_recv, p_send, p_recv,
):
    d = lax.axis_index("dp")
    z = lax.axis_index("mp")
    rows = x_ref.shape[0]
    slot = bx_ref.shape[0]
    width = w_ref.shape[1]
    heads = width // HEAD_DIM
    tiles = slot // TILE
    scale = HEAD_DIM**-0.5
    sources = (wo_src, wu_src, wd_src)
    gathered = (wo_out, wu_out, wd_out)
    others = [(z + k) % n_mp for k in range(1, n_mp)]
    depth = len(plans[0])
    labels = [plan_label(d, plan) for plan in plans]

    loads = []
    for c in range(tiles):
        part = pl.ds(c * TILE, TILE)
        pair = (
            pltpu.make_async_copy(bx_hbm.at[part], bx_ref.at[part], b_sem.at[0, c]),
            pltpu.make_async_copy(by_hbm.at[part], by_ref.at[part], b_sem.at[1, c]),
        )
        for copy in pair:
            copy.start()
        loads.append(pair)

    barrier = pltpu.get_barrier_semaphore()
    peers = [(d, to) for to in others] + [(flip(d, bit), z) for bit in plans[0]]
    for peer in peers:
        pl.semaphore_signal(barrier, inc=1, device_id=peer, device_id_type=MESH)
    xf_ref[z] = x_ref[...]
    bf_ref[z] = jnp.broadcast_to(bu_ref[...].astype(F32).reshape(1, -1), bf_ref.shape[1:])
    pl.semaphore_wait(barrier, len(peers))

    def x_hop(block, to, sem):
        return pltpu.make_async_remote_copy(
            xf_ref.at[block], xf_ref.at[block], x_send.at[sem], x_recv.at[block], device_id=(d, to), device_id_type=MESH
        )

    def w_hop(w, block, to, sem, own=False):
        held = sources[w].at[labels[w]] if own else gathered[w].at[block, labels[w]]
        return pltpu.make_async_remote_copy(
            held, gathered[w].at[block, labels[w]], z_send.at[w, sem], z_recv.at[w, block], device_id=(d, to), device_id_type=MESH
        )

    def all_w(block, to, sem, own=False):
        return [w_hop(w, block, to, sem, own) for w in range(3)]

    def start_all(copies):
        for copy in copies:
            copy.start()

    def on_step(step, act):
        for block, ahead in ((z - step, z + 1), (z + step, z - 1)):

            @pl.when(jnp.logical_and(block >= 0, block < n_mp))
            def _():
                act(block, ahead, jnp.logical_and(ahead >= 0, ahead < n_mp))

    def ends(act):
        for ahead, sem in ((z + 1, z), (z - 1, n_mp)):

            @pl.when(jnp.logical_and(ahead >= 0, ahead < n_mp))
            def _():
                act(ahead, sem)

    ends(lambda ahead, sem: x_hop(z, ahead, sem).start())
    ends(lambda ahead, sem: start_all(all_w(z, ahead, sem, True)))

    def u_copy(to, source):
        return pltpu.make_async_remote_copy(
            bf_ref.at[source], bf_ref.at[source], u_send.at[to], u_recv.at[source], device_id=(d, to), device_id_type=MESH
        )

    for to in others:
        u_copy(to, z).start()

    def x_arrived(step):
        def act(block, ahead, more):
            x_hop(block, z, block).wait_recv()

            @pl.when(more)
            def _():
                x_hop(block, ahead, block).start()

        on_step(step, act)

    def plane_copy(w, place, shard, incoming):
        size = 2**place
        base = (labels[w] // size) * size
        if incoming:
            base = flip(base, place)
        part = gathered[w].at[shard, pl.ds(base, size)]
        return pltpu.make_async_remote_copy(
            part, part, p_send.at[w, place, shard], p_recv.at[w, place, shard],
            device_id=(flip(d, plans[w][place]), z), device_id_type=MESH,
        )

    def w_arrived(step):
        def act(block, ahead, more):
            for w in range(3):
                w_hop(w, block, z, block).wait_recv()

            @pl.when(more)
            def _():
                start_all(all_w(block, ahead, block))

            for w in range(3):
                plane_copy(w, 0, block, False).start()

        on_step(step, act)

    def plane_next(step, place):
        def act(block, ahead, more):
            for w in range(3):
                plane_copy(w, place - 1, block, True).wait_recv()
                plane_copy(w, place, block, False).start()

        on_step(step, act)

    def plane_done(step):
        def act(block, ahead, more):
            for w in range(3):
                plane_copy(w, depth - 1, block, True).wait_recv()

        on_step(step, act)

    tab = [
        jnp.broadcast_to(
            jnp.concatenate([tx_ref[h : h + 1, :].astype(F32), ty_ref[h : h + 1, :].astype(F32)], axis=1) * scale, (8, TILE)
        )
        for h in range(heads)
    ]
    bins_x = tx_ref.shape[1]
    pad = jnp.zeros((1, TILE - tp_ref.shape[1]), F32)
    ltab = [
        jnp.broadcast_to(jnp.concatenate([tp_ref[h : h + 1, :].astype(F32) * scale, pad], axis=1), (8, TILE))
        for h in range(heads)
    ]
    ci = lax.broadcasted_iota(jnp.int32, (8, TILE), 1)
    ri = lax.broadcasted_iota(jnp.int32, (8, TILE), 0)

    @pl.loop(0, TILE // 8)
    def _(g):
        at = pl.ds(pl.multiple_of(g * 8, 8), 8)
        for off in range(5):
            idx = line_bucket(ci - ri - g * 8 + (off - 2) * TILE)
            for h in range(heads):
                line_ref[h, off, at, :] = jnp.take_along_axis(ltab[h], idx, axis=1)

    place_ids = lax.broadcasted_iota(jnp.int32, (1, slot), 1)
    live = place_ids < 1 + PATCHES + len_ref[0]
    seen = jnp.where(live & ((km_ref[...].reshape(1, slot) == 1) | (place_ids == 0)), 0.0, -1e30)

    def bias_chunk(c):
        for copy in loads[c]:
            copy.wait()

        @pl.loop(0, TILE // 8)
        def _(g):
            at = pl.ds(pl.multiple_of(c * TILE + g * 8, 8), 8)
            near = pl.ds(pl.multiple_of(g * 8, 8), 8)
            for j in range(tiles):
                cols = slice(j * TILE, (j + 1) * TILE)
                ix = bx_ref[at, cols]
                iy = by_ref[at, cols] + bins_x
                hide = seen[:, cols]
                off = min(max(j - c + 2, 0), 4)
                for h in range(heads):
                    b = jnp.take_along_axis(tab[h], ix, axis=1) + jnp.take_along_axis(tab[h], iy, axis=1)
                    bias_ref[h, at, cols] = (b + line_ref[h, off, near, :]) + hide

    for c in range(tiles):
        if c == tiles // 2:
            x_arrived(1)
        bias_chunk(c)
    w_arrived(1)
    x_arrived(2)
    plane_next(1, 1)
    w_arrived(2)
    for place in range(2, depth):
        plane_next(1, place)
    x_arrived(3)

    lane = lax.broadcasted_iota(jnp.int32, (1, width), 1)
    mine = [(lane >= h * HEAD_DIM) & (lane < (h + 1) * HEAD_DIM) for h in range(heads)]
    b_q = bq_ref[...].astype(F32).reshape(1, width)
    b_v = bv_ref[...].astype(F32).reshape(1, width)
    for b in range(n_mp):
        at = pl.ds(b * rows, rows)
        xb = xf_ref[b]
        q_ref[at, :] = ((dot(xb, w_ref[0], 1, 1) + b_q).astype(BF16).astype(F32) * scale).astype(BF16)
        k_ref[at, :] = dot(xb, w_ref[1], 1, 1).astype(BF16)
        v_ref[at, :] = (dot(xb, w_ref[2], 1, 1) + b_v).astype(BF16)

    def c_copy(turn, to, source):
        return pltpu.make_async_remote_copy(
            cs_ref.at[turn], cr_ref.at[source], c_send.at[turn], c_recv.at[source], device_id=(d, to), device_id_type=MESH
        )

    def attend(turn):
        to = (z + 1 + turn) % n_mp
        at = pl.ds(pl.multiple_of(to * rows, rows), rows)
        q = q_ref[at, :]
        out = jnp.zeros((rows, width), F32)
        for h in range(heads):
            s = dot(jnp.where(mine[h], q, jnp.zeros((), BF16)), k_ref[...], 1, 1) + bias_ref[h, at, :]
            top = jnp.max(s, axis=1, keepdims=True)
            e = jnp.exp(s - top).astype(BF16)
            e_ref[h, at, :] = e
            inv = 1.0 / jnp.sum(e.astype(F32), axis=1, keepdims=True)
            inv_ref[at, h : h + 1] = inv
            out = out + jnp.where(mine[h], dot(e, v_ref[...], 1, 0) * inv, 0.0)
        if turn == n_mp - 1:
            cr_ref[z] = out.astype(BF16)
        else:
            cs_ref[turn] = out.astype(BF16)
            c_copy(turn, to, z).start()

    between = {0: lambda: plane_next(2, 1), 1: lambda: w_arrived(3)}
    for turn in range(n_mp):
        attend(turn)
        if turn in between:
            between[turn]()

    for place in range(2, depth):
        plane_next(2, place)
    for place in range(1, depth):
        plane_next(3, place)
    for step in range(1, n_mp):
        plane_done(step)

    for source in others:
        c_copy(0, z, source).wait_recv()
        u_copy(z, source).wait_recv()
    for turn in range(n_mp - 1):
        c_copy(turn, z, z).wait_send()
    for to in others:
        u_copy(to, z).wait_send()

    def wait_all(copies):
        for copy in copies:
            copy.wait_send()

    def sent(block, ahead, more):
        @pl.when(more)
        def _():
            wait_all([x_hop(block, ahead, block)] + all_w(block, ahead, block))

        for w in range(3):
            for place in range(depth):
                plane_copy(w, place, block, False).wait_send()

    ends(lambda ahead, sem: wait_all([x_hop(z, ahead, sem)] + all_w(z, ahead, sem, True)))
    for step in range(1, n_mp):
        on_step(step, sent)


def front(n_mp, n_dp, x, w_qkv, b_q, b_v, bx, by, t_x, t_y, t_pos, text_lens, key_mask, b_up, w_out, w_up, w_down):
    rows, wide = x.shape
    slot = bx.shape[0]
    width = w_qkv.shape[1]
    heads = width // HEAD_DIM
    plans = [gather_plan(n_dp, False), gather_plan(n_dp, False), gather_plan(n_dp, True)]
    depth = len(plans[0])
    slices = [w.reshape(n_dp, w.shape[0] // n_dp, w.shape[1]) for w in (w_out, w_up, w_down)]
    sds = jax.ShapeDtypeStruct
    dma = pltpu.SemaphoreType.DMA
    return pl.pallas_call(
        functools.partial(front_kernel, n_mp, n_dp, plans),
        out_shape=[
            sds((n_mp, rows, wide), BF16), sds((slot, width), BF16), sds((slot, width), BF16), sds((slot, width), BF16),
            sds((heads, slot, slot), BF16), sds((slot, heads), F32), sds((n_mp, rows, width), BF16),
            sds((n_mp, 8) + b_up.shape, F32),
        ] + [sds((n_mp,) + s.shape, BF16) for s in slices],
        in_specs=[VMEM] * 4 + [ANY, ANY] + [VMEM] * 3 + [pl.BlockSpec(memory_space=pltpu.SMEM), VMEM, VMEM] + [ANY] * 3,
        out_specs=[VMEM] * 8 + [ANY] * 3,
        scratch_shapes=[
            pltpu.VMEM((slot, slot), jnp.int32), pltpu.VMEM((slot, slot), jnp.int32), pltpu.VMEM((heads, slot, slot), F32),
            pltpu.VMEM((heads, 5, TILE, TILE), F32), pltpu.VMEM((n_mp - 1, rows, width), BF16),
            dma((2, slot // TILE)), dma((n_mp + 1,)), dma((n_mp,)), dma((n_mp - 1,)), dma((n_mp,)), dma((n_mp,)), dma((n_mp,)),
            dma((3, n_mp + 1)), dma((3, n_mp)), dma((3, depth, n_mp)), dma((3, depth, n_mp)),
        ],
        compiler_params=pltpu.CompilerParams(collective_id=0, has_side_effects=True, vmem_limit_bytes=BIG),
        name="front",
    )(x, w_qkv, b_q, b_v, bx, by, t_x, t_y, t_pos, text_lens, key_mask, b_up, *slices)

EPS = 1e-05


def mid_kernel(
    n_mp,
    x_ref, ctx_ref, wo_own, wu_own, wd_own, wo_hbm, wu_hbm, wd_hbm, bu_ref, bo_ref, ga_ref, na_ref, bd_ref, gf_ref, nf_ref,
    cot_ref, len_ref,
    lo_ref, nl_ref, df_ref, da_ref, dc_ref, go_ref, gs_ref,
    wo_ref, wu_ref, wd_ref, gp_ref, sem,
):
    z = lax.axis_index("mp")
    rows, wide = x_ref.shape
    others = [(z + k) % n_mp for k in range(1, n_mp)]
    loads = []
    for w, (own, rest, held) in enumerate(((wo_own, wo_hbm, wo_ref), (wu_own, wu_hbm, wu_ref), (wd_own, wd_hbm, wd_ref))):
        copies = [pltpu.make_async_copy(own, held.at[z], sem.at[w, z])]
        copies += [pltpu.make_async_copy(rest.at[s], held.at[s], sem.at[w, s]) for s in others]
        for copy in copies:
            copy.start()
        loads.append(copies)

    def vec(ref):
        return ref[...].astype(F32).reshape(1, wide)

    def norm(values):
        spread = values - jnp.mean(values, axis=1, keepdims=True)
        rate = lax.rsqrt(jnp.mean(spread * spread, axis=1, keepdims=True) + EPS)
        return spread * rate, rate

    def norm_back(up, gain, hat, rate):
        scaled = up * gain
        first = jnp.mean(scaled, axis=1, keepdims=True)
        second = jnp.mean(scaled * hat, axis=1, keepdims=True)
        return rate * (scaled - first - hat * second)

    def total(values):
        return jnp.sum(values, axis=0, keepdims=True)

    for copy in loads[0]:
        copy.wait()
    attn = dot(ctx_ref[0], wo_ref[0], 1, 0)
    for s in range(1, n_mp):
        attn = attn + dot(ctx_ref[s], wo_ref[s], 1, 0)
    hat_one, rate_one = norm(x_ref[...].astype(F32) + attn + vec(bo_ref))
    normed = hat_one * vec(ga_ref) + vec(na_ref)
    low = normed.astype(BF16)
    nl_ref[...] = low

    for copies in loads[1:]:
        for copy in copies:
            copy.wait()
    ffn = jnp.zeros((rows, wide), F32)
    for s in range(n_mp):
        pre = dot(low, wu_ref[s], 1, 0) + bu_ref[s, 0:1, :]
        cdf = 0.5 * (1.0 + lax.erf(pre * (0.5**0.5)))
        gp_ref[s] = cdf + pre * (jnp.exp(-0.5 * pre * pre) * 0.3989422804014327)
        ffn = ffn + dot((pre * cdf).astype(BF16), wd_ref[s], 1, 0)
    hat_two, rate_two = norm(normed + ffn + vec(bd_ref))
    lo_ref[...] = (hat_two * vec(gf_ref) + vec(nf_ref)).astype(BF16)

    place = z * rows + lax.broadcasted_iota(jnp.int32, (rows, 1), 0)
    grad_y = jnp.where(place < 1 + PATCHES + len_ref[0], cot_ref[...].astype(F32), 0.0)
    d_two = norm_back(grad_y, vec(gf_ref), hat_two, rate_two)
    d_ffn = d_two.astype(BF16)
    df_ref[...] = d_ffn
    d_normed = d_two
    for s in range(n_mp):
        d_pre = (dot(d_ffn, wd_ref[s], 1, 1) * gp_ref[s]).astype(BF16)
        d_normed = d_normed + dot(d_pre, wu_ref[s], 1, 1)
    d_one = norm_back(d_normed, vec(ga_ref), hat_one, rate_one)
    da_ref[...] = d_one
    d_attn = d_one.astype(BF16)
    for s in range(n_mp):
        dc_ref[s] = dot(d_attn, wo_ref[s], 1, 1).astype(BF16)
        go_ref[s] = dot(ctx_ref[s].astype(F32).T.astype(BF16), d_attn, 1, 0).astype(BF16)
    gs_ref[...] = jnp.concatenate(
        [
            total(grad_y * hat_two), total(grad_y), total(d_two), total(d_normed * hat_one), total(d_normed), total(d_one),
            jnp.zeros((2, wide), F32),
        ],
        axis=0,
    )


def middle(n_mp, x, ctx, owns, gathered, b_up_all, b_out, g_attn, n_attn, b_down, g_ffn, n_ffn, cotangent, text_lens):
    rows, wide = x.shape
    sds = jax.ShapeDtypeStruct
    width, units = owns[0].shape[0], owns[1].shape[1]
    return pl.pallas_call(
        functools.partial(mid_kernel, n_mp),
        out_shape=[
            sds((rows, wide), BF16), sds((rows, wide), BF16), sds((rows, wide), BF16), sds((rows, wide), F32),
            sds((n_mp, rows, width), BF16), sds((n_mp, width, wide), BF16), sds((8, wide), F32),
        ],
        in_specs=[VMEM] * 2 + [ANY] * 6 + [VMEM] * 8 + [pl.BlockSpec(memory_space=pltpu.SMEM)],
        out_specs=[VMEM] * 7,
        scratch_shapes=[
            pltpu.VMEM((n_mp, width, wide), BF16), pltpu.VMEM((n_mp, wide, units), BF16), pltpu.VMEM((n_mp, units, wide), BF16),
            pltpu.VMEM((n_mp, rows, units), F32), pltpu.SemaphoreType.DMA((3, n_mp)),
        ],
        compiler_params=pltpu.CompilerParams(vmem_limit_bytes=BIG),
        name="middle",
    )(x, ctx, *owns, *gathered, b_up_all, b_out, g_attn, n_attn, b_down, g_ffn, n_ffn, cotangent, text_lens)

HI, LO, GROUP, STEP = 4, 16, 16, 2
PACK = 48


def sums_in_kernel(n_dp, *sizes):
    return all(size % (8 * n_dp) == 0 for size in sizes)


def rear_kernel(
    n_mp, n_dp, plans, summed,
    nl_ref, df_ref, dc_in, go_ref, gs_ref, da_ref, q_ref, k_ref, v_ref, e_ref, inv_ref, w_ref, xf_ref, wu_ref, wd_ref, bu_ref,
    bx_hbm, by_hbm,
    ig_ref, pack_ref, uo_ref, do_ref, qo_ref, oo_ref,
    dc_ref, ds_ref, dt_ref, dn_ref, acc_ref, near_ref, part_ref, got_ref, bx_ref, by_ref, nf_ref, dff_ref, act_ref, gp_ref,
    sp_ref, b_sem, d_send, d_recv, r_send, r_recv, h_send, h_recv,
    *for_sums,
):
    if summed:
        (
            ua_ref, da2_ref, qa_ref, oa_ref, us_ref, ds2_ref, qs_ref, os_ref, ur_ref, dr_ref, qr_ref, or_ref, oz_ref, sr_ref, sz_ref,
            rs_send, rs_recv, ag_send, ag_recv, oz_send, oz_recv, sp_send, sp_recv, sz_send, sz_recv,
        ) = for_sums
    d = lax.axis_index("dp")
    z = lax.axis_index("mp")
    heads, slot, _ = e_ref.shape
    width = k_ref.shape[1]
    rows, wide = da_ref.shape
    tiles = slot // TILE
    scale = HEAD_DIM**-0.5
    others = [(z + k) % n_mp for k in range(1, n_mp)]
    depth = len(plans[0])

    loads = [pltpu.make_async_copy(bx_hbm, bx_ref, b_sem.at[0]), pltpu.make_async_copy(by_hbm, by_ref, b_sem.at[1])]
    for copy in loads:
        copy.start()
    barrier = pltpu.get_barrier_semaphore()
    peers = [(d, to) for to in others] + [(flip(d, bit), z) for bit in plans[0] if summed]
    for peer in peers:
        pl.semaphore_signal(barrier, inc=1, device_id=peer, device_id_type=MESH)
    nf_ref[z] = nl_ref[...]
    dff_ref[z] = df_ref[...]
    dc_ref[z] = dc_in[z]
    pl.semaphore_wait(barrier, len(peers))

    def remote(src, dst, send, recv, to):
        return pltpu.make_async_remote_copy(src, dst, send, recv, device_id=to, device_id_type=MESH)

    def d_copy(to, source):
        return remote(dc_in.at[to], dc_ref.at[source], d_send.at[to], d_recv.at[source], (d, to))

    for to in others:
        d_copy(to, z).start()

    lines = (nf_ref, dff_ref)

    def hop(a, block, to, sem):
        return remote(lines[a].at[block], lines[a].at[block], h_send.at[a, sem], h_recv.at[a, block], (d, to))

    def ends(act):
        for ahead, sem in ((z + 1, z), (z - 1, n_mp)):

            @pl.when(jnp.logical_and(ahead >= 0, ahead < n_mp))
            def _():
                act(ahead, sem)

    def on_step(step, act):
        for block, ahead in ((z - step, z + 1), (z + step, z - 1)):

            @pl.when(jnp.logical_and(block >= 0, block < n_mp))
            def _():
                act(block, ahead, jnp.logical_and(ahead >= 0, ahead < n_mp))

    def arrived(a, step):
        def act(block, ahead, more):
            hop(a, block, z, block).wait_recv()

            @pl.when(more)
            def _():
                hop(a, block, ahead, block).start()

        on_step(step, act)

    for a in range(2):
        ends(lambda ahead, sem: hop(a, z, ahead, sem).start())

    items = ((None, None, None, plans[0]),) if not summed else (
        (ua_ref, us_ref, ur_ref, plans[0]), (da2_ref, ds2_ref, dr_ref, plans[1]), (qa_ref, qs_ref, qr_ref, plans[0]),
        (oa_ref, os_ref, or_ref, plans[1]),
    )
    outs = (uo_ref, do_ref, qo_ref, oo_ref)
    labels = [plan_label(d, item[3]) for item in items]

    def halves(i, place):
        size = 2**place
        base = (labels[i] // size) * size
        return pl.ds(base, size), pl.ds(flip(base, place), size), size

    def rs_copy(i, place):
        _, away, size = halves(i, place)
        _, staged, got, plan = items[i]
        return remote(staged.at[away], got.at[pl.ds(size, size)], rs_send.at[i, place], rs_recv.at[i, place], (flip(d, plan[place]), z))

    def rs_start(i, place):
        if not summed:
            return
        _, away, _ = halves(i, place)
        items[i][1][away] = items[i][0][away].astype(BF16)
        rs_copy(i, place).start()

    def rs_finish(i, place):
        if not summed:
            return
        kept, _, size = halves(i, place)
        rs_copy(i, place).wait_recv()
        total, _, got, _ = items[i]
        total[kept] = total[kept] + got[size : 2 * size].astype(F32)

    def ag_copy(i, place, incoming=False):
        kept, away, _ = halves(i, place)
        part = outs[i].at[away if incoming else kept]
        return remote(part, part, ag_send.at[i, place], ag_recv.at[i, place], (flip(d, items[i][3][place]), z))

    if summed:
        for s in range(n_mp):
            oa_ref[:, s] = go_ref[s].astype(F32).reshape(n_dp, -1, wide)
    else:
        oo_ref[...] = go_ref[...]
    rs_start(3, depth - 1)

    sp_ref[0:8, :] = gs_ref[...]

    def sz_copy(to, source):
        return remote(gs_ref, sz_ref.at[source], sz_send.at[to], sz_recv.at[source], (d, to))

    if summed:
        for to in others:
            sz_copy(to, z).start()

    lane = lax.broadcasted_iota(jnp.int32, (1, width), 1)
    mine = [(lane >= h * HEAD_DIM) & (lane < (h + 1) * HEAD_DIM) for h in range(heads)]
    zero = jnp.zeros((), BF16)
    factor = jnp.zeros((slot, width), F32)
    for h in range(heads):
        factor = jnp.where(mine[h], inv_ref[:, h : h + 1], factor)
    qt = q_ref[...].astype(F32).T.astype(BF16)
    for source in others:
        d_copy(source, source).wait_recv()
    for a in range(2):
        arrived(a, 1)

    dctx = dc_ref[...].reshape(slot, width)
    gt = (dctx.astype(F32) * factor).T.astype(BF16)
    block = 384
    dq = [None] * (slot // block)
    for h in range(heads):
        hs = slice(h * HEAD_DIM, (h + 1) * HEAD_DIM)
        dk = dv = None
        for r in range(slot // block):
            rs = slice(r * block, (r + 1) * block)
            e = e_ref[h, rs, :]
            p = e.astype(F32) * inv_ref[rs, h : h + 1]
            dp = dot(jnp.where(mine[h], dctx[rs, :], zero), v_ref[...], 1, 1)
            ds = (p * (dp - jnp.sum(p * dp, axis=1, keepdims=True))).astype(BF16)
            ds_ref[h, rs, :] = ds
            a = jnp.where(mine[h], dot(ds, k_ref[...], 1, 0), 0.0)
            dq[r] = a if dq[r] is None else dq[r] + a
            b = dot(qt[hs, rs], ds, 1, 0)
            dk = b if dk is None else dk + b
            c = dot(gt[hs, rs], e, 1, 0)
            dv = c if dv is None else dv + c
        dt_ref[1, hs, :] = dk.astype(BF16)
        dt_ref[2, hs, :] = dv.astype(BF16)
    for r in range(slot // block):
        rs = slice(r * block, (r + 1) * block)
        low = (dq[r] * scale).astype(BF16)
        dn_ref[0, rs, :] = low
        dt_ref[0, :, rs] = low.astype(F32).T.astype(BF16)
    for c in (1, 2):
        dn_ref[c] = dt_ref[c].astype(F32).T.astype(BF16)

    for a in range(2):
        arrived(a, 2)
    rs_finish(3, depth - 1)
    rs_start(3, depth - 2)

    def r_copy(turn, to, source):
        return remote(part_ref.at[turn], got_ref.at[source], r_send.at[turn], r_recv.at[source], (d, to))

    def dx_part(to):
        at = pl.ds(pl.multiple_of(to * rows, rows), rows)
        out = dot(dn_ref[0, at, :], w_ref[0], 1, 0)
        for c in (1, 2):
            out = out + dot(dn_ref[c, at, :], w_ref[c], 1, 0)
        return out

    for turn in range(n_mp - 1):
        part_ref[turn] = dx_part(others[turn]).astype(BF16)
        r_copy(turn, others[turn], z).start()
    dx = da_ref[...] + dx_part(z)

    ones = jnp.ones((8, slot), BF16)
    xf = xf_ref[...].reshape(slot, wide)
    def keep(i, values, part=0, parts=1):
        if summed:
            total = items[i][0]
            count_ = total.shape[0] // parts
            total[part * count_ : (part + 1) * count_] = values.reshape(count_, -1, values.shape[1])
        else:
            outs[i][part] = values.astype(BF16)

    for c in range(3):
        gw = dot(dt_ref[c], xf, 1, 0)
        if summed:
            qa_ref[:, c] = gw.reshape(n_dp, -1, wide)
        else:
            qo_ref[c] = gw.astype(BF16)
    sp_ref[9:10, 0:width] = dot(ones, dn_ref[0], 1, 0)[0:1]
    sp_ref[10:11, 0:width] = dot(ones, dn_ref[2], 1, 0)[0:1]
    rs_start(2, depth - 1)

    for copy in loads:
        copy.wait()
    acc_ref[...] = jnp.zeros_like(acc_ref)
    one = jnp.ones((), BF16)

    def count(first, last):
        @pl.loop(first, last)
        def _(i):
            at = [pl.ds(pl.multiple_of(i * GROUP * STEP + g * GROUP, GROUP), GROUP) for g in range(STEP)]
            ds = [[ds_ref[h, at[g], :] for h in range(heads)] for g in range(STEP)]
            for t, b_ref in enumerate((bx_ref, by_ref)):
                tot = None
                for g in range(STEP):
                    b = b_ref[at[g], :]
                    hi = (b >> 4).astype(F32).astype(BF16)
                    lo = (b & 15).astype(F32).astype(BF16)
                    left = []
                    for a in range(HI):
                        m = hi == jnp.asarray(a, BF16)
                        left += [jnp.where(m, ds[g][h], zero) for h in range(heads)]
                    right = [jnp.where(lo == jnp.asarray(c, BF16), one, zero) for c in range(LO)]
                    o = dot(jnp.concatenate(left, 0), jnp.concatenate(right, 0), 1, 1)
                    tot = o if tot is None else tot + o
                acc_ref[t] += tot

    waiting = {2: depth - 1, 3: depth - 2}

    def onward(i):
        if waiting[i] > 0:
            rs_finish(i, waiting[i])
            waiting[i] -= 1
            rs_start(i, waiting[i])

    trips = slot // (GROUP * STEP)
    for part in range(4):
        count(part * trips // 4, (part + 1) * trips // 4)
        onward(2)
        onward(3)
    for i in (2, 3):
        while waiting[i] > 0:
            onward(i)

    m, n = HI * heads * GROUP, LO * GROUP
    same = (lax.broadcasted_iota(jnp.int32, (m, n), 0) & (GROUP - 1)) == (lax.broadcasted_iota(jnp.int32, (m, n), 1) & (GROUP - 1))
    pick = (lax.broadcasted_iota(jnp.int32, (n, LO), 0) // GROUP == lax.broadcasted_iota(jnp.int32, (n, LO), 1)).astype(F32)
    for t in range(2):
        kept = jnp.sum(jnp.where(same, acc_ref[t], 0.0).reshape(m // GROUP, GROUP, n), axis=1)
        found = lax.dot_general(
            kept, pick, (((1,), (0,)), ((), ())), precision=lax.Precision.HIGHEST, preferred_element_type=F32
        )
        sp_ref[16 : 16 + HI * heads, t * TILE : t * TILE + LO] = found * scale

    for h in range(heads):
        for off in range(5):
            tot = jnp.zeros((TILE, TILE), F32)
            for i in range(tiles):
                for j in range(tiles):
                    if min(max(j - i, -2), 2) + 2 == off:
                        tot = tot + ds_ref[h, i * TILE : (i + 1) * TILE, j * TILE : (j + 1) * TILE].astype(F32)
            near_ref[h, off] = tot
    ci = lax.broadcasted_iota(jnp.int32, (TILE, TILE), 1)
    ri = lax.broadcasted_iota(jnp.int32, (TILE, TILE), 0)
    bins = 32
    half = bins // 2
    ids = [line_bucket(ci - ri + (off - 2) * TILE) for off in range(5)]
    for h in range(heads):
        found = []
        for b in range(bins):
            tot = None
            for off in range(5):
                if off in (1, 2, 3) and (off == 2 or (b >= half) == (off == 3)):
                    piece = jnp.where(ids[off] == b, near_ref[h, off], 0.0)
                elif off == 0 and b == half - 1 or off == 4 and b == bins - 1:
                    piece = near_ref[h, off]
                else:
                    continue
                tot = piece if tot is None else tot + piece
            found.append(jnp.sum(tot, axis=0, keepdims=True))
        lines_h = jnp.sum(jnp.concatenate(found, 0), axis=1, keepdims=True) * scale
        sp_ref[16 : 16 + bins, (2 + h) * TILE : (2 + h) * TILE + 1] = lines_h

    for a in range(2):
        arrived(a, 3)
    b_up = bu_ref[...].astype(F32).reshape(1, -1)
    for b in range(n_mp):
        at = slice(b * rows, (b + 1) * rows)
        pre = dot(nf_ref[b], wu_ref[...], 1, 0) + b_up
        cdf = 0.5 * (1.0 + lax.erf(pre * (0.5**0.5)))
        act_ref[at, :] = (pre * cdf).astype(BF16)
        gp_ref[at, :] = cdf + pre * (jnp.exp(-0.5 * pre * pre) * 0.3989422804014327)
    dff = dff_ref[...].reshape(slot, wide)
    keep(1, dot(act_ref[...], dff, 0, 0))
    rs_start(1, depth - 1)
    act_ref[...] = (dot(dff, wd_ref[...], 1, 1) * gp_ref[...]).astype(BF16)
    keep(0, dot(nf_ref[...].reshape(slot, wide), act_ref[...], 0, 0))
    rs_start(0, depth - 1)
    sp_ref[8:9, :] = dot(ones, act_ref[...], 1, 0)[0:1]

    def sp_copy(place):
        return remote(sp_ref, sr_ref.at[place], sp_send.at[place], sp_recv.at[place], (flip(d, plans[0][place]), z))

    def oz_copy(to, source):
        return remote(os_ref.at[labels[3], to], oz_ref.at[source], oz_send.at[to], oz_recv.at[source], (d, to))

    def finish_sums():
        for source in others:
            sz_copy(z, source).wait_recv()
            sp_ref[0:8, :] = sp_ref[0:8, :] + sz_ref[source]

        sp_copy(depth - 1).start()
        rs_finish(2, 0)
        rs_finish(3, 0)
        qo_ref[labels[2]] = qa_ref[labels[2]].astype(BF16)
        ag_copy(2, 0).start()
        os_ref[labels[3]] = oa_ref[labels[3]].astype(BF16)
        for to in others:
            oz_copy(to, z).start()
        for place in range(depth - 1, -1, -1):
            for i in (1, 0):
                rs_finish(i, place)
                if place:
                    rs_start(i, place - 1)
            sp_copy(place).wait_send()
            sp_copy(place).wait_recv()
            sp_ref[...] = sp_ref[...] + sr_ref[place]
            if place:
                sp_copy(place - 1).start()
            if place == depth - 1:
                out = oa_ref[labels[3], z]
                for source in others:
                    oz_copy(z, source).wait_recv()
                    out = out + oz_ref[source].astype(F32)
                oo_ref[labels[3]] = out.astype(BF16)
                ag_copy(3, 0).start()
        for i, ref in ((0, uo_ref), (1, do_ref)):
            ref[labels[i]] = items[i][0][labels[i]].astype(BF16)
            ag_copy(i, 0).start()
        pack_ref[...] = sp_ref[...]
        for place in range(1, depth):
            for i in (2, 3, 0, 1):
                ag_copy(i, place - 1, True).wait_recv()
                ag_copy(i, place).start()

    if summed:
        finish_sums()
    else:
        pack_ref[...] = sp_ref[...]

    for source in others:
        r_copy(0, z, source).wait_recv()
        dx = dx + got_ref[source].astype(F32)
    ig_ref[...] = dx.astype(BF16)

    for turn in range(n_mp - 1):
        r_copy(turn, z, z).wait_send()
    for to in others:
        d_copy(to, z).wait_send()
    if summed:
        for i in range(4):
            ag_copy(i, depth - 1, True).wait_recv()
        for to in others:
            sz_copy(to, z).wait_send()
            oz_copy(to, z).wait_send()
        for i in range(4):
            for place in range(depth):
                rs_copy(i, place).wait_send()
                ag_copy(i, place).wait_send()
    for a in range(2):
        ends(lambda ahead, sem: hop(a, z, ahead, sem).wait_send())

        def sent(block, ahead, more):
            @pl.when(more)
            def _():
                hop(a, block, ahead, block).wait_send()

        for step in range(1, n_mp):
            on_step(step, sent)


def rear(n_mp, n_dp, nl, df, dctx, d_wo, over_rows, d_a1, q, k, v, e, inv, w_t, xf, w_up, w_down, b_up, bx, by):
    heads, slot, _ = e.shape
    width = k.shape[1]
    rows, wide = d_a1.shape
    units = w_up.shape[1]
    plans = [gather_plan(n_dp, False), gather_plan(n_dp, True)]
    depth = len(plans[0])
    summed = sums_in_kernel(n_dp, width, units, wide)
    if summed:
        ru, rd, ro = wide // n_dp, units // n_dp, width // n_dp
        shapes = [(n_dp, ru, units), (n_dp, rd, wide), (n_dp, 3, ro, wide), (n_dp, ro, wide)]
    else:
        shapes = [(1, wide, units), (1, units, wide), (3, width, wide), (n_mp, width, wide)]
    sds = jax.ShapeDtypeStruct
    dma = pltpu.SemaphoreType.DMA
    vm = pltpu.VMEM
    return pl.pallas_call(
        functools.partial(rear_kernel, n_mp, n_dp, plans, summed),
        out_shape=[
            sds((rows, wide), BF16), sds((PACK, wide), F32)] + [sds(shape, BF16) for shape in shapes],
        in_specs=[VMEM] * 16 + [ANY] * 2,
        out_specs=[VMEM] * 6,
        scratch_shapes=[
            vm((n_mp, rows, width), BF16), vm((heads, slot, slot), BF16), vm((3, width, slot), BF16), vm((3, slot, width), BF16),
            vm((2, HI * heads * GROUP, LO * GROUP), F32), vm((heads, 5, TILE, TILE), F32), vm((n_mp - 1, rows, wide), BF16),
            vm((n_mp, rows, wide), BF16), vm((slot, slot), jnp.int32), vm((slot, slot), jnp.int32),
            vm((n_mp, rows, wide), BF16), vm((n_mp, rows, wide), BF16), vm((slot, units), BF16), vm((slot, units), F32),
            vm((PACK, wide), F32), dma((2,)), dma((n_mp,)), dma((n_mp,)), dma((n_mp - 1,)), dma((n_mp,)), dma((2, n_mp + 1)), dma((2, n_mp)),
        ] + ([
            vm((n_dp, ru, units), F32), vm((n_dp, rd, wide), F32), vm((n_dp, 3, ro, wide), F32), vm((n_dp, n_mp, ro, wide), F32),
        ] + 2 * [
            vm((n_dp, ru, units), BF16), vm((n_dp, rd, wide), BF16), vm((n_dp, 3, ro, wide), BF16), vm((n_dp, n_mp, ro, wide), BF16),
        ] + [
            vm((n_mp, ro, wide), BF16), vm((depth, PACK, wide), F32), vm((n_mp, 8, wide), F32),
            dma((4, depth)), dma((4, depth)), dma((4, depth)), dma((4, depth)), dma((n_mp,)), dma((n_mp,)), dma((depth,)), dma((depth,)),
            dma((n_mp,)), dma((n_mp,)),
        ] if summed else []),
        compiler_params=pltpu.CompilerParams(collective_id=1, has_side_effects=True, vmem_limit_bytes=60 << 20),
        name="rear",
    )(nl, df, dctx, d_wo, over_rows, d_a1, q, k, v, e, inv, w_t, xf, w_up, w_down, b_up, bx, by)


def layer(n_mp, n_dp):
    def on_device(
        hidden_in, text_lens, key_mask, bucket_x, bucket_y, w_qkv, b_q, b_v, w_out, b_out, g_attn, n_attn,
        w_up, b_up, w_down, b_down, g_ffn, n_ffn, t_pos, t_x, t_y, cotangent,
    ):
        rows, wide = hidden_in.shape
        slot = bucket_x.shape[1]
        width = w_qkv.shape[2]
        heads = width // HEAD_DIM
        bx, by = bucket_x[0], bucket_y[0]
        w_t = jnp.transpose(w_qkv, (0, 2, 1))
        xf, q, k, v, e, inv, ctx, b_up_all, wo, wu, wd = front(
            n_mp, n_dp, hidden_in, w_t, b_q, b_v, bx, by, t_x, t_y, t_pos, text_lens, key_mask, b_up, w_out, w_up, w_down
        )
        gathered = (wo.reshape((n_mp,) + w_out.shape), wu.reshape((n_mp,) + w_up.shape), wd.reshape((n_mp,) + w_down.shape))
        layer_out, normed_low, d_ffn, d_a1, d_ctx, d_wo, over_rows = middle(
            n_mp, hidden_in, ctx, (w_out, w_up, w_down), gathered, b_up_all, b_out, g_attn, n_attn, b_down, g_ffn, n_ffn,
            cotangent, text_lens,
        )
        input_grad, pack, g_up, g_down, g_qkv, g_out = rear(
            n_mp, n_dp, normed_low, d_ffn, d_ctx, d_wo, over_rows, d_a1, q, k, v, e, inv, w_t, xf, w_up, w_down, b_up, bx, by
        )

        if sums_in_kernel(n_dp, width, w_up.shape[1], wide):
            g_qkv = jnp.transpose(g_qkv, (1, 0, 2, 3))
        else:
            g_out = lax.psum_scatter(g_out.reshape(-1, wide), "mp", scatter_dimension=0, tiled=True)
            g_up, g_down, g_qkv, g_out, pack = lax.psum((g_up, g_down, g_qkv, g_out, pack), "dp")
            pack = jnp.concatenate([lax.psum(pack[:8], "mp"), pack[8:]], axis=0)
        grad_w_up = g_up.reshape(w_up.shape).astype(F32)
        grad_w_down = g_down.reshape(w_down.shape).astype(F32)
        grad_w_out = g_out.reshape(w_out.shape).astype(F32)
        grad_w_qkv = jnp.transpose(g_qkv.reshape(3, width, wide).astype(F32), (0, 2, 1))
        grad_g_ffn, grad_n_ffn, grad_b_down, grad_g_attn, grad_n_attn, grad_b_out, _, _, grad_b_up = [pack[i] for i in range(9)]
        grad_b_q, grad_b_v = pack[9, :width], pack[10, :width]
        tables = [
            pack[16 : 16 + HI * heads, t * TILE : t * TILE + LO].reshape(HI, heads, LO).transpose(1, 0, 2).reshape(heads, HI * LO)
            for t in range(2)
        ]
        grad_t_pos = jnp.stack([pack[16:, (2 + h) * TILE] for h in range(heads)])
        return (
            layer_out, input_grad, grad_w_qkv, grad_b_q, grad_b_v, grad_w_out, grad_b_out, grad_g_attn, grad_n_attn,
            grad_w_up, grad_b_up, grad_w_down, grad_b_down, grad_g_ffn, grad_n_ffn, grad_t_pos, tables[0], tables[1],
        )

    return on_device


def solution(mesh):
    both, split = P(("dp", "mp"), None), P("mp")
    rows_mp, cols_mp, qkv = P("mp", None), P(None, "mp"), P(None, None, "mp")
    doc = P("dp", None, None)
    return jax.shard_map(
        layer(mesh.shape["mp"], mesh.shape["dp"]),
        mesh=mesh,
        in_specs=(
            both, P("dp"), P("dp"), doc, doc, qkv, split, split, rows_mp, P(), P(), P(), cols_mp, split, rows_mp, P(), P(), P(),
            rows_mp, rows_mp, rows_mp, both,
        ),
        out_specs=(
            both, both, qkv, split, split, rows_mp, P(), P(), P(), cols_mp, split, rows_mp, P(), P(), P(), rows_mp, rows_mp, rows_mp,
        ),
        check_vma=False,
    )
```

time: 351 us -> 214 us (0.61)
  blocking collectives: 76.9 us -> 0 us
  matrix products: 43.9 us -> 0 us
  Pallas kernels: 159 us -> 197 us
  waiting for transfers between devices: 23.6 us -> 0 us
  other arithmetic: 21.6 us -> 6.4 us
  between operations: 14.8 us -> 1.36 us
    pallas_call x1 -> x2, Pallas kernels: 54 us -> 125 us  [the longest x1 112 us: rear(): pl.pallas_call(functools.partial(rear_kernel, n_mp, n_dp, plans, summed),...]
    psum x2 -> x0, blocking collectives: 63.6 us -> none  [the longest x1 39.9 us: on_device(): lax.psum((grad_b_out, grad_g_attn, grad_n_attn, grad_b_down, grad_g_ffn,...]
    dot_general x10 -> x0, matrix products: 43.9 us -> none  [the longest x1 13.1 us: on_device(): jnp.einsum('srf,sdf->rd', d_pre, wu, preferred_element_type=F32)]
    pallas_call x1, Pallas kernels: 105 us -> 72.2 us  [front(): pl.pallas_call(functools.partial(front_kernel, n_mp, n_dp, plans), out_sh...]
    all_gather x1 -> x0, blocking collectives: 13.4 us -> none  [on_device(): b_up_all = lax.all_gather(b_up, 'mp', axis=0)]
    psum x1 -> x0, waiting for transfers between devices: 13 us -> none  [on_device(): lax.psum((gw.astype(BF16), grad_w_out, grad_w_up.astype(BF16), grad_w_dow...]
    reduce_scatter x1 -> x0, waiting for transfers between devices: 10.6 us -> none  [on_device(): lax.psum_scatter(d_wo.reshape(-1, wide), 'mp', scatter_dimension=0, tiled...]
    reduce_sum x6 -> x0, other arithmetic: 7.55 us -> none  [the longest x2 3.56 us: layer_norm(): spread = values - center]
  transfers between devices with their start and end apart: 4 -> 0, of which waited for: 2 -> 0; matrix products, arithmetic and copies ran while one was open for 16% -> 0% of each run, Pallas kernels for 15% -> 0%
where the time goes in v2:
time: 214 us; the launch traced here: 213 us
  Pallas kernels  197 us (92%)
  local copies, waits for them, and re-layouts  8.91 us (4%)
  other arithmetic  6.4 us (3%)
    pallas_call x1, Pallas kernels, rear(): pl.pallas_call(functools.partial(rear_kernel, n_mp, n_dp, plans, summed),...  112 us
    pallas_call x1, Pallas kernels, front(): pl.pallas_call(functools.partial(front_kernel, n_mp, n_dp, plans), out_sh...  72.2 us
    pallas_call x1, Pallas kernels, middle(): pl.pallas_call(functools.partial(mid_kernel, n_mp), out_shape=[sds((rows,...  13.1 us

profile of v2, /device:TPU:0, one launch (start us, length us, event | category | flops | bytes accessed | tf_op | source)
XLA Modules:
  0.0 213.4 jit_solution(13016905373035524799)
XLA Ops:
  1.3 72.2 %front.1 = (bf16[4,192,768]{2,1,0:T(8,128)(2,1)}, bf16[768,192]{1,0:T(8,128)(2,1)}, bf16[768,192]{1,0:T(8,128)(2,1)}, bf16[768,192]{1,0:T(8,128)(2,1)}, bf16[3,7...) custom-call(bf16[192,768]{1,0:T(8,128)(2,1)} %x_ref.3, ...), custom_call_target="tpu_custom_call" | custom-call | tf_op jit(solution)/shard_map/front/pallas_call | solution.py:323
  73.5 13.1 %middle.1 = (bf16[192,768]{1,0:T(8,128)(2,1)}, bf16[192,768]{1,0:T(8,128)(2,1)}, bf16[192,768]{1,0:T(8,128)(2,1)}, f32[192,768]{1,0:T(8,128)}, bf16[4,192,192]{2...) custom-call(bf16[192,768]{1,0:T(8,128)(2,1)} %x_ref.3, ...), custom_call_target="tpu_custom_call" | custom-call | tf_op jit(solution)/shard_map/middle/pallas_call | solution.py:430
  86.5 111.5 %rear.1 = (bf16[192,768]{1,0:T(8,128)(2,1)}, f32[48,768]{1,0:T(8,128)}, bf16[8,96,768]{2,1,0:T(8,128)(2,1)}, bf16[8,96,768]{2,1,0:T(8,128)(2,1)}, bf16[8,3,24,76...) custom-call(bf16[192,768]{1,0:T(8,128)(2,1)} %get-tuple-element.48.nl_ref, bf16[192,768]{1,0:T(8,128)(2,1)} %get-tuple-element.49.df_ref, ...), custom_call_target="tpu_custom_call" | custom-call | tf_op jit(solution)/shard_map/rear/pallas_call | solution.py:861
  198.1 0.9 slice_reduce_fusion.2
  199.0 0.6 pad_maximum_fusion
  199.6 1.3 fusion.1
  200.9 0.7 fusion
  201.6 1.6 slice_reduce_fusion.3
  203.3 0.7 reshape.87
  203.9 0.7 reshape.85
  204.6 1.8 bitcast_convert_fusion.2
  206.4 1.3 convert_bitcast_fusion
  207.7 0.0 copy-start
  207.7 0.0 copy-start.1
  207.7 1.4 copy.43
  209.1 0.3 copy-done
  209.4 0.6 copy-done.1
  210.0 0.0 copy-start.2
  210.0 2.7 %bitcast_convert_fusion = (f32[768,768]{1,0:T(8,128)}, f32[768,768]{1,0:T(8,128)}) fusion(bf16[8,96,768]{2,1,0:T(8,128)(2,1)S(1)} %copy-done.1, bf16[8,96,768]{2,1,0:T(8,128)(2,1)S(1)} %copy-done), kind=kLoop, calls=%fused_computation.1 | loop fusion | flops 1179648 | bytes 7077888 | tf_op jit(solution)/shard_map/convert_element_type | solution.py:917
  212.7 0.0 copy-done.2
  212.7 0.7 copy.48
  (4 shorter events, 0.0 us)
Async XLA Ops:
  207.7 1.7 copy-start
  207.7 2.3 %copy-start.1 = (bf16[8,96,768]{2,1,0:T(8,128)(2,1)S(1)}, bf16[8,96,768]{2,1,0:T(8,128)(2,1)}, u32[]{:S(2)}) copy-start(bf16[8,96,768]{2,1,0:T(8,128)(2,1)} %get-tuple-element.65) | copy-start | bytes 3538948
  210.0 2.7 %copy-start.2 = (bf16[192,768]{1,0:T(8,128)(2,1)S(1)}, bf16[192,768]{1,0:T(8,128)(2,1)}, u32[]{:S(2)}) copy-start(bf16[192,768]{1,0:T(8,128)(2,1)} %get-tuple-element.101) | copy-start | bytes 884740

commit v3 on v2

--- a/solution.py
+++ b/solution.py
@@ -340,109 +340,6 @@
     )(x, w_qkv, b_q, b_v, bx, by, t_x, t_y, t_pos, text_lens, key_mask, b_up, *slices)
 
 EPS = 1e-05
-
-
-def mid_kernel(
-    n_mp,
-    x_ref, ctx_ref, wo_own, wu_own, wd_own, wo_hbm, wu_hbm, wd_hbm, bu_ref, bo_ref, ga_ref, na_ref, bd_ref, gf_ref, nf_ref,
-    cot_ref, len_ref,
-    lo_ref, nl_ref, df_ref, da_ref, dc_ref, go_ref, gs_ref,
-    wo_ref, wu_ref, wd_ref, gp_ref, sem,
-):
-    z = lax.axis_index("mp")
-    rows, wide = x_ref.shape
-    others = [(z + k) % n_mp for k in range(1, n_mp)]
-    loads = []
-    for w, (own, rest, held) in enumerate(((wo_own, wo_hbm, wo_ref), (wu_own, wu_hbm, wu_ref), (wd_own, wd_hbm, wd_ref))):
-        copies = [pltpu.make_async_copy(own, held.at[z], sem.at[w, z])]
-        copies += [pltpu.make_async_copy(rest.at[s], held.at[s], sem.at[w, s]) for s in others]
-        for copy in copies:
-            copy.start()
-        loads.append(copies)
-
-    def vec(ref):
-        return ref[...].astype(F32).reshape(1, wide)
-
-    def norm(values):
-        spread = values - jnp.mean(values, axis=1, keepdims=True)
-        rate = lax.rsqrt(jnp.mean(spread * spread, axis=1, keepdims=True) + EPS)
-        return spread * rate, rate
-
-    def norm_back(up, gain, hat, rate):
-        scaled = up * gain
-        first = jnp.mean(scaled, axis=1, keepdims=True)
-        second = jnp.mean(scaled * hat, axis=1, keepdims=True)
-        return rate * (scaled - first - hat * second)
-
-    def total(values):
-        return jnp.sum(values, axis=0, keepdims=True)
-
-    for copy in loads[0]:
-        copy.wait()
-    attn = dot(ctx_ref[0], wo_ref[0], 1, 0)
-    for s in range(1, n_mp):
-        attn = attn + dot(ctx_ref[s], wo_ref[s], 1, 0)
-    hat_one, rate_one = norm(x_ref[...].astype(F32) + attn + vec(bo_ref))
-    normed = hat_one * vec(ga_ref) + vec(na_ref)
-    low = normed.astype(BF16)
-    nl_ref[...] = low
-
-    for copies in loads[1:]:
-        for copy in copies:
-            copy.wait()
-    ffn = jnp.zeros((rows, wide), F32)
-    for s in range(n_mp):
-        pre = dot(low, wu_ref[s], 1, 0) + bu_ref[s, 0:1, :]
-        cdf = 0.5 * (1.0 + lax.erf(pre * (0.5**0.5)))
-        gp_ref[s] = cdf + pre * (jnp.exp(-0.5 * pre * pre) * 0.3989422804014327)
-        ffn = ffn + dot((pre * cdf).astype(BF16), wd_ref[s], 1, 0)
-    hat_two, rate_two = norm(normed + ffn + vec(bd_ref))
-    lo_ref[...] = (hat_two * vec(gf_ref) + vec(nf_ref)).astype(BF16)
-
-    place = z * rows + lax.broadcasted_iota(jnp.int32, (rows, 1), 0)
-    grad_y = jnp.where(place < 1 + PATCHES + len_ref[0], cot_ref[...].astype(F32), 0.0)
-    d_two = norm_back(grad_y, vec(gf_ref), hat_two, rate_two)
-    d_ffn = d_two.astype(BF16)
-    df_ref[...] = d_ffn
-    d_normed = d_two
-    for s in range(n_mp):
-        d_pre = (dot(d_ffn, wd_ref[s], 1, 1) * gp_ref[s]).astype(BF16)
-        d_normed = d_normed + dot(d_pre, wu_ref[s], 1, 1)
-    d_one = norm_back(d_normed, vec(ga_ref), hat_one, rate_one)
-    da_ref[...] = d_one
-    d_attn = d_one.astype(BF16)
-    for s in range(n_mp):
-        dc_ref[s] = dot(d_attn, wo_ref[s], 1, 1).astype(BF16)
-        go_ref[s] = dot(ctx_ref[s].astype(F32).T.astype(BF16), d_attn, 1, 0).astype(BF16)
-    gs_ref[...] = jnp.concatenate(
-        [
-            total(grad_y * hat_two), total(grad_y), total(d_two), total(d_normed * hat_one), total(d_normed), total(d_one),
-            jnp.zeros((2, wide), F32),
-        ],
-        axis=0,
-    )
-
-
-def middle(n_mp, x, ctx, owns, gathered, b_up_all, b_out, g_attn, n_attn, b_down, g_ffn, n_ffn, cotangent, text_lens):
-    rows, wide = x.shape
-    sds = jax.ShapeDtypeStruct
-    width, units = owns[0].shape[0], owns[1].shape[1]
-    return pl.pallas_call(
-        functools.partial(mid_kernel, n_mp),
-        out_shape=[
-            sds((rows, wide), BF16), sds((rows, wide), BF16), sds((rows, wide), BF16), sds((rows, wide), F32),
-            sds((n_mp, rows, width), BF16), sds((n_mp, width, wide), BF16), sds((8, wide), F32),
-        ],
-        in_specs=[VMEM] * 2 + [ANY] * 6 + [VMEM] * 8 + [pl.BlockSpec(memory_space=pltpu.SMEM)],
-        out_specs=[VMEM] * 7,
-        scratch_shapes=[
-            pltpu.VMEM((n_mp, width, wide), BF16), pltpu.VMEM((n_mp, wide, units), BF16), pltpu.VMEM((n_mp, units, wide), BF16),
-            pltpu.VMEM((n_mp, rows, units), F32), pltpu.SemaphoreType.DMA((3, n_mp)),
-        ],
-        compiler_params=pltpu.CompilerParams(vmem_limit_bytes=BIG),
-        name="middle",
-    )(x, ctx, *owns, *gathered, b_up_all, b_out, g_attn, n_attn, b_down, g_ffn, n_ffn, cotangent, text_lens)
-
 HI, LO, GROUP, STEP = 4, 16, 16, 2
 PACK = 48
 
@@ -451,13 +348,19 @@
     return all(size % (8 * n_dp) == 0 for size in sizes)
 
 
+def gelu_parts(pre):
+    cdf = 0.5 * (1.0 + lax.erf(pre * (0.5**0.5)))
+    return (pre * cdf).astype(BF16), cdf + pre * (jnp.exp(-0.5 * pre * pre) * 0.3989422804014327)
+
+
 def rear_kernel(
     n_mp, n_dp, plans, summed,
-    nl_ref, df_ref, dc_in, go_ref, gs_ref, da_ref, q_ref, k_ref, v_ref, e_ref, inv_ref, w_ref, xf_ref, wu_ref, wd_ref, bu_ref,
-    bx_hbm, by_hbm,
-    ig_ref, pack_ref, uo_ref, do_ref, qo_ref, oo_ref,
-    dc_ref, ds_ref, dt_ref, dn_ref, acc_ref, near_ref, part_ref, got_ref, bx_ref, by_ref, nf_ref, dff_ref, act_ref, gp_ref,
-    sp_ref, b_sem, d_send, d_recv, r_send, r_recv, h_send, h_recv,
+    x_ref, ctx_ref, bu_ref, ball_ref, bo_ref, ga_ref, na_ref, bd_ref, gf_ref, nf_gain_ref, cot_ref, len_ref,
+    q_ref, k_ref, v_ref, e_ref, inv_ref, w_ref, xf_ref, wu_own, wd_own, wo_own, wo_hbm, wu_hbm, wd_hbm, bx_hbm, by_hbm,
+    lo_ref, ig_ref, pack_ref, uo_ref, do_ref, qo_ref, oo_ref,
+    wo_ref, wu_ref, wd_ref, gp_ref, wdo_ref, da_ref, gs_ref, dc_in, dc_ref, dt_ref, dn_ref, acc_ref, near_ref, part_ref, got_ref, bx_ref, by_ref,
+    nf_ref, dff_ref, sp_ref,
+    w_sem, b_sem, d_send, d_recv, r_send, r_recv, h_send, h_recv,
     *for_sums,
 ):
     if summed:
@@ -475,26 +378,26 @@
     others = [(z + k) % n_mp for k in range(1, n_mp)]
     depth = len(plans[0])
 
+    weights = []
+    for w, (own, rest, held) in enumerate(((wo_own, wo_hbm, wo_ref), (wu_own, wu_hbm, wu_ref), (wd_own, wd_hbm, wd_ref))):
+        copies = [pltpu.make_async_copy(own, held.at[z], w_sem.at[w, z])]
+        copies += [pltpu.make_async_copy(rest.at[s], held.at[s], w_sem.at[w, s]) for s in others]
+        for copy in copies:
+            copy.start()
+        weights.append(copies)
+    again = pltpu.make_async_copy(wd_own, wdo_ref, b_sem.at[2])
+    again.start()
     loads = [pltpu.make_async_copy(bx_hbm, bx_ref, b_sem.at[0]), pltpu.make_async_copy(by_hbm, by_ref, b_sem.at[1])]
     for copy in loads:
         copy.start()
+    loads.append(again)
     barrier = pltpu.get_barrier_semaphore()
     peers = [(d, to) for to in others] + [(flip(d, bit), z) for bit in plans[0] if summed]
     for peer in peers:
         pl.semaphore_signal(barrier, inc=1, device_id=peer, device_id_type=MESH)
-    nf_ref[z] = nl_ref[...]
-    dff_ref[z] = df_ref[...]
-    dc_ref[z] = dc_in[z]
-    pl.semaphore_wait(barrier, len(peers))
 
     def remote(src, dst, send, recv, to):
         return pltpu.make_async_remote_copy(src, dst, send, recv, device_id=to, device_id_type=MESH)
-
-    def d_copy(to, source):
-        return remote(dc_in.at[to], dc_ref.at[source], d_send.at[to], d_recv.at[source], (d, to))
-
-    for to in others:
-        d_copy(to, z).start()
 
     lines = (nf_ref, dff_ref)
 
@@ -525,7 +428,7 @@
 
         on_step(step, act)
 
-    for a in range(2):
+    def set_off(a):
         ends(lambda ahead, sem: hop(a, z, ahead, sem).start())
 
     items = ((None, None, None, plans[0]),) if not summed else (
@@ -546,32 +449,140 @@
         return remote(staged.at[away], got.at[pl.ds(size, size)], rs_send.at[i, place], rs_recv.at[i, place], (flip(d, plan[place]), z))
 
     def rs_start(i, place):
-        if not summed:
-            return
         _, away, _ = halves(i, place)
         items[i][1][away] = items[i][0][away].astype(BF16)
         rs_copy(i, place).start()
-
-    def rs_finish(i, place):
-        if not summed:
-            return
-        kept, _, size = halves(i, place)
-        rs_copy(i, place).wait_recv()
-        total, _, got, _ = items[i]
-        total[kept] = total[kept] + got[size : 2 * size].astype(F32)
 
     def ag_copy(i, place, incoming=False):
         kept, away, _ = halves(i, place)
         part = outs[i].at[away if incoming else kept]
         return remote(part, part, ag_send.at[i, place], ag_recv.at[i, place], (flip(d, items[i][3][place]), z))
 
-    if summed:
-        for s in range(n_mp):
-            oa_ref[:, s] = go_ref[s].astype(F32).reshape(n_dp, -1, wide)
-    else:
-        oo_ref[...] = go_ref[...]
-    rs_start(3, depth - 1)
-
+    def oz_copy(to, source):
+        return remote(os_ref.at[labels[3], to], oz_ref.at[source], oz_send.at[to], oz_recv.at[source], (d, to))
+
+    stage = {}
+
+    def begin(i):
+        if summed:
+            rs_start(i, depth - 1)
+            stage[i] = ("halve", depth - 1)
+
+    def onward(i):
+        if not summed or stage[i] is None:
+            return
+        kind, place = stage[i]
+        if kind == "halve":
+            kept, _, size = halves(i, place)
+            rs_copy(i, place).wait_recv()
+            total, _, got, _ = items[i]
+            total[kept] = total[kept] + got[size : 2 * size].astype(F32)
+            if place:
+                rs_start(i, place - 1)
+                stage[i] = ("halve", place - 1)
+            elif i == 3:
+                os_ref[labels[3]] = oa_ref[labels[3]].astype(BF16)
+                for to in others:
+                    oz_copy(to, z).start()
+                stage[i] = ("line", 0)
+            else:
+                outs[i][labels[i]] = total[labels[i]].astype(BF16)
+                ag_copy(i, 0).start()
+                stage[i] = ("gather", 0)
+        elif kind == "line":
+            out = oa_ref[labels[3], z]
+            for source in others:
+                oz_copy(z, source).wait_recv()
+                out = out + oz_ref[source].astype(F32)
+            oo_ref[labels[3]] = out.astype(BF16)
+            ag_copy(3, 0).start()
+            stage[i] = ("gather", 0)
+        else:
+            ag_copy(i, place, True).wait_recv()
+            if place < depth - 1:
+                ag_copy(i, place + 1).start()
+                stage[i] = ("gather", place + 1)
+            else:
+                stage[i] = None
+
+    def vec(ref):
+        return ref[...].astype(F32).reshape(1, wide)
+
+    def norm(values):
+        spread = values - jnp.mean(values, axis=1, keepdims=True)
+        rate = lax.rsqrt(jnp.mean(spread * spread, axis=1, keepdims=True) + EPS)
+        return spread * rate, rate
+
+    def norm_back(up, gain, hat, rate):
+        scaled = up * gain
+        first = jnp.mean(scaled, axis=1, keepdims=True)
+        second = jnp.mean(scaled * hat, axis=1, keepdims=True)
+        return rate * (scaled - first - hat * second)
+
+    def total_rows(values):
+        return jnp.sum(values, axis=0, keepdims=True)
+
+    for copy in weights[0]:
+        copy.wait()
+    attn = dot(ctx_ref[0], wo_ref[0], 1, 0)
+    for s in range(1, n_mp):
+        attn = attn + dot(ctx_ref[s], wo_ref[s], 1, 0)
+    hat_one, rate_one = norm(x_ref[...].astype(F32) + attn + vec(bo_ref))
+    normed = hat_one * vec(ga_ref) + vec(na_ref)
+    low = normed.astype(BF16)
+    nf_ref[z] = low
+    pl.semaphore_wait(barrier, len(peers))
+    set_off(0)
+
+    for copies in weights[1:]:
+        for copy in copies:
+            copy.wait()
+    ffn = jnp.zeros((rows, wide), F32)
+    for s in range(n_mp):
+        act, slope = gelu_parts(dot(low, wu_ref[s], 1, 0) + ball_ref[s, 0:1, :])
+        gp_ref[s] = slope
+        ffn = ffn + dot(act, wd_ref[s], 1, 0)
+    hat_two, rate_two = norm(normed + ffn + vec(bd_ref))
+    lo_ref[...] = (hat_two * vec(gf_ref) + vec(nf_gain_ref)).astype(BF16)
+
+    place_row = z * rows + lax.broadcasted_iota(jnp.int32, (rows, 1), 0)
+    grad_y = jnp.where(place_row < 1 + PATCHES + len_ref[0], cot_ref[...].astype(F32), 0.0)
+    d_two = norm_back(grad_y, vec(gf_ref), hat_two, rate_two)
+    d_ffn = d_two.astype(BF16)
+    dff_ref[z] = d_ffn
+    set_off(1)
+    arrived(0, 1)
+    d_normed = d_two
+    for s in range(n_mp):
+        d_pre = (dot(d_ffn, wd_ref[s], 1, 1) * gp_ref[s]).astype(BF16)
+        d_normed = d_normed + dot(d_pre, wu_ref[s], 1, 1)
+    d_one = norm_back(d_normed, vec(ga_ref), hat_one, rate_one)
+    da_ref[...] = d_one
+    d_attn = d_one.astype(BF16)
+
+    def d_copy(to, source):
+        return remote(dc_in.at[to], dc_ref.at[source], d_send.at[to], d_recv.at[source], (d, to))
+
+    for s in range(n_mp):
+        dc_in[s] = dot(d_attn, wo_ref[s], 1, 1).astype(BF16)
+    for to in others:
+        d_copy(to, z).start()
+    dc_ref[z] = dc_in[z]
+
+    for s in range(n_mp):
+        go = dot(ctx_ref[s].astype(F32).T.astype(BF16), d_attn, 1, 0)
+        if summed:
+            oa_ref[:, s] = go.reshape(n_dp, -1, wide)
+        else:
+            oo_ref[s] = go.astype(BF16)
+    begin(3)
+    gs_ref[...] = jnp.concatenate(
+        [
+            total_rows(grad_y * hat_two), total_rows(grad_y), total_rows(d_two), total_rows(d_normed * hat_one),
+            total_rows(d_normed), total_rows(d_one), jnp.zeros((2, wide), F32),
+        ],
+        axis=0,
+    )
     sp_ref[0:8, :] = gs_ref[...]
 
     def sz_copy(to, source):
@@ -588,11 +599,13 @@
     for h in range(heads):
         factor = jnp.where(mine[h], inv_ref[:, h : h + 1], factor)
     qt = q_ref[...].astype(F32).T.astype(BF16)
+    arrived(0, 2)
+    arrived(1, 1)
+    onward(3)
     for source in others:
         d_copy(source, source).wait_recv()
-    for a in range(2):
-        arrived(a, 1)
-
+
+    ds_ref = wd_ref
     dctx = dc_ref[...].reshape(slot, width)
     gt = (dctx.astype(F32) * factor).T.astype(BF16)
     block = 384
@@ -615,44 +628,21 @@
             dv = c if dv is None else dv + c
         dt_ref[1, hs, :] = dk.astype(BF16)
         dt_ref[2, hs, :] = dv.astype(BF16)
+        if h == 0:
+            arrived(1, 2)
+        elif h == 1:
+            arrived(0, 3)
+    onward(3)
     for r in range(slot // block):
         rs = slice(r * block, (r + 1) * block)
-        low = (dq[r] * scale).astype(BF16)
-        dn_ref[0, rs, :] = low
-        dt_ref[0, :, rs] = low.astype(F32).T.astype(BF16)
+        low_q = (dq[r] * scale).astype(BF16)
+        dn_ref[0, rs, :] = low_q
+        dt_ref[0, :, rs] = low_q.astype(F32).T.astype(BF16)
     for c in (1, 2):
         dn_ref[c] = dt_ref[c].astype(F32).T.astype(BF16)
 
-    for a in range(2):
-        arrived(a, 2)
-    rs_finish(3, depth - 1)
-    rs_start(3, depth - 2)
-
-    def r_copy(turn, to, source):
-        return remote(part_ref.at[turn], got_ref.at[source], r_send.at[turn], r_recv.at[source], (d, to))
-
-    def dx_part(to):
-        at = pl.ds(pl.multiple_of(to * rows, rows), rows)
-        out = dot(dn_ref[0, at, :], w_ref[0], 1, 0)
-        for c in (1, 2):
-            out = out + dot(dn_ref[c, at, :], w_ref[c], 1, 0)
-        return out
-
-    for turn in range(n_mp - 1):
-        part_ref[turn] = dx_part(others[turn]).astype(BF16)
-        r_copy(turn, others[turn], z).start()
-    dx = da_ref[...] + dx_part(z)
-
     ones = jnp.ones((8, slot), BF16)
     xf = xf_ref[...].reshape(slot, wide)
-    def keep(i, values, part=0, parts=1):
-        if summed:
-            total = items[i][0]
-            count_ = total.shape[0] // parts
-            total[part * count_ : (part + 1) * count_] = values.reshape(count_, -1, values.shape[1])
-        else:
-            outs[i][part] = values.astype(BF16)
-
     for c in range(3):
         gw = dot(dt_ref[c], xf, 1, 0)
         if summed:
@@ -661,15 +651,58 @@
             qo_ref[c] = gw.astype(BF16)
     sp_ref[9:10, 0:width] = dot(ones, dn_ref[0], 1, 0)[0:1]
     sp_ref[10:11, 0:width] = dot(ones, dn_ref[2], 1, 0)[0:1]
-    rs_start(2, depth - 1)
+    begin(2)
+    onward(3)
+
+    b_up = bu_ref[...].astype(F32).reshape(1, -1)
+    last = heads
+    for b in range(n_mp):
+        act, slope = gelu_parts(dot(nf_ref[b], wu_ref[z], 1, 0) + b_up)
+        wd_ref[last, b * rows : (b + 1) * rows, :] = act
+        gp_ref[b] = slope
+    onward(2)
+    onward(3)
+    arrived(1, 3)
+
+    def keep(i, values):
+        if summed:
+            items[i][0][...] = values.reshape(n_dp, -1, values.shape[1])
+        else:
+            outs[i][0] = values.astype(BF16)
 
     for copy in loads:
         copy.wait()
+    dff = dff_ref[...].reshape(slot, wide)
+    act_ref = wd_ref.at[last]
+    keep(1, dot(act_ref[...], dff, 0, 0))
+    begin(1)
+    act_ref[...] = (dot(dff, wdo_ref[...], 1, 1) * gp_ref[...].reshape(slot, -1)).astype(BF16)
+    keep(0, dot(nf_ref[...].reshape(slot, wide), act_ref[...], 0, 0))
+    begin(0)
+    sp_ref[8:9, :] = dot(ones, act_ref[...], 1, 0)[0:1]
+
+    def r_copy(turn, to, source):
+        return remote(part_ref.at[turn], got_ref.at[turn], r_send.at[turn], r_recv.at[turn], (d, to))
+
+    def dx_part(to):
+        at = pl.ds(pl.multiple_of(to * rows, rows), rows)
+        out = dot(dn_ref[0, at, :], w_ref[0], 1, 0)
+        for c in (1, 2):
+            out = out + dot(dn_ref[c, at, :], w_ref[c], 1, 0)
+        return out
+
+    for turn in range(n_mp - 1):
+        part_ref[turn] = dx_part(others[turn]).astype(BF16)
+        r_copy(turn, others[turn], z).start()
+    da_ref[...] = da_ref[...] + dx_part(z)
+    for i in (1, 0, 2, 3):
+        onward(i)
+
     acc_ref[...] = jnp.zeros_like(acc_ref)
     one = jnp.ones((), BF16)
 
-    def count(first, last):
-        @pl.loop(first, last)
+    def count(first, last_):
+        @pl.loop(first, last_)
         def _(i):
             at = [pl.ds(pl.multiple_of(i * GROUP * STEP + g * GROUP, GROUP), GROUP) for g in range(STEP)]
             ds = [[ds_ref[h, at[g], :] for h in range(heads)] for g in range(STEP)]
@@ -688,21 +721,11 @@
                     tot = o if tot is None else tot + o
                 acc_ref[t] += tot
 
-    waiting = {2: depth - 1, 3: depth - 2}
-
-    def onward(i):
-        if waiting[i] > 0:
-            rs_finish(i, waiting[i])
-            waiting[i] -= 1
-            rs_start(i, waiting[i])
-
     trips = slot // (GROUP * STEP)
-    for part in range(4):
-        count(part * trips // 4, (part + 1) * trips // 4)
-        onward(2)
-        onward(3)
-    for i in (2, 3):
-        while waiting[i] > 0:
+    parts = 4
+    for part in range(parts):
+        count(part * trips // parts, (part + 1) * trips // parts)
+        for i in (1, 0, 2, 3):
             onward(i)
 
     m, n = HI * heads * GROUP, LO * GROUP
@@ -741,88 +764,38 @@
                     continue
                 tot = piece if tot is None else tot + piece
             found.append(jnp.sum(tot, axis=0, keepdims=True))
-        lines_h = jnp.sum(jnp.concatenate(found, 0), axis=1, keepdims=True) * scale
-        sp_ref[16 : 16 + bins, (2 + h) * TILE : (2 + h) * TILE + 1] = lines_h
-
-    for a in range(2):
-        arrived(a, 3)
-    b_up = bu_ref[...].astype(F32).reshape(1, -1)
-    for b in range(n_mp):
-        at = slice(b * rows, (b + 1) * rows)
-        pre = dot(nf_ref[b], wu_ref[...], 1, 0) + b_up
-        cdf = 0.5 * (1.0 + lax.erf(pre * (0.5**0.5)))
-        act_ref[at, :] = (pre * cdf).astype(BF16)
-        gp_ref[at, :] = cdf + pre * (jnp.exp(-0.5 * pre * pre) * 0.3989422804014327)
-    dff = dff_ref[...].reshape(slot, wide)
-    keep(1, dot(act_ref[...], dff, 0, 0))
-    rs_start(1, depth - 1)
-    act_ref[...] = (dot(dff, wd_ref[...], 1, 1) * gp_ref[...]).astype(BF16)
-    keep(0, dot(nf_ref[...].reshape(slot, wide), act_ref[...], 0, 0))
-    rs_start(0, depth - 1)
-    sp_ref[8:9, :] = dot(ones, act_ref[...], 1, 0)[0:1]
+        line_sums = jnp.sum(jnp.concatenate(found, 0), axis=1, keepdims=True) * scale
+        sp_ref[16 : 16 + bins, (2 + h) * TILE : (2 + h) * TILE + 1] = line_sums
 
     def sp_copy(place):
         return remote(sp_ref, sr_ref.at[place], sp_send.at[place], sp_recv.at[place], (flip(d, plans[0][place]), z))
 
-    def oz_copy(to, source):
-        return remote(os_ref.at[labels[3], to], oz_ref.at[source], oz_send.at[to], oz_recv.at[source], (d, to))
-
-    def finish_sums():
+    if summed:
         for source in others:
             sz_copy(z, source).wait_recv()
             sp_ref[0:8, :] = sp_ref[0:8, :] + sz_ref[source]
-
-        sp_copy(depth - 1).start()
-        rs_finish(2, 0)
-        rs_finish(3, 0)
-        qo_ref[labels[2]] = qa_ref[labels[2]].astype(BF16)
-        ag_copy(2, 0).start()
-        os_ref[labels[3]] = oa_ref[labels[3]].astype(BF16)
-        for to in others:
-            oz_copy(to, z).start()
         for place in range(depth - 1, -1, -1):
-            for i in (1, 0):
-                rs_finish(i, place)
-                if place:
-                    rs_start(i, place - 1)
+            sp_copy(place).start()
+            for i in (1, 0, 2, 3):
+                onward(i)
             sp_copy(place).wait_send()
             sp_copy(place).wait_recv()
             sp_ref[...] = sp_ref[...] + sr_ref[place]
-            if place:
-                sp_copy(place - 1).start()
-            if place == depth - 1:
-                out = oa_ref[labels[3], z]
-                for source in others:
-                    oz_copy(z, source).wait_recv()
-                    out = out + oz_ref[source].astype(F32)
-                oo_ref[labels[3]] = out.astype(BF16)
-                ag_copy(3, 0).start()
-        for i, ref in ((0, uo_ref), (1, do_ref)):
-            ref[labels[i]] = items[i][0][labels[i]].astype(BF16)
-            ag_copy(i, 0).start()
-        pack_ref[...] = sp_ref[...]
-        for place in range(1, depth):
-            for i in (2, 3, 0, 1):
-                ag_copy(i, place - 1, True).wait_recv()
-                ag_copy(i, place).start()
-
-    if summed:
-        finish_sums()
-    else:
-        pack_ref[...] = sp_ref[...]
-
-    for source in others:
-        r_copy(0, z, source).wait_recv()
-        dx = dx + got_ref[source].astype(F32)
-    ig_ref[...] = dx.astype(BF16)
-
+    pack_ref[...] = sp_ref[...]
+
+    for turn in range(n_mp - 1):
+        r_copy(turn, z, z).wait_recv()
+        da_ref[...] = da_ref[...] + got_ref[turn].astype(F32)
+    ig_ref[...] = da_ref[...].astype(BF16)
+
+    while any(stage.values()):
+        for i in (1, 0, 2, 3):
+            onward(i)
     for turn in range(n_mp - 1):
         r_copy(turn, z, z).wait_send()
     for to in others:
         d_copy(to, z).wait_send()
     if summed:
-        for i in range(4):
-            ag_copy(i, depth - 1, True).wait_recv()
         for to in others:
             sz_copy(to, z).wait_send()
             oz_copy(to, z).wait_send()
@@ -842,10 +815,13 @@
             on_step(step, sent)
 
 
-def rear(n_mp, n_dp, nl, df, dctx, d_wo, over_rows, d_a1, q, k, v, e, inv, w_t, xf, w_up, w_down, b_up, bx, by):
+def rear(
+    n_mp, n_dp, x, ctx, b_up, b_up_all, b_out, g_attn, n_attn, b_down, g_ffn, n_ffn, cotangent, text_lens,
+    q, k, v, e, inv, w_t, xf, w_up, w_down, w_out, gathered, bx, by,
+):
     heads, slot, _ = e.shape
     width = k.shape[1]
-    rows, wide = d_a1.shape
+    rows, wide = x.shape
     units = w_up.shape[1]
     plans = [gather_plan(n_dp, False), gather_plan(n_dp, True)]
     depth = len(plans[0])
@@ -858,30 +834,32 @@
     sds = jax.ShapeDtypeStruct
     dma = pltpu.SemaphoreType.DMA
     vm = pltpu.VMEM
+    sums = []
+    if summed:
+        whole = [(n_dp, ru, units), (n_dp, rd, wide), (n_dp, 3, ro, wide), (n_dp, n_mp, ro, wide)]
+        sums = [vm(shape, F32) for shape in whole] + 2 * [vm(shape, BF16) for shape in whole]
+        sums += [vm((n_mp, ro, wide), BF16), vm((depth, PACK, wide), F32), vm((n_mp, 8, wide), F32)]
+        sums += [dma((4, depth))] * 4 + [dma((n_mp,))] * 2 + [dma((depth,))] * 2 + [dma((n_mp,))] * 2
     return pl.pallas_call(
         functools.partial(rear_kernel, n_mp, n_dp, plans, summed),
-        out_shape=[
-            sds((rows, wide), BF16), sds((PACK, wide), F32)] + [sds(shape, BF16) for shape in shapes],
-        in_specs=[VMEM] * 16 + [ANY] * 2,
-        out_specs=[VMEM] * 6,
+        out_shape=[sds((rows, wide), BF16), sds((rows, wide), BF16), sds((PACK, wide), F32)] + [sds(shape, BF16) for shape in shapes],
+        in_specs=[VMEM] * 11 + [pl.BlockSpec(memory_space=pltpu.SMEM)] + [VMEM] * 7 + [ANY] * 8,
+        out_specs=[VMEM] * 7,
         scratch_shapes=[
-            vm((n_mp, rows, width), BF16), vm((heads, slot, slot), BF16), vm((3, width, slot), BF16), vm((3, slot, width), BF16),
+            vm((n_mp, width, wide), BF16), vm((n_mp, wide, units), BF16), vm((n_mp, units, wide), BF16), vm((n_mp, rows, units), F32),
+            vm((units, wide), BF16), vm((rows, wide), F32), vm((8, wide), F32), vm((n_mp, rows, width), BF16), vm((n_mp, rows, width), BF16),
+            vm((3, width, slot), BF16), vm((3, slot, width), BF16),
             vm((2, HI * heads * GROUP, LO * GROUP), F32), vm((heads, 5, TILE, TILE), F32), vm((n_mp - 1, rows, wide), BF16),
-            vm((n_mp, rows, wide), BF16), vm((slot, slot), jnp.int32), vm((slot, slot), jnp.int32),
-            vm((n_mp, rows, wide), BF16), vm((n_mp, rows, wide), BF16), vm((slot, units), BF16), vm((slot, units), F32),
-            vm((PACK, wide), F32), dma((2,)), dma((n_mp,)), dma((n_mp,)), dma((n_mp - 1,)), dma((n_mp,)), dma((2, n_mp + 1)), dma((2, n_mp)),
-        ] + ([
-            vm((n_dp, ru, units), F32), vm((n_dp, rd, wide), F32), vm((n_dp, 3, ro, wide), F32), vm((n_dp, n_mp, ro, wide), F32),
-        ] + 2 * [
-            vm((n_dp, ru, units), BF16), vm((n_dp, rd, wide), BF16), vm((n_dp, 3, ro, wide), BF16), vm((n_dp, n_mp, ro, wide), BF16),
-        ] + [
-            vm((n_mp, ro, wide), BF16), vm((depth, PACK, wide), F32), vm((n_mp, 8, wide), F32),
-            dma((4, depth)), dma((4, depth)), dma((4, depth)), dma((4, depth)), dma((n_mp,)), dma((n_mp,)), dma((depth,)), dma((depth,)),
-            dma((n_mp,)), dma((n_mp,)),
-        ] if summed else []),
-        compiler_params=pltpu.CompilerParams(collective_id=1, has_side_effects=True, vmem_limit_bytes=60 << 20),
+            vm((n_mp - 1, rows, wide), BF16), vm((slot, slot), jnp.int32), vm((slot, slot), jnp.int32),
+            vm((n_mp, rows, wide), BF16), vm((n_mp, rows, wide), BF16), vm((PACK, wide), F32),
+            dma((3, n_mp)), dma((3,)), dma((n_mp,)), dma((n_mp,)), dma((n_mp - 1,)), dma((n_mp - 1,)), dma((2, n_mp + 1)), dma((2, n_mp)),
+        ] + sums,
+        compiler_params=pltpu.CompilerParams(collective_id=1, has_side_effects=True, vmem_limit_bytes=62 << 20),
         name="rear",
-    )(nl, df, dctx, d_wo, over_rows, d_a1, q, k, v, e, inv, w_t, xf, w_up, w_down, b_up, bx, by)
+    )(
+        x, ctx, b_up, b_up_all, b_out, g_attn, n_attn, b_down, g_ffn, n_ffn, cotangent, text_lens,
+        q, k, v, e, inv, w_t, xf, w_up, w_down, w_out, *gathered, bx, by,
+    )
 
 
 def layer(n_mp, n_dp):
@@ -899,12 +877,9 @@
             n_mp, n_dp, hidden_in, w_t, b_q, b_v, bx, by, t_x, t_y, t_pos, text_lens, key_mask, b_up, w_out, w_up, w_down
         )
         gathered = (wo.reshape((n_mp,) + w_out.shape), wu.reshape((n_mp,) + w_up.shape), wd.reshape((n_mp,) + w_down.shape))
-        layer_out, normed_low, d_ffn, d_a1, d_ctx, d_wo, over_rows = middle(
-            n_mp, hidden_in, ctx, (w_out, w_up, w_down), gathered, b_up_all, b_out, g_attn, n_attn, b_down, g_ffn, n_ffn,
-            cotangent, text_lens,
-        )
-        input_grad, pack, g_up, g_down, g_qkv, g_out = rear(
-            n_mp, n_dp, normed_low, d_ffn, d_ctx, d_wo, over_rows, d_a1, q, k, v, e, inv, w_t, xf, w_up, w_down, b_up, bx, by
+        layer_out, input_grad, pack, g_up, g_down, g_qkv, g_out = rear(
+            n_mp, n_dp, hidden_in, ctx, b_up, b_up_all, b_out, g_attn, n_attn, b_down, g_ffn, n_ffn, cotangent, text_lens,
+            q, k, v, e, inv, w_t, xf, w_up, w_down, w_out, gathered, bx, by,
         )
 
         if sums_in_kernel(n_dp, width, w_up.shape[1], wide):

time: 214 us -> 201 us (0.939)
  Pallas kernels: 197 us -> 183 us
    pallas_call x1 -> x0, Pallas kernels: 13.1 us -> none  [middle(): pl.pallas_call(functools.partial(mid_kernel, n_mp), out_shape=[sds((rows,...]
where the time goes in v3:
time: 201 us; the launch traced here: 200 us
  Pallas kernels  183 us (91%)
  local copies, waits for them, and re-layouts  9.63 us (5%)
  other arithmetic  6.4 us (3%)
    pallas_call x1, Pallas kernels, rear(): pl.pallas_call(functools.partial(rear_kernel, n_mp, n_dp, plans, summed),...  111 us
    pallas_call x1, Pallas kernels, front(): pl.pallas_call(functools.partial(front_kernel, n_mp, n_dp, plans), out_sh...  72.1 us

profile of v3, /device:TPU:0, one launch (start us, length us, event | category | flops | bytes accessed | tf_op | source)
XLA Modules:
  0.0 200.2 jit_solution(18387798731108988185)
XLA Ops:
  1.3 72.1 %front.1 = (bf16[4,192,768]{2,1,0:T(8,128)(2,1)}, bf16[768,192]{1,0:T(8,128)(2,1)}, bf16[768,192]{1,0:T(8,128)(2,1)}, bf16[768,192]{1,0:T(8,128)(2,1)}, bf16[3,7...) custom-call(bf16[192,768]{1,0:T(8,128)(2,1)} %x_ref.3, ...), custom_call_target="tpu_custom_call" | custom-call | tf_op jit(solution)/shard_map/front/pallas_call | solution.py:323
  73.4 110.8 %rear.1 = (bf16[192,768]{1,0:T(8,128)(2,1)}, bf16[192,768]{1,0:T(8,128)(2,1)}, f32[48,768]{1,0:T(8,128)}, bf16[8,96,768]{2,1,0:T(8,128)(2,1)}, bf16[8,96,768]{2,...) custom-call(bf16[192,768]{1,0:T(8,128)(2,1)} %x_ref.3, ...), custom_call_target="tpu_custom_call" | custom-call | tf_op jit(solution)/shard_map/rear/pallas_call | solution.py:843
  184.2 0.9 slice_reduce_fusion.2
  185.1 0.6 pad_maximum_fusion
  185.7 1.3 fusion.1
  187.0 0.7 fusion
  187.7 1.6 slice_reduce_fusion.3
  189.4 0.7 reshape.87
  190.1 0.7 reshape.85
  190.7 1.8 bitcast_convert_fusion.2
  192.5 1.3 convert_bitcast_fusion
  193.8 0.0 copy-start
  193.8 0.0 copy-start.1
  193.9 1.4 copy.43
  195.2 0.3 copy-done
  195.5 0.6 copy-done.1
  196.1 0.0 copy-start.3
  196.1 0.0 copy-start.2
  196.1 2.7 %bitcast_convert_fusion = (f32[768,768]{1,0:T(8,128)}, f32[768,768]{1,0:T(8,128)}) fusion(bf16[8,96,768]{2,1,0:T(8,128)(2,1)S(1)} %copy-done.1, bf16[8,96,768]{2,1,0:T(8,128)(2,1)S(1)} %copy-done), kind=kLoop, calls=%fused_computation.1 | loop fusion | flops 1179648 | bytes 7077888 | tf_op jit(solution)/shard_map/convert_element_type | solution.py:892
  198.8 0.0 copy-done.3
  198.8 0.7 copy.49
  199.5 0.0 copy-done.2
  199.5 0.7 copy.50
  (4 shorter events, 0.0 us)
Async XLA Ops:
  193.8 1.7 copy-start
  193.8 2.3 %copy-start.1 = (bf16[8,96,768]{2,1,0:T(8,128)(2,1)S(1)}, bf16[8,96,768]{2,1,0:T(8,128)(2,1)}, u32[]{:S(2)}) copy-start(bf16[8,96,768]{2,1,0:T(8,128)(2,1)} %get-tuple-element.53) | copy-start | bytes 3538948
  196.1 2.7 %copy-start.3 = (bf16[192,768]{1,0:T(8,128)(2,1)S(1)}, bf16[192,768]{1,0:T(8,128)(2,1)}, u32[]{:S(2)}) copy-start(bf16[192,768]{1,0:T(8,128)(2,1)} %get-tuple-element.88) | copy-start | bytes 884740
  196.1 3.4 %copy-start.2 = (bf16[192,768]{1,0:T(8,128)(2,1)S(1)}, bf16[192,768]{1,0:T(8,128)(2,1)}, u32[]{:S(2)}) copy-start(bf16[192,768]{1,0:T(8,128)(2,1)} %get-tuple-element.89) | copy-start | bytes 884740

commit v4 on v1

v4 whole, which is shorter than its diff:
```python
import functools
import jax
import jax.numpy as jnp
from jax import lax
from jax.experimental import pallas as pl
from jax.experimental.pallas import tpu as pltpu
from jax.sharding import PartitionSpec as P

HEAD_DIM = 64
PATCHES = 196
THRESHOLDS = (12, 16, 23, 32, 46, 64, 91)
TILE = 128
F32, BF16 = jnp.float32, jnp.bfloat16
MESH = pl.DeviceIdType.MESH
VMEM = pl.BlockSpec(memory_space=pltpu.VMEM)
ANY = pl.BlockSpec(memory_space=pl.ANY)
BIG = 58 << 20


def line_bucket(off):
    mag = jnp.abs(off)
    far = jnp.full(off.shape, 8, jnp.int32)
    for border in THRESHOLDS:
        far = far + (mag >= border).astype(jnp.int32)
    return jnp.where(off > 0, 16, 0) + jnp.where(mag < 8, mag, far)


def dot(a, b, ca, cb):
    return lax.dot_general(a, b, (((ca,), (cb,)), ((), ())), preferred_element_type=F32)


def flip(index, bit):
    step = 2**bit
    return index + step * (1 - 2 * ((index // step) % 2))


SLICES = 8
EPS = 1e-05
HI, LO, GROUP, STEP = 4, 16, 16, 2


def plane_bits(dp_size):
    chips = list(range(1, dp_size.bit_length() - 1))
    used = SLICES.bit_length() - 2
    return chips[:used], chips[used:]


def plan_label(index, plan):
    label = 0
    for place, bit in enumerate(plan):
        label = label + ((index // 2**bit) % 2) * 2**place
    return label


def gelu_parts(pre):
    cdf = 0.5 * (1.0 + lax.erf(pre * (0.5**0.5)))
    return (pre * cdf).astype(BF16), cdf + pre * (jnp.exp(-0.5 * pre * pre) * 0.3989422804014327)


def layer_kernel(
    n_mp, plans, extra,
    x_ref, w_ref, bq_ref, bv_ref, tx_ref, ty_ref, tp_ref, km_ref, bu_ref, bo_ref, ga_ref, na_ref, bd_ref, gf_ref, nn_ref, cot_ref,
    len_ref, bx_hbm, by_hbm, wo_src, wu_src, wd_src,
    lo_ref, ig_ref, pack_ref, tab_out, uo_ref, do_ref, qo_ref, oo_ref,
    xf_ref, q_ref, k_ref, v_ref, e_ref, inv_ref, cr_ref, ball_ref, bx_ref, by_ref, bias_ref, line_ref, wo_ref, wu_ref, wd_ref,
    da_ref, ffn_ref, gs_ref, di_ref, dc_ref, qt_ref, gt_ref, dq_ref, dt_ref, dn_ref, acc_ref, got_ref, nf_ref, dff_ref,
    sp_ref, st_ref, sr_ref, sv_ref, sz_ref, qa_ref, oa_ref, qs_ref, ur_ref, dr_ref, qr_ref, or_ref, oy_ref, oz_ref, ux_ref, dx_ref, qx_ref, ox_ref,
    own_sem, b_sem, x_send, x_recv, c_send, c_recv, u_send, u_recv, z_send, z_recv, p_send, p_recv,
    d_send, d_recv, r_send, r_recv, h_send, h_recv, rs_send, rs_recv, ag_send, ag_recv, ex_send, ex_recv, oz_send, oz_recv,
    sp_send, sp_recv, sz_send, sz_recv,
):
    d = lax.axis_index("dp")
    z = lax.axis_index("mp")
    rows, wide = x_ref.shape
    slot = bx_ref.shape[0]
    width = w_ref.shape[1]
    heads = width // HEAD_DIM
    tiles = slot // TILE
    units = wu_ref.shape[3]
    scale = HEAD_DIM**-0.5
    sources = (wo_src, wu_src, wd_src)
    gathered = (wo_ref, wu_ref, wd_ref)
    others = [(z + k) % n_mp for k in range(1, n_mp)]
    depth = len(plans[0])
    labels = [plan_label(d, plan) for plan in plans]
    w_plan = (0, 0, 1)

    def remote(src, dst, send, recv, to):
        return pltpu.make_async_remote_copy(src, dst, send, recv, device_id=to, device_id_type=MESH)

    loads = []
    for c in range(tiles):
        part = pl.ds(c * TILE, TILE)
        pair = (
            pltpu.make_async_copy(bx_hbm.at[part], bx_ref.at[part], b_sem.at[0, c]),
            pltpu.make_async_copy(by_hbm.at[part], by_ref.at[part], b_sem.at[1, c]),
        )
        for copy in pair:
            copy.start()
        loads.append(pair)

    barrier = pltpu.get_barrier_semaphore()
    peers = [(d, to) for to in others] + [(flip(d, bit), z) for bit in plans[0] + extra]
    for peer in peers:
        pl.semaphore_signal(barrier, inc=1, device_id=peer, device_id_type=MESH)
    xf_ref[z] = x_ref[...]
    ball_ref[z] = jnp.broadcast_to(bu_ref[...].astype(F32).reshape(1, -1), ball_ref.shape[1:])
    pl.semaphore_wait(barrier, len(peers))

    def on_step(step, act):
        for block, ahead in ((z - step, z + 1), (z + step, z - 1)):

            @pl.when(jnp.logical_and(block >= 0, block < n_mp))
            def _():
                act(block, ahead, jnp.logical_and(ahead >= 0, ahead < n_mp))

    def ends(act):
        for ahead, sem in ((z + 1, z), (z - 1, n_mp)):

            @pl.when(jnp.logical_and(ahead >= 0, ahead < n_mp))
            def _():
                act(ahead, sem)

    def start_all(copies):
        for copy in copies:
            copy.start()

    def x_hop(block, to, sem):
        return remote(xf_ref.at[block], xf_ref.at[block], x_send.at[sem], x_recv.at[block], (d, to))

    def w_hop(w, block, to, sem, own=False):
        label = labels[w_plan[w]]
        held = sources[w].at[label] if own else gathered[w].at[block, label]
        return remote(held, gathered[w].at[block, label], z_send.at[w, sem], z_recv.at[w, block], (d, to))

    def all_w(block, to, sem, own=False):
        return [w_hop(w, block, to, sem, own) for w in range(3)]

    ends(lambda ahead, sem: x_hop(z, ahead, sem).start())
    ends(lambda ahead, sem: start_all(all_w(z, ahead, sem, True)))

    def u_copy(to, source):
        return remote(ball_ref.at[source], ball_ref.at[source], u_send.at[to], u_recv.at[source], (d, to))

    for to in others:
        u_copy(to, z).start()
    own = [pltpu.make_async_copy(sources[w], gathered[w].at[z], own_sem.at[w]) for w in range(3)]
    start_all(own)

    def x_arrived(step):
        def act(block, ahead, more):
            x_hop(block, z, block).wait_recv()

            @pl.when(more)
            def _():
                x_hop(block, ahead, block).start()

        on_step(step, act)

    def plane_copy(w, place, shard, incoming):
        plan = w_plan[w]
        size = 2**place
        base = (labels[plan] // size) * size
        if incoming:
            base = flip(base, place)
        part = gathered[w].at[shard, pl.ds(base, size)]
        return remote(part, part, p_send.at[w, place, shard], p_recv.at[w, place, shard], (flip(d, plans[plan][place]), z))

    def w_arrived(step):
        def act(block, ahead, more):
            for w in range(3):
                w_hop(w, block, z, block).wait_recv()

            @pl.when(more)
            def _():
                start_all(all_w(block, ahead, block))

            for w in range(3):
                plane_copy(w, 0, block, False).start()

        on_step(step, act)

    def plane_next(step, place, which=(0, 1, 2)):
        def act(block, ahead, more):
            for w in which:
                plane_copy(w, place - 1, block, True).wait_recv()
                plane_copy(w, place, block, False).start()

        on_step(step, act)

    def plane_done(step, which):
        def act(block, ahead, more):
            for w in which:
                plane_copy(w, depth - 1, block, True).wait_recv()

        on_step(step, act)

    tab = [
        jnp.broadcast_to(
            jnp.concatenate([tx_ref[h : h + 1, :].astype(F32), ty_ref[h : h + 1, :].astype(F32)], axis=1) * scale, (8, TILE)
        )
        for h in range(heads)
    ]
    bins_x = tx_ref.shape[1]
    bins = tp_ref.shape[1]
    pad = jnp.zeros((1, TILE - bins), F32)
    ltab = [
        jnp.broadcast_to(jnp.concatenate([tp_ref[h : h + 1, :].astype(F32) * scale, pad], axis=1), (8, TILE))
        for h in range(heads)
    ]
    ci = lax.broadcasted_iota(jnp.int32, (8, TILE), 1)
    ri = lax.broadcasted_iota(jnp.int32, (8, TILE), 0)

    @pl.loop(0, TILE // 8)
    def _(g):
        at = pl.ds(pl.multiple_of(g * 8, 8), 8)
        for off in range(5):
            idx = line_bucket(ci - ri - g * 8 + (off - 2) * TILE)
            for h in range(heads):
                line_ref[h, off, at, :] = jnp.take_along_axis(ltab[h], idx, axis=1)

    place_ids = lax.broadcasted_iota(jnp.int32, (1, slot), 1)
    live = place_ids < 1 + PATCHES + len_ref[0]
    seen = jnp.where(live & ((km_ref[...].reshape(1, slot) == 1) | (place_ids == 0)), 0.0, -1e30)

    def bias_chunk(c):
        for copy in loads[c]:
            copy.wait()

        @pl.loop(0, TILE // 8)
        def _(g):
            at = pl.ds(pl.multiple_of(c * TILE + g * 8, 8), 8)
            near = pl.ds(pl.multiple_of(g * 8, 8), 8)
            for j in range(tiles):
                cols = slice(j * TILE, (j + 1) * TILE)
                ix = bx_ref[at, cols]
                iy = by_ref[at, cols] + bins_x
                hide = seen[:, cols]
                off = min(max(j - c + 2, 0), 4)
                for h in range(heads):
                    b = jnp.take_along_axis(tab[h], ix, axis=1) + jnp.take_along_axis(tab[h], iy, axis=1)
                    bias_ref[h, at, cols] = (b + line_ref[h, off, near, :]) + hide

    for c in range(tiles):
        if c == tiles // 2:
            x_arrived(1)
        bias_chunk(c)
    w_arrived(1)
    x_arrived(2)
    plane_next(1, 1)
    w_arrived(2)
    for place in range(2, depth):
        plane_next(1, place)
    x_arrived(3)

    lane = lax.broadcasted_iota(jnp.int32, (1, width), 1)

    def mine(h):
        return (lane >= h * HEAD_DIM) & (lane < (h + 1) * HEAD_DIM)

    zero = jnp.zeros((), BF16)
    b_q = bq_ref[...].astype(F32).reshape(1, width)
    b_v = bv_ref[...].astype(F32).reshape(1, width)

    @pl.loop(0, n_mp)
    def _(b):
        at = pl.ds(pl.multiple_of(b * rows, rows), rows)
        xb = xf_ref[b]
        q_ref[at, :] = ((dot(xb, w_ref[0], 1, 1) + b_q).astype(BF16).astype(F32) * scale).astype(BF16)
        k_ref[at, :] = dot(xb, w_ref[1], 1, 1).astype(BF16)
        v_ref[at, :] = (dot(xb, w_ref[2], 1, 1) + b_v).astype(BF16)

    def c_copy(turn, to, source):
        return remote(di_ref.at[turn], cr_ref.at[source], c_send.at[turn], c_recv.at[source], (d, to))

    @pl.loop(0, n_mp)
    def _(turn):
        to = (z + 1 + turn) % n_mp
        at = pl.ds(pl.multiple_of(to * rows, rows), rows)
        q = q_ref[at, :]
        out = jnp.zeros((rows, width), F32)
        for h in range(heads):
            s = dot(jnp.where(mine(h), q, zero), k_ref[...], 1, 1) + bias_ref[h, at, :]
            top = jnp.max(s, axis=1, keepdims=True)
            e = jnp.exp(s - top).astype(BF16)
            e_ref[h, at, :] = e
            inv = 1.0 / jnp.sum(e.astype(F32), axis=1, keepdims=True)
            inv_ref[h, at, :] = inv
            out = out + jnp.where(mine(h), dot(e, v_ref[...], 1, 0) * inv, 0.0)
        low = out.astype(BF16)

        @pl.when(turn == n_mp - 1)
        def _():
            cr_ref[z] = low

        @pl.when(turn < n_mp - 1)
        def _():
            di_ref[turn] = low
            c_copy(turn, to, z).start()

        @pl.when(turn == 0)
        def _():
            plane_next(2, 1)

        @pl.when(turn == 1)
        def _():
            w_arrived(3)

    for place in range(2, depth):
        plane_next(2, place)
    for place in range(1, depth):
        plane_next(3, place, (0,))
        if place == 1:
            plane_next(3, 1, (1, 2))
    for step in range(1, n_mp):
        plane_done(step, (0,))
    own[0].wait()
    for source in others:
        c_copy(0, z, source).wait_recv()
    for turn in range(n_mp - 1):
        c_copy(turn, z, z).wait_send()

    lines = (nf_ref, dff_ref)

    def hop(a, block, to, sem):
        return remote(lines[a].at[block], lines[a].at[block], h_send.at[a, sem], h_recv.at[a, block], (d, to))

    def arrived(a, step):
        def act(block, ahead, more):
            hop(a, block, z, block).wait_recv()

            @pl.when(more)
            def _():
                hop(a, block, ahead, block).start()

        on_step(step, act)

    def set_off(a):
        ends(lambda ahead, sem: hop(a, z, ahead, sem).start())

    def vec(ref):
        return ref[...].astype(F32).reshape(1, wide)

    def norm(values):
        spread = values - jnp.mean(values, axis=1, keepdims=True)
        rate = lax.rsqrt(jnp.mean(spread * spread, axis=1, keepdims=True) + EPS)
        return spread * rate, rate

    def norm_back(up, gain, hat, rate):
        scaled = up * gain
        first = jnp.mean(scaled, axis=1, keepdims=True)
        second = jnp.mean(scaled * hat, axis=1, keepdims=True)
        return rate * (scaled - first - hat * second)

    def total_rows(values):
        return jnp.sum(values, axis=0, keepdims=True)

    def slab(ref, s):
        return ref[s].reshape(-1, wide)

    attn = dot(cr_ref[0], slab(wo_ref, 0), 1, 0)
    for s in range(1, n_mp):
        attn = attn + dot(cr_ref[s], slab(wo_ref, s), 1, 0)
    hat_one, rate_one = norm(x_ref[...].astype(F32) + attn + vec(bo_ref))
    normed = hat_one * vec(ga_ref) + vec(na_ref)
    low_own = normed.astype(BF16)
    nf_ref[z] = low_own
    set_off(0)

    for place in range(2, depth):
        plane_next(3, place, (1, 2))
    for step in range(1, n_mp):
        plane_done(step, (1, 2))
    for w in (1, 2):
        own[w].wait()
    for source in others:
        u_copy(z, source).wait_recv()

    slope_at = heads - 1
    ffn_ref[...] = jnp.zeros_like(ffn_ref)

    @pl.loop(0, n_mp)
    def _(s):
        at = pl.ds(pl.multiple_of(s * rows, rows), rows)
        act, slope = gelu_parts(dot(nf_ref[z], slab(wu_ref, s), 1, 0) + ball_ref[s, 0:1, :])
        bias_ref[slope_at, at, :] = slope
        ffn_ref[...] += dot(act, slab(wd_ref, s), 1, 0)

        @pl.when(s == n_mp - 1)
        def _():
            arrived(0, 1)

    hat_two, rate_two = norm(normed + ffn_ref[...] + vec(bd_ref))
    lo_ref[...] = (hat_two * vec(gf_ref) + vec(nn_ref)).astype(BF16)

    place_row = z * rows + lax.broadcasted_iota(jnp.int32, (rows, 1), 0)
    grad_y = jnp.where(place_row < 1 + PATCHES + len_ref[0], cot_ref[...].astype(F32), 0.0)
    d_two = norm_back(grad_y, vec(gf_ref), hat_two, rate_two)
    dff_ref[z] = d_two.astype(BF16)
    set_off(1)
    ffn_ref[...] = d_two

    @pl.loop(0, n_mp)
    def _(s):
        at = pl.ds(pl.multiple_of(s * rows, rows), rows)
        d_pre = (dot(dff_ref[z], slab(wd_ref, s), 1, 1) * bias_ref[slope_at, at, :]).astype(BF16)
        ffn_ref[...] += dot(d_pre, slab(wu_ref, s), 1, 1)

    d_normed = ffn_ref[...]
    d_one = norm_back(d_normed, vec(ga_ref), hat_one, rate_one)
    da_ref[...] = d_one
    d_attn = d_one.astype(BF16)

    def d_copy(to, source):
        return remote(di_ref.at[to], dc_ref.at[source], d_send.at[to], d_recv.at[source], (d, to))

    for s in range(n_mp):
        di_ref[s] = dot(d_attn, slab(wo_ref, s), 1, 1).astype(BF16)
    for to in others:
        d_copy(to, z).start()
    dc_ref[z] = di_ref[z]
    arrived(0, 2)

    def wait_all(copies):
        for copy in copies:
            copy.wait_send()

    def sent(block, ahead, more):
        @pl.when(more)
        def _():
            wait_all([x_hop(block, ahead, block)] + all_w(block, ahead, block))

        for w in range(3):
            for place in range(depth):
                plane_copy(w, place, block, False).wait_send()

    ends(lambda ahead, sem: wait_all([x_hop(z, ahead, sem)] + all_w(z, ahead, sem, True)))
    for step in range(1, n_mp):
        on_step(step, sent)
    for to in others:
        u_copy(to, z).wait_send()

    per_u = wide // SLICES

    def flat(slab_index):
        def at(base, size):
            return bias_ref.at[slab_index, pl.ds(pl.multiple_of(base * per_u, per_u), size * per_u)]

        return at

    def lead(ref):
        return lambda base, size: ref.at[pl.ds(base, size)]

    def inside(ref, s):
        return lambda base, size: ref.at[s, pl.ds(base, size)]

    totals = (flat(0), flat(1), lead(qa_ref), lead(oa_ref))
    staged = (inside(wu_ref, others[0]), inside(wu_ref, others[1]), lead(qs_ref), inside(wu_ref, others[2]))
    taken = (ur_ref, dr_ref, qr_ref, or_ref)
    beyond = (ux_ref, dx_ref, qx_ref, ox_ref)
    outs = (uo_ref, do_ref, qo_ref, oo_ref)
    item_plan = (0, 1, 0, 1)

    def own_label(i):
        return labels[item_plan[i]]

    def halves(i, place):
        size = 2**place
        base = (own_label(i) // size) * size
        return base, flip(base, place), size

    def partner(i, place):
        return (flip(d, plans[item_plan[i]][place]), z)

    def rs_copy(i, place):
        _, away, size = halves(i, place)
        return remote(
            staged[i](away, size), taken[i].at[pl.ds(size, size)], rs_send.at[i, place], rs_recv.at[i, place], partner(i, place)
        )

    def rs_start(i, place):
        _, away, size = halves(i, place)
        target = staged[i](away, size)
        target[...] = totals[i](away, size)[...].astype(BF16).reshape(target.shape)
        rs_copy(i, place).start()

    def ex_copy(i, turn):
        return remote(
            staged[i](own_label(i), 1), beyond[i].at[pl.ds(turn, 1)], ex_send.at[i, turn], ex_recv.at[i, turn],
            (flip(d, extra[turn]), z),
        )

    def ex_start(i, turn):
        target = staged[i](own_label(i), 1)
        target[...] = totals[i](own_label(i), 1)[...].astype(BF16).reshape(target.shape)
        ex_copy(i, turn).start()

    def ag_copy(i, place, incoming=False):
        base, away, size = halves(i, place)
        part = outs[i].at[pl.ds(away if incoming else base, size)]
        return remote(part, part, ag_send.at[i, place], ag_recv.at[i, place], partner(i, place))

    def oz_copy(to, source):
        return remote(oy_ref.at[to], oz_ref.at[source], oz_send.at[to], oz_recv.at[source], (d, to))

    stage = {}

    def begin(i):
        rs_start(i, depth - 1)
        stage[i] = ("halve", depth - 1)

    def spread(i):
        if i == 3:
            per = oy_ref.shape[1]
            for s in range(n_mp):
                oy_ref[s] = oa_ref[own_label(3), s * per : (s + 1) * per, :].astype(BF16)
            for to in others:
                oz_copy(to, z).start()
            stage[i] = ("line", 0)
        else:
            outs[i][own_label(i)] = totals[i](own_label(i), 1)[...].astype(BF16).reshape(outs[i].shape[1:])
            ag_copy(i, 0).start()
            stage[i] = ("gather", 0)

    def onward(*which):
        for i in which:
            if stage[i] is None:
                continue
            kind, place = stage[i]
            if kind == "halve":
                kept, _, size = halves(i, place)
                rs_copy(i, place).wait_recv()
                total = totals[i](kept, size)
                total[...] = total[...] + taken[i][size : 2 * size].astype(F32).reshape(total.shape)
                if place:
                    rs_start(i, place - 1)
                    stage[i] = ("halve", place - 1)
                elif extra:
                    ex_start(i, 0)
                    stage[i] = ("swap", 0)
                else:
                    spread(i)
            elif kind == "swap":
                ex_copy(i, place).wait_send()
                ex_copy(i, place).wait_recv()
                total = totals[i](own_label(i), 1)
                total[...] = total[...] + beyond[i][place : place + 1].astype(F32).reshape(total.shape)
                if place < len(extra) - 1:
                    ex_start(i, place + 1)
                    stage[i] = ("swap", place + 1)
                else:
                    spread(i)
            elif kind == "line":
                per = oz_ref.shape[1]
                out = oa_ref[own_label(3), pl.ds(pl.multiple_of(z * per, per), per), :]
                for source in others:
                    oz_copy(z, source).wait_recv()
                    out = out + oz_ref[source].astype(F32)
                oo_ref[own_label(3)] = out.astype(BF16)
                ag_copy(3, 0).start()
                stage[i] = ("gather", 0)
            else:
                ag_copy(i, place, True).wait_recv()
                if place < depth - 1:
                    ag_copy(i, place + 1).start()
                    stage[i] = ("gather", place + 1)
                else:
                    stage[i] = None

    per_o = width // SLICES
    for s in range(n_mp):
        go = dot(cr_ref[s].astype(F32).T.astype(BF16), d_attn, 1, 0)
        oa_ref[:, s * per_o : (s + 1) * per_o, :] = go.reshape(SLICES, per_o, wide)
    begin(3)
    gs_ref[...] = jnp.concatenate(
        [
            total_rows(grad_y * hat_two), total_rows(grad_y), total_rows(d_two), total_rows(d_normed * hat_one),
            total_rows(d_normed), total_rows(d_one), jnp.zeros((2, wide), F32),
        ],
        axis=0,
    )
    sp_ref[0:8, :] = gs_ref[...]

    def sz_copy(to, source):
        return remote(gs_ref, sz_ref.at[source], sz_send.at[to], sz_recv.at[source], (d, to))

    for to in others:
        sz_copy(to, z).start()

    factor = jnp.zeros((slot, width), F32)
    for h in range(heads):
        factor = jnp.where(mine(h), inv_ref[h], factor)
    qt_ref[...] = q_ref[...].astype(F32).T.astype(BF16)
    arrived(1, 1)
    onward(3)
    for source in others:
        d_copy(source, source).wait_recv()

    gt_ref[...] = (dc_ref[...].reshape(slot, width).astype(F32) * factor).T.astype(BF16)
    dq_ref[...] = jnp.zeros_like(dq_ref)
    block = slot // 2
    groups = block // rows

    def score_slab(h):
        return (z + 1 + h) % n_mp

    @pl.loop(0, heads)
    def _(h):
        hs = pl.ds(pl.multiple_of(h * HEAD_DIM, HEAD_DIM), HEAD_DIM)
        dk = dv = None
        for r in range(slot // block):
            rs = slice(r * block, (r + 1) * block)
            e = e_ref[h, rs, :]
            p = e.astype(F32) * inv_ref[h, rs, :]
            up = dc_ref[r * groups : (r + 1) * groups].reshape(block, width)
            dp = dot(jnp.where(mine(h), up, zero), v_ref[...], 1, 1)
            ds = (p * (dp - jnp.sum(p * dp, axis=1, keepdims=True))).astype(BF16)
            cut = block // per_u
            wd_ref[score_slab(h), r * cut : (r + 1) * cut] = ds.reshape(cut, per_u, slot)
            dq_ref[rs, :] += jnp.where(mine(h), dot(ds, k_ref[...], 1, 0), 0.0)
            b = dot(qt_ref[hs, rs], ds, 1, 0)
            dk = b if dk is None else dk + b
            c = dot(gt_ref[hs, rs], e, 1, 0)
            dv = c if dv is None else dv + c
        dt_ref[1, hs, :] = dk.astype(BF16)
        dt_ref[2, hs, :] = dv.astype(BF16)

        @pl.when(h == 0)
        def _():
            arrived(0, 3)

        @pl.when(h == 1)
        def _():
            arrived(1, 2)

    onward(3)
    low_q = (dq_ref[...] * scale).astype(BF16)
    dn_ref[0] = low_q
    dt_ref[0] = low_q.astype(F32).T.astype(BF16)
    for c in (1, 2):
        dn_ref[c] = dt_ref[c].astype(F32).T.astype(BF16)

    ones = jnp.ones((8, slot), BF16)
    xf = xf_ref[...].reshape(slot, wide)
    for c in range(3):
        qa_ref[:, c * per_o : (c + 1) * per_o, :] = dot(dt_ref[c], xf, 1, 0).reshape(SLICES, per_o, wide)
    sp_ref[8:16, :] = jnp.zeros((8, wide), F32)
    sp_ref[9:10, 0:width] = dot(ones, dn_ref[0], 1, 0)[0:1]
    sp_ref[10:11, 0:width] = dot(ones, dn_ref[2], 1, 0)[0:1]
    begin(2)
    onward(3)

    b_up = bu_ref[...].astype(F32).reshape(1, -1)

    @pl.loop(0, n_mp)
    def _(b):
        at = pl.ds(pl.multiple_of(b * rows, rows), rows)
        act, slope = gelu_parts(dot(nf_ref[b], slab(wu_ref, z), 1, 0) + b_up)
        e_ref[0, at, :] = act
        bias_ref[slope_at, at, :] = slope

    onward(2, 3)
    arrived(1, 3)

    dff = dff_ref[...].reshape(slot, wide)
    bias_ref[1] = dot(e_ref[0], dff, 0, 0)
    begin(1)
    e_ref[1] = (dot(dff, slab(wd_ref, z), 1, 1) * bias_ref[slope_at]).astype(BF16)
    bias_ref[0] = dot(nf_ref[...].reshape(slot, wide), e_ref[1], 0, 0)
    begin(0)
    sp_ref[8:9, :] = dot(ones, e_ref[1], 1, 0)[0:1]

    def r_copy(turn, to):
        return remote(wo_ref.at[turn], got_ref.at[turn], r_send.at[turn], r_recv.at[turn], (d, to))

    def dx_part(to):
        at = pl.ds(pl.multiple_of(to * rows, rows), rows)
        out = dot(dn_ref[0, at, :], w_ref[0], 1, 0)
        for c in (1, 2):
            out = out + dot(dn_ref[c, at, :], w_ref[c], 1, 0)
        return out

    @pl.loop(0, n_mp)
    def _(turn):
        to = (z + 1 + turn) % n_mp
        out = dx_part(to)

        @pl.when(turn < n_mp - 1)
        def _():
            wo_ref[turn] = out.astype(BF16).reshape(wo_ref.shape[1:])
            r_copy(turn, to).start()

        @pl.when(turn == n_mp - 1)
        def _():
            da_ref[...] += out

    onward(1, 0, 2, 3)

    acc_ref[...] = jnp.zeros_like(acc_ref)
    one = jnp.ones((), BF16)
    trips = slot // (GROUP * STEP)
    per_slice = per_u // (GROUP * STEP)
    polls = {trips // 5: (1, 0, 2), 2 * trips // 5: (1, 0, 2), 3 * trips // 5: (1, 0, 2, 3), 4 * trips // 5: (1, 0, 2, 3)}

    @pl.loop(0, trips)
    def _(i):
        first = pl.multiple_of((i % per_slice) * GROUP * STEP, GROUP * STEP)
        flat_at = pl.multiple_of(i * GROUP * STEP, GROUP * STEP)
        ds = [
            [wd_ref[score_slab(h), i // per_slice, pl.ds(first + g * GROUP, GROUP), :] for h in range(heads)] for g in range(STEP)
        ]
        for t, b_ref in enumerate((bx_ref, by_ref)):
            tot = None
            for g in range(STEP):
                b = b_ref[pl.ds(flat_at + g * GROUP, GROUP), :]
                hi = (b >> 4).astype(F32).astype(BF16)
                lo = (b & 15).astype(F32).astype(BF16)
                left = []
                for a in range(HI):
                    m = hi == jnp.asarray(a, BF16)
                    left += [jnp.where(m, ds[g][h], zero) for h in range(heads)]
                right = [jnp.where(lo == jnp.asarray(c, BF16), one, zero) for c in range(LO)]
                o = dot(jnp.concatenate(left, 0), jnp.concatenate(right, 0), 1, 1)
                tot = o if tot is None else tot + o
            acc_ref[t] += tot
        for trip, which in polls.items():

            @pl.when(i == trip)
            def _():
                onward(*which)

    m, n = HI * heads * GROUP, LO * GROUP
    same = (lax.broadcasted_iota(jnp.int32, (m, n), 0) & (GROUP - 1)) == (lax.broadcasted_iota(jnp.int32, (m, n), 1) & (GROUP - 1))
    pick = (lax.broadcasted_iota(jnp.int32, (n, LO), 0) // GROUP == lax.broadcasted_iota(jnp.int32, (n, LO), 1)).astype(F32)
    st_ref[...] = jnp.zeros_like(st_ref)
    for t in range(2):
        kept = jnp.sum(jnp.where(same, acc_ref[t], 0.0).reshape(m // GROUP, GROUP, n), axis=1)
        found = lax.dot_general(
            kept, pick, (((1,), (0,)), ((), ())), precision=lax.Precision.HIGHEST, preferred_element_type=F32
        )
        st_ref[0 : HI * heads, t * LO : (t + 1) * LO] = found * scale

    cw = lax.broadcasted_iota(jnp.int32, (TILE, TILE), 1)
    rw = lax.broadcasted_iota(jnp.int32, (TILE, TILE), 0)
    half = bins // 2

    for h in range(heads):
        tots = [jnp.zeros((TILE, TILE), F32) for _ in range(5)]
        for i in range(tiles):
            pieces = []
            at = i * TILE
            while at < (i + 1) * TILE:
                inner = at % per_u
                take = min(per_u - inner, (i + 1) * TILE - at)
                pieces.append(wd_ref[score_slab(h), at // per_u, inner : inner + take, :])
                at += take
            strip = (jnp.concatenate(pieces, 0) if len(pieces) > 1 else pieces[0]).astype(F32)
            for j in range(tiles):
                off = min(max(j - i, -2), 2) + 2
                tots[off] = tots[off] + strip[:, j * TILE : (j + 1) * TILE]
        for off in range(5):
            line_ref[h, off] = tots[off]
    ids = [line_bucket(cw - rw + (off - 2) * TILE) for off in range(5)]
    for h in range(heads):
        found = []
        for b in range(bins):
            tot = None
            for off in range(5):
                if off in (1, 2, 3) and (off == 2 or (b >= half) == (off == 3)):
                    piece = jnp.where(ids[off] == b, line_ref[h, off], 0.0)
                elif off == 0 and b == half - 1 or off == 4 and b == bins - 1:
                    piece = line_ref[h, off]
                else:
                    continue
                tot = piece if tot is None else tot + piece
            found.append(jnp.sum(tot, axis=0, keepdims=True))
        st_ref[0:bins, 2 * LO + h : 2 * LO + h + 1] = jnp.sum(jnp.concatenate(found, 0), axis=1, keepdims=True) * scale

    bits = plans[0] + extra

    def small(turn):
        to = (flip(d, bits[turn]), z)
        return (
            remote(sp_ref, sr_ref.at[turn], sp_send.at[0, turn], sp_recv.at[0, turn], to),
            remote(st_ref, sv_ref.at[turn], sp_send.at[1, turn], sp_recv.at[1, turn], to),
        )

    for source in others:
        sz_copy(z, source).wait_recv()
        sp_ref[0:8, :] = sp_ref[0:8, :] + sz_ref[source]
    for turn in range(len(bits)):
        start_all(small(turn))
        onward(1, 0, 2, 3)
        for copy in small(turn):
            copy.wait_send()
            copy.wait_recv()
        sp_ref[...] = sp_ref[...] + sr_ref[turn]
        st_ref[...] = st_ref[...] + sv_ref[turn]
    pack_ref[...] = sp_ref[...]
    tab_out[...] = st_ref[...]

    for turn in range(n_mp - 1):
        r_copy(turn, z).wait_recv()
        da_ref[...] = da_ref[...] + got_ref[turn].astype(F32).reshape(rows, wide)
    ig_ref[...] = da_ref[...].astype(BF16)

    while any(stage.values()):
        onward(1, 0, 2, 3)
    for turn in range(n_mp - 1):
        r_copy(turn, z).wait_send()
    for to in others:
        d_copy(to, z).wait_send()
        sz_copy(to, z).wait_send()
        oz_copy(to, z).wait_send()
    for i in range(4):
        for place in range(depth):
            rs_copy(i, place).wait_send()
            ag_copy(i, place).wait_send()
    for a in range(2):
        ends(lambda ahead, sem: hop(a, z, ahead, sem).wait_send())

        def gone(block, ahead, more):
            @pl.when(more)
            def _():
                hop(a, block, ahead, block).wait_send()

        for step in range(1, n_mp):
            on_step(step, gone)


def finish_kernel(
    lo_hbm, ig_hbm, sp_hbm, st_hbm, u_hbm, d_hbm, q_hbm, o_hbm,
    lo_ref, ig_ref, gq_ref, bq_ref, bv_ref, go_ref, bo_ref, ga_ref, na_ref, gu_ref, bu_ref, gd_ref, bd_ref, gf_ref, nf_ref,
    tp_ref, tx_ref, ty_ref,
    u32, d32, q32, sp_ref, st_ref, u_ref, d_ref, q_ref, o_ref, sem, in_sem,
):
    pairs = ((u_hbm, u_ref), (d_hbm, d_ref), (q_hbm, q_ref), (o_hbm, o_ref), (sp_hbm, sp_ref), (st_hbm, st_ref), (lo_hbm, lo_ref), (ig_hbm, ig_ref))
    loads = [pltpu.make_async_copy(src, dst, in_sem.at[i]) for i, (src, dst) in enumerate(pairs)]
    for copy in loads:
        copy.start()
    loads[0].wait()
    wide = sp_ref.shape[1]
    width = bq_ref.shape[0]
    heads = width // HEAD_DIM
    per = width // SLICES
    u32[...] = u_ref[...].astype(F32)
    cu = pltpu.make_async_copy(u32, gu_ref, sem.at[0])
    cu.start()
    loads[1].wait()
    d32[...] = d_ref[...].astype(F32)
    cd = pltpu.make_async_copy(d32, gd_ref, sem.at[1])
    cd.start()
    loads[2].wait()
    for c in range(3):
        q32[c] = q_ref[:, c * per : (c + 1) * per, :].astype(F32).reshape(width, wide)
    cq = pltpu.make_async_copy(q32, gq_ref, sem.at[2])
    cq.start()
    for copy in loads[3:]:
        copy.wait()
    go_ref[...] = o_ref[...].astype(F32).reshape(width, wide)
    for row, ref in enumerate((gf_ref, nf_ref, bd_ref, ga_ref, na_ref, bo_ref)):
        ref[...] = sp_ref[row : row + 1, :].reshape(wide)
    bu_ref[...] = sp_ref[8:9, :].reshape(wide)
    bq_ref[...] = sp_ref[9:10, 0:width].reshape(width)
    bv_ref[...] = sp_ref[10:11, 0:width].reshape(width)
    table = st_ref[...]
    turned = table.T
    bins = tp_ref.shape[1]
    tp_ref[...] = turned[2 * LO : 2 * LO + heads, 0:bins]
    for t, ref in enumerate((tx_ref, ty_ref)):
        for h in range(heads):
            ref[h : h + 1, :] = jnp.concatenate(
                [table[a * heads + h : a * heads + h + 1, t * LO : (t + 1) * LO] for a in range(HI)], axis=1
            )
    for copy in (cu, cd, cq):
        copy.wait()


def layer(n_mp, n_dp):
    chips, extra = plane_bits(n_dp)
    plans = [chips + [0], chips[::-1] + [0]]
    depth = len(plans[0])

    def on_device(
        hidden_in, text_lens, key_mask, bucket_x, bucket_y, w_qkv, b_q, b_v, w_out, b_out, g_attn, n_attn,
        w_up, b_up, w_down, b_down, g_ffn, n_ffn, t_pos, t_x, t_y, cotangent,
    ):
        rows, wide = hidden_in.shape
        slot = bucket_x.shape[1]
        width = w_qkv.shape[2]
        heads = width // HEAD_DIM
        units = w_up.shape[1]
        per_u, per_o = wide // SLICES, width // SLICES
        bins = t_pos.shape[1]
        sds = jax.ShapeDtypeStruct
        dma = pltpu.SemaphoreType.DMA
        vm = pltpu.VMEM
        more = max(1, len(extra))
        n_bits = depth + len(extra)
        slices = [w.reshape(SLICES, w.shape[0] // SLICES, w.shape[1]) for w in (w_out, w_up, w_down)]
        whole = [(SLICES, per_u, units), (SLICES, units // SLICES, wide), (SLICES, 3 * per_o, wide), (SLICES, per_o, wide)]
        got = whole[:3] + [(SLICES, n_mp * per_o, wide)]
        outs = pl.pallas_call(
            functools.partial(layer_kernel, n_mp, plans, extra),
            out_shape=[sds((rows, wide), BF16), sds((rows, wide), BF16), sds((16, wide), F32), sds((bins, TILE), F32)]
            + [sds(shape, BF16) for shape in whole],
            in_specs=[VMEM] * 16 + [pl.BlockSpec(memory_space=pltpu.SMEM)] + [ANY] * 5,
            out_specs=[VMEM] * 8,
            scratch_shapes=[
                vm((n_mp, rows, wide), BF16), vm((slot, width), BF16), vm((slot, width), BF16), vm((slot, width), BF16),
                vm((heads, slot, slot), BF16), vm((heads, slot, 1), F32), vm((n_mp, rows, width), BF16),
                vm((n_mp, 8, units), F32), vm((slot, slot), jnp.int32), vm((slot, slot), jnp.int32), vm((heads, slot, slot), F32),
                vm((heads, 5, TILE, TILE), F32),
            ] + [vm((n_mp,) + s.shape, BF16) for s in slices] + [
                vm((rows, wide), F32), vm((rows, wide), F32), vm((8, wide), F32), vm((n_mp, rows, width), BF16), vm((n_mp, rows, width), BF16),
                vm((width, slot), BF16), vm((width, slot), BF16), vm((slot, width), F32), vm((3, width, slot), BF16), vm((3, slot, width), BF16),
                vm((2, HI * heads * GROUP, LO * GROUP), F32), vm((n_mp - 1,) + slices[0].shape, BF16), vm((n_mp, rows, wide), BF16), vm((n_mp, rows, wide), BF16),
                vm((16, wide), F32), vm((bins, TILE), F32), vm((n_bits, 16, wide), F32), vm((n_bits, bins, TILE), F32), vm((n_mp, 8, wide), F32),
                vm((SLICES, 3 * per_o, wide), F32), vm((SLICES, n_mp * per_o, wide), F32), vm((SLICES, 3 * per_o, wide), BF16),
            ] + [vm(shape, BF16) for shape in got] + [vm((n_mp, per_o, wide), BF16)] * 2 + [vm((more,) + shape[1:], BF16) for shape in got] + [
                dma((3,)), dma((2, slot // TILE)), dma((n_mp + 1,)), dma((n_mp,)), dma((n_mp - 1,)), dma((n_mp,)), dma((n_mp,)), dma((n_mp,)),
                dma((3, n_mp + 1)), dma((3, n_mp)), dma((3, depth, n_mp)), dma((3, depth, n_mp)),
                dma((n_mp,)), dma((n_mp,)), dma((n_mp - 1,)), dma((n_mp - 1,)), dma((2, n_mp + 1)), dma((2, n_mp)),
                dma((4, depth)), dma((4, depth)), dma((4, depth)), dma((4, depth)), dma((4, more)), dma((4, more)), dma((n_mp,)), dma((n_mp,)),
                dma((2, n_bits)), dma((2, n_bits)), dma((n_mp,)), dma((n_mp,)),
            ],
            compiler_params=pltpu.CompilerParams(collective_id=0, has_side_effects=True, vmem_limit_bytes=62 << 20),
            name="layer",
        )(
            hidden_in, jnp.transpose(w_qkv, (0, 2, 1)), b_q, b_v, t_x, t_y, t_pos, key_mask, b_up, b_out, g_attn, n_attn, b_down, g_ffn,
            n_ffn, cotangent, text_lens, bucket_x[0], bucket_y[0], *slices,
        )
        vec = lambda like: sds(like.shape, F32)
        final = pl.pallas_call(
            finish_kernel,
            out_shape=[
                sds((rows, wide), BF16), sds((rows, wide), BF16), sds((3, width, wide), F32), vec(b_q), vec(b_v), vec(w_out), vec(b_out),
                vec(g_attn), vec(n_attn), sds((SLICES, per_u, units), F32), vec(b_up), sds((SLICES, units // SLICES, wide), F32), vec(b_down),
                vec(g_ffn), vec(n_ffn), vec(t_pos), vec(t_x), vec(t_y),
            ],
            in_specs=[ANY] * 8,
            out_specs=[VMEM] * 2 + [ANY] + [VMEM] * 6 + [ANY] + [VMEM] + [ANY] + [VMEM] * 6,
            scratch_shapes=[
                vm((SLICES, per_u, units), F32), vm((SLICES, units // SLICES, wide), F32), vm((3, width, wide), F32),
                vm((16, wide), F32), vm((bins, TILE), F32),
            ] + [vm(shape, BF16) for shape in whole] + [dma((3,)), dma((8,))],
            compiler_params=pltpu.CompilerParams(vmem_limit_bytes=62 << 20),
            name="finish",
        )(*outs)
        final = list(final)
        final[2] = jnp.transpose(final[2], (0, 2, 1))
        final[9] = final[9].reshape(w_up.shape)
        final[11] = final[11].reshape(w_down.shape)
        return tuple(final)

    return on_device


def solution(mesh):
    both, split = P(("dp", "mp"), None), P("mp")
    rows_mp, cols_mp, qkv = P("mp", None), P(None, "mp"), P(None, None, "mp")
    doc = P("dp", None, None)
    return jax.shard_map(
        layer(mesh.shape["mp"], mesh.shape["dp"]),
        mesh=mesh,
        in_specs=(
            both, P("dp"), P("dp"), doc, doc, qkv, split, split, rows_mp, P(), P(), P(), cols_mp, split, rows_mp, P(), P(), P(),
            rows_mp, rows_mp, rows_mp, both,
        ),
        out_specs=(
            both, both, qkv, split, split, rows_mp, P(), P(), P(), cols_mp, split, rows_mp, P(), P(), P(), rows_mp, rows_mp, rows_mp,
        ),
        check_vma=False,
    )
```

time: 351 us -> 175 us (0.50)
  blocking collectives: 76.9 us -> 0 us
  matrix products: 43.9 us -> 0 us
  waiting for transfers between devices: 23.6 us -> 0 us
  other arithmetic: 21.6 us -> 0 us
  Pallas kernels: 159 us -> 173 us
  between operations: 14.8 us -> 1.48 us
  local copies, waits for them, and re-layouts: 10 us -> 0 us
    psum x2 -> x0, blocking collectives: 63.6 us -> none  [the longest x1 39.9 us: on_device(): lax.psum((grad_b_out, grad_g_attn, grad_n_attn, grad_b_down, grad_g_ffn,...]
    dot_general x10 -> x0, matrix products: 43.9 us -> none  [the longest x1 13.1 us: on_device(): jnp.einsum('srf,sdf->rd', d_pre, wu, preferred_element_type=F32)]
    pallas_call x2, Pallas kernels: 159 us -> 173 us  [the longest x1 168 us: on_device(): pl.pallas_call(functools.partial(layer_kernel, n_mp, plans, extra), out_s...]
    all_gather x1 -> x0, blocking collectives: 13.4 us -> none  [on_device(): b_up_all = lax.all_gather(b_up, 'mp', axis=0)]
    psum x1 -> x0, waiting for transfers between devices: 13 us -> none  [on_device(): lax.psum((gw.astype(BF16), grad_w_out, grad_w_up.astype(BF16), grad_w_dow...]
    reduce_scatter x1 -> x0, waiting for transfers between devices: 10.6 us -> none  [on_device(): lax.psum_scatter(d_wo.reshape(-1, wide), 'mp', scatter_dimension=0, tiled...]
    reduce_sum x6 -> x0, other arithmetic: 7.55 us -> none  [the longest x2 3.56 us: layer_norm(): spread = values - center]
    convert_element_type x8 -> x0, other arithmetic: 6.18 us -> none  [the longest x3 4.01 us: on_device(): gw, grad_w_out, grad_w_up, grad_w_down = [g.astype(F32) for g in big]]
  transfers between devices with their start and end apart: 4 -> 0, of which waited for: 2 -> 0; matrix products, arithmetic and copies ran while one was open for 16% -> 0% of each run, Pallas kernels for 15% -> 0%
where the time goes in v4:
time: 175 us
  Pallas kernels  173 us (99%)
    pallas_call x1, Pallas kernels, on_device(): pl.pallas_call(functools.partial(layer_kernel, n_mp, plans, extra), out_s...  168 us
    pallas_call x1, Pallas kernels, on_device(): pl.pallas_call(finish_kernel, out_shape=[sds((rows, wide), BF16), sds((ro...  5.34 us

profile of v4, /device:TPU:0, one launch (start us, length us, event | category | flops | bytes accessed | tf_op | source)
XLA Modules:
  0.0 174.8 jit_solution(165394893343713598)
XLA Ops:
  1.3 168.0 %layer.1 = (bf16[192,768]{1,0:T(8,128)(2,1)}, bf16[192,768]{1,0:T(8,128)(2,1)}, f32[16,768]{1,0:T(8,128)}, f32[32,128]{1,0:T(8,128)}, bf16[8,96,768]{2,1,0:T(8,1...) custom-call(bf16[192,768]{1,0:T(8,128)(2,1)} %x_ref.1, ...), custom_call_target="tpu_custom_call" | custom-call | tf_op jit(solution)/shard_map/layer/pallas_call | solution.py:903
  169.3 5.3 %finish.1 = (bf16[192,768]{1,0:T(8,128)(2,1)}, bf16[192,768]{1,0:T(8,128)(2,1)}, f32[3,192,768]{2,1,0:T(8,128)}, f32[192]{0:T(256)}, f32[192]{0:T(256)}, /*index...) custom-call(bf16[192,768]{1,0:T(8,128)(2,1)} %get-tuple-element.44.l, ...), custom_call_target="tpu_custom_call" | custom-call | tf_op jit(solution)/shard_map/finish/pallas_call | solution.py:934

commit v5 on v4

--- a/solution.py
+++ b/solution.py
@@ -78,9 +78,20 @@
     tiles = slot // TILE
     units = wu_ref.shape[3]
     scale = HEAD_DIM**-0.5
+    mirrored = z // 2
+    toward = 1 - 2 * mirrored
+    inner = z + mirrored * (n_mp - 1 - 2 * z)
+
+    def in_line(k):
+        if isinstance(k, int):
+            found = k if k > 1 else (inner if k == 0 else 1 - inner)
+        else:
+            found = jnp.where(k < 2, jnp.where(k == 0, inner, 1 - inner), k)
+        return found + mirrored * (n_mp - 1 - 2 * found)
+
     sources = (wo_src, wu_src, wd_src)
     gathered = (wo_ref, wu_ref, wd_ref)
-    others = [(z + k) % n_mp for k in range(1, n_mp)]
+    others = [in_line(k) for k in range(n_mp - 1, 0, -1)]
     depth = len(plans[0])
     labels = [plan_label(d, plan) for plan in plans]
     w_plan = (0, 0, 1)
@@ -108,7 +119,7 @@
     pl.semaphore_wait(barrier, len(peers))
 
     def on_step(step, act):
-        for block, ahead in ((z - step, z + 1), (z + step, z - 1)):
+        for block, ahead in ((z + toward * step, z - toward), (z - toward * step, z + toward)):
 
             @pl.when(jnp.logical_and(block >= 0, block < n_mp))
             def _():
@@ -133,11 +144,12 @@
         held = sources[w].at[label] if own else gathered[w].at[block, label]
         return remote(held, gathered[w].at[block, label], z_send.at[w, sem], z_recv.at[w, block], (d, to))
 
-    def all_w(block, to, sem, own=False):
-        return [w_hop(w, block, to, sem, own) for w in range(3)]
-
+    def some_w(which, block, to, sem, own=False):
+        return [w_hop(w, block, to, sem, own) for w in which]
+
+    every, narrow, broad = (0, 1, 2), (0,), (1, 2)
     ends(lambda ahead, sem: x_hop(z, ahead, sem).start())
-    ends(lambda ahead, sem: start_all(all_w(z, ahead, sem, True)))
+    ends(lambda ahead, sem: start_all(some_w(every, z, ahead, sem, True)))
 
     def u_copy(to, source):
         return remote(ball_ref.at[source], ball_ref.at[source], u_send.at[to], u_recv.at[source], (d, to))
@@ -166,21 +178,21 @@
         part = gathered[w].at[shard, pl.ds(base, size)]
         return remote(part, part, p_send.at[w, place, shard], p_recv.at[w, place, shard], (flip(d, plans[plan][place]), z))
 
-    def w_arrived(step):
+    def w_arrived(step, which):
         def act(block, ahead, more):
-            for w in range(3):
+            for w in which:
                 w_hop(w, block, z, block).wait_recv()
 
             @pl.when(more)
             def _():
-                start_all(all_w(block, ahead, block))
-
-            for w in range(3):
+                start_all(some_w(which, block, ahead, block))
+
+            for w in which:
                 plane_copy(w, 0, block, False).start()
 
         on_step(step, act)
 
-    def plane_next(step, place, which=(0, 1, 2)):
+    def plane_next(step, place, which):
         def act(block, ahead, more):
             for w in which:
                 plane_copy(w, place - 1, block, True).wait_recv()
@@ -244,14 +256,17 @@
     for c in range(tiles):
         if c == tiles // 2:
             x_arrived(1)
+            w_arrived(1, narrow)
         bias_chunk(c)
-    w_arrived(1)
+    w_arrived(1, broad)
     x_arrived(2)
-    plane_next(1, 1)
-    w_arrived(2)
-    for place in range(2, depth):
-        plane_next(1, place)
+    w_arrived(2, narrow)
+    plane_next(1, 1, every)
+    w_arrived(2, broad)
+    plane_next(1, 2, every)
+    plane_next(2, 1, narrow)
     x_arrived(3)
+    w_arrived(3, narrow)
 
     lane = lax.broadcasted_iota(jnp.int32, (1, width), 1)
 
@@ -275,7 +290,7 @@
 
     @pl.loop(0, n_mp)
     def _(turn):
-        to = (z + 1 + turn) % n_mp
+        to = in_line(n_mp - 1 - turn)
         at = pl.ds(pl.multiple_of(to * rows, rows), rows)
         q = q_ref[at, :]
         out = jnp.zeros((rows, width), F32)
@@ -300,20 +315,22 @@
 
         @pl.when(turn == 0)
         def _():
-            plane_next(2, 1)
+            plane_next(2, 1, broad)
+            plane_next(2, 2, narrow)
+            plane_next(3, 1, narrow)
 
         @pl.when(turn == 1)
         def _():
-            w_arrived(3)
-
-    for place in range(2, depth):
-        plane_next(2, place)
-    for place in range(1, depth):
-        plane_next(3, place, (0,))
-        if place == 1:
-            plane_next(3, 1, (1, 2))
+            w_arrived(3, broad)
+
+        @pl.when(turn == 2)
+        def _():
+            plane_next(2, 2, broad)
+            plane_next(3, 2, narrow)
+
+    plane_next(3, 1, broad)
     for step in range(1, n_mp):
-        plane_done(step, (0,))
+        plane_done(step, narrow)
     own[0].wait()
     for source in others:
         c_copy(0, z, source).wait_recv()
@@ -337,6 +354,9 @@
 
     def set_off(a):
         ends(lambda ahead, sem: hop(a, z, ahead, sem).start())
+
+    def g_copy(to, source):
+        return remote(dff_ref.at[source], dff_ref.at[source], h_send.at[1, to], h_recv.at[1, source], (d, to))
 
     def vec(ref):
         return ref[...].astype(F32).reshape(1, wide)
@@ -367,28 +387,28 @@
     nf_ref[z] = low_own
     set_off(0)
 
-    for place in range(2, depth):
-        plane_next(3, place, (1, 2))
-    for step in range(1, n_mp):
-        plane_done(step, (1, 2))
-    for w in (1, 2):
+    slope_at = heads - 1
+    ffn_ref[...] = jnp.zeros_like(ffn_ref)
+    plane_done(1, broad)
+    plane_done(2, broad)
+    for w in broad:
         own[w].wait()
     for source in others:
         u_copy(z, source).wait_recv()
 
-    slope_at = heads - 1
-    ffn_ref[...] = jnp.zeros_like(ffn_ref)
-
     @pl.loop(0, n_mp)
-    def _(s):
+    def _(k):
+        @pl.when(k == n_mp - 1)
+        def _():
+            arrived(0, 1)
+            plane_next(3, 2, broad)
+            plane_done(3, broad)
+
+        s = in_line(k)
         at = pl.ds(pl.multiple_of(s * rows, rows), rows)
         act, slope = gelu_parts(dot(nf_ref[z], slab(wu_ref, s), 1, 0) + ball_ref[s, 0:1, :])
         bias_ref[slope_at, at, :] = slope
         ffn_ref[...] += dot(act, slab(wd_ref, s), 1, 0)
-
-        @pl.when(s == n_mp - 1)
-        def _():
-            arrived(0, 1)
 
     hat_two, rate_two = norm(normed + ffn_ref[...] + vec(bd_ref))
     lo_ref[...] = (hat_two * vec(gf_ref) + vec(nn_ref)).astype(BF16)
@@ -406,6 +426,10 @@
         d_pre = (dot(dff_ref[z], slab(wd_ref, s), 1, 1) * bias_ref[slope_at, at, :]).astype(BF16)
         ffn_ref[...] += dot(d_pre, slab(wu_ref, s), 1, 1)
 
+        @pl.when(s == 0)
+        def _():
+            arrived(0, 2)
+
     d_normed = ffn_ref[...]
     d_one = norm_back(d_normed, vec(ga_ref), hat_one, rate_one)
     da_ref[...] = d_one
@@ -419,7 +443,6 @@
     for to in others:
         d_copy(to, z).start()
     dc_ref[z] = di_ref[z]
-    arrived(0, 2)
 
     def wait_all(copies):
         for copy in copies:
@@ -428,13 +451,13 @@
     def sent(block, ahead, more):
         @pl.when(more)
         def _():
-            wait_all([x_hop(block, ahead, block)] + all_w(block, ahead, block))
+            wait_all([x_hop(block, ahead, block)] + some_w(every, block, ahead, block))
 
         for w in range(3):
             for place in range(depth):
                 plane_copy(w, place, block, False).wait_send()
 
-    ends(lambda ahead, sem: wait_all([x_hop(z, ahead, sem)] + all_w(z, ahead, sem, True)))
+    ends(lambda ahead, sem: wait_all([x_hop(z, ahead, sem)] + some_w(every, z, ahead, sem, True)))
     for step in range(1, n_mp):
         on_step(step, sent)
     for to in others:
@@ -591,6 +614,18 @@
     for h in range(heads):
         factor = jnp.where(mine(h), inv_ref[h], factor)
     qt_ref[...] = q_ref[...].astype(F32).T.astype(BF16)
+    arrived(0, 3)
+
+    b_up = bu_ref[...].astype(F32).reshape(1, -1)
+    cut_r = rows // per_u
+
+    @pl.loop(0, n_mp)
+    def _(b):
+        at = pl.ds(pl.multiple_of(b * rows, rows), rows)
+        act, slope = gelu_parts(dot(nf_ref[b], slab(wu_ref, z), 1, 0) + b_up)
+        uo_ref[pl.ds(b * cut_r, cut_r)] = act.reshape(cut_r, per_u, units)
+        bias_ref[slope_at, at, :] = slope
+
     arrived(1, 1)
     onward(3)
     for source in others:
@@ -625,10 +660,6 @@
         dt_ref[1, hs, :] = dk.astype(BF16)
         dt_ref[2, hs, :] = dv.astype(BF16)
 
-        @pl.when(h == 0)
-        def _():
-            arrived(0, 3)
-
         @pl.when(h == 1)
         def _():
             arrived(1, 2)
@@ -650,28 +681,18 @@
     begin(2)
     onward(3)
 
-    b_up = bu_ref[...].astype(F32).reshape(1, -1)
-
-    @pl.loop(0, n_mp)
-    def _(b):
-        at = pl.ds(pl.multiple_of(b * rows, rows), rows)
-        act, slope = gelu_parts(dot(nf_ref[b], slab(wu_ref, z), 1, 0) + b_up)
-        e_ref[0, at, :] = act
-        bias_ref[slope_at, at, :] = slope
-
     onward(2, 3)
     arrived(1, 3)
-
     dff = dff_ref[...].reshape(slot, wide)
-    bias_ref[1] = dot(e_ref[0], dff, 0, 0)
+    bias_ref[1] = dot(uo_ref[...].reshape(slot, units), dff, 0, 0)
     begin(1)
     e_ref[1] = (dot(dff, slab(wd_ref, z), 1, 1) * bias_ref[slope_at]).astype(BF16)
     bias_ref[0] = dot(nf_ref[...].reshape(slot, wide), e_ref[1], 0, 0)
     begin(0)
     sp_ref[8:9, :] = dot(ones, e_ref[1], 1, 0)[0:1]
 
-    def r_copy(turn, to):
-        return remote(wo_ref.at[turn], got_ref.at[turn], r_send.at[turn], r_recv.at[turn], (d, to))
+    def r_copy(turn, to, place):
+        return remote(wo_ref.at[turn], got_ref.at[place], r_send.at[turn], r_recv.at[place], (d, to))
 
     def dx_part(to):
         at = pl.ds(pl.multiple_of(to * rows, rows), rows)
@@ -682,13 +703,13 @@
 
     @pl.loop(0, n_mp)
     def _(turn):
-        to = (z + 1 + turn) % n_mp
+        to = in_line(n_mp - 1 - turn)
         out = dx_part(to)
 
         @pl.when(turn < n_mp - 1)
         def _():
             wo_ref[turn] = out.astype(BF16).reshape(wo_ref.shape[1:])
-            r_copy(turn, to).start()
+            r_copy(turn, to, (to - z + n_mp - 1) % n_mp).start()
 
         @pl.when(turn == n_mp - 1)
         def _():
@@ -800,14 +821,14 @@
     tab_out[...] = st_ref[...]
 
     for turn in range(n_mp - 1):
-        r_copy(turn, z).wait_recv()
+        r_copy(turn, z, turn).wait_recv()
         da_ref[...] = da_ref[...] + got_ref[turn].astype(F32).reshape(rows, wide)
     ig_ref[...] = da_ref[...].astype(BF16)
 
     while any(stage.values()):
         onward(1, 0, 2, 3)
     for turn in range(n_mp - 1):
-        r_copy(turn, z).wait_send()
+        r_copy(turn, z, turn).wait_send()
     for to in others:
         d_copy(to, z).wait_send()
         sz_copy(to, z).wait_send()

time: 175 us -> 171 us (0.977)
  Pallas kernels: 173 us -> 169 us
    pallas_call x1, Pallas kernels: 168 us -> 164 us  [on_device(): pl.pallas_call(functools.partial(layer_kernel, n_mp, plans, extra), out_s...]
where the time goes in v5:
time: 171 us
  Pallas kernels  169 us (99%)
    pallas_call x1, Pallas kernels, on_device(): pl.pallas_call(functools.partial(layer_kernel, n_mp, plans, extra), out_s...  164 us
    pallas_call x1, Pallas kernels, on_device(): pl.pallas_call(finish_kernel, out_shape=[sds((rows, wide), BF16), sds((ro...  5.34 us

profile of v5, /device:TPU:0, one launch (start us, length us, event | category | flops | bytes accessed | tf_op | source)
XLA Modules:
  0.0 171.0 jit_solution(15818785072817049146)
XLA Ops:
  1.3 164.1 %layer.1 = (bf16[192,768]{1,0:T(8,128)(2,1)}, bf16[192,768]{1,0:T(8,128)(2,1)}, f32[16,768]{1,0:T(8,128)}, f32[32,128]{1,0:T(8,128)}, bf16[8,96,768]{2,1,0:T(8,1...) custom-call(bf16[192,768]{1,0:T(8,128)(2,1)} %x_ref.1, ...), custom_call_target="tpu_custom_call" | custom-call | tf_op jit(solution)/shard_map/layer/pallas_call | solution.py:924
  165.5 5.3 %finish.1 = (bf16[192,768]{1,0:T(8,128)(2,1)}, bf16[192,768]{1,0:T(8,128)(2,1)}, f32[3,192,768]{2,1,0:T(8,128)}, f32[192]{0:T(256)}, f32[192]{0:T(256)}, /*index...) custom-call(bf16[192,768]{1,0:T(8,128)(2,1)} %get-tuple-element.44.l, ...), custom_call_target="tpu_custom_call" | custom-call | tf_op jit(solution)/shard_map/finish/pallas_call | solution.py:955

commit v6 on v5

--- a/solution.py
+++ b/solution.py
@@ -36,7 +36,7 @@
 
 SLICES = 8
 EPS = 1e-05
-HI, LO, GROUP, STEP = 4, 16, 16, 2
+HI, LO, GROUP, STEP = 4, 16, 16, 3
 
 
 def plane_bits(dp_size):
@@ -721,7 +721,7 @@
     one = jnp.ones((), BF16)
     trips = slot // (GROUP * STEP)
     per_slice = per_u // (GROUP * STEP)
-    polls = {trips // 5: (1, 0, 2), 2 * trips // 5: (1, 0, 2), 3 * trips // 5: (1, 0, 2, 3), 4 * trips // 5: (1, 0, 2, 3)}
+    polls = {trips // 3: (1, 0, 2), 2 * trips // 3: (1, 0, 2)}
 
     @pl.loop(0, trips)
     def _(i):

time: 171 us -> 164 us (0.959)
  Pallas kernels: 169 us -> 162 us
    pallas_call x1, Pallas kernels: 164 us -> 157 us  [on_device(): pl.pallas_call(functools.partial(layer_kernel, n_mp, plans, extra), out_s...]
where the time goes in v6:
time: 164 us; the launch traced here: 163 us
  Pallas kernels  162 us (99%)
    pallas_call x1, Pallas kernels, on_device(): pl.pallas_call(functools.partial(layer_kernel, n_mp, plans, extra), out_s...  157 us
    pallas_call x1, Pallas kernels, on_device(): pl.pallas_call(finish_kernel, out_shape=[sds((rows, wide), BF16), sds((ro...  5.34 us

profile of v6, /device:TPU:0, one launch (start us, length us, event | category | flops | bytes accessed | tf_op | source)
XLA Modules:
  0.0 163.4 jit_solution(1989806090377238566)
XLA Ops:
  1.3 156.5 %layer.1 = (bf16[192,768]{1,0:T(8,128)(2,1)}, bf16[192,768]{1,0:T(8,128)(2,1)}, f32[16,768]{1,0:T(8,128)}, f32[32,128]{1,0:T(8,128)}, bf16[8,96,768]{2,1,0:T(8,1...) custom-call(bf16[192,768]{1,0:T(8,128)(2,1)} %x_ref.1, ...), custom_call_target="tpu_custom_call" | custom-call | tf_op jit(solution)/shard_map/layer/pallas_call | solution.py:924
  157.9 5.3 %finish.1 = (bf16[192,768]{1,0:T(8,128)(2,1)}, bf16[192,768]{1,0:T(8,128)(2,1)}, f32[3,192,768]{2,1,0:T(8,128)}, f32[192]{0:T(256)}, f32[192]{0:T(256)}, /*index...) custom-call(bf16[192,768]{1,0:T(8,128)(2,1)} %get-tuple-element.44.l, ...), custom_call_target="tpu_custom_call" | custom-call | tf_op jit(solution)/shard_map/finish/pallas_call | solution.py:955
